TPU v7x, 32 devices: a whole 2x2x4 slice. The times are simulated.
32 devices in a mesh: pages: 8 (over y, x, core), seq: 4 (over z).
Axes of the slice: x: 2, y: 2, z: 4, core: 2. Of those that a mesh axis runs over, the one named last changes fastest.
Arguments:
- tokens: bfloat16 [32, 576, 768], P('pages', 'seq'), may hold values from -6 to 6
- cotangent: bfloat16 [32, 576, 768], P('pages', 'seq'), may hold values from -6 to 6
- conv_text: float32 [3, 3, 768], replicated, may hold values from -4 to 4
- conv_patch: float32 [3, 3, 768], replicated, may hold values from -4 to 4
- proj_query: bfloat16 [768, 768], replicated, may hold values from -0.21875 to 0.21875
- bias_query: float32 [768], replicated, may hold values from -4 to 4
- proj_key: bfloat16 [768, 768], replicated, may hold values from -0.21875 to 0.21875
- proj_value: bfloat16 [768, 768], replicated, may hold values from -0.21875 to 0.21875
- bias_value: float32 [768], replicated, may hold values from -0.4375 to 0.4375
- proj_output: bfloat16 [768, 768], replicated, may hold values from -3 to 3
- bias_output: float32 [768], replicated, may hold values from -4 to 4
- rel_order: float32 [12, 33], replicated, may hold values from -6 to 6
- rel_horiz: float32 [12, 33], replicated, may hold values from -6 to 6
- rel_vert: float32 [12, 33], replicated, may hold values from -6 to 6
- norm_gain: float32 [768], replicated, may hold values from 0.5 to 1.5
- norm_shift: float32 [768], replicated, may hold values from -4 to 4
- expand_weight: bfloat16 [768, 3072], replicated, may hold values from -0.21875 to 0.21875
- expand_bias: float32 [3072], replicated, may hold values from -4 to 4
- reduce_weight: bfloat16 [3072, 768], replicated, may hold values from -0.109375 to 0.109375
- reduce_bias: float32 [768], replicated, may hold values from -4 to 4
- final_gain: float32 [768], replicated, may hold values from 0.5 to 1.5
- final_shift: float32 [768], replicated, may hold values from -4 to 4
- text_count: int32 [32], P('pages'), may hold values from 128 to 512, as said below
- box_left: int32 [32, 576], P('pages'), may hold values from 0 to 63
- box_top: int32 [32, 576], P('pages'), may hold values from 0 to 63
Outputs:
- mixed_out: bfloat16 [32, 576, 768], P('pages', 'seq')
- grad_tokens: float32 [32, 576, 768], P('pages', 'seq')
- grad_conv_text: float32 [3, 3, 768], replicated
- grad_conv_patch: float32 [3, 3, 768], replicated
- grad_query: float32 [768, 768], P('pages')
- grad_bias_query: float32 [768], replicated
- grad_key: float32 [768, 768], P('pages')
- grad_value: float32 [768, 768], P('pages')
- grad_bias_value: float32 [768], replicated
- grad_output: float32 [768, 768], P('pages')
- grad_bias_output: float32 [768], replicated
- grad_order: float32 [12, 33], replicated
- grad_horiz: float32 [12, 33], replicated
- grad_vert: float32 [12, 33], replicated
- grad_norm_gain: float32 [768], replicated
- grad_norm_shift: float32 [768], replicated
- grad_expand: float32 [768, 3072], P('pages')
- grad_expand_bias: float32 [3072], replicated
- grad_reduce: float32 [3072, 768], P('pages')
- grad_reduce_bias: float32 [768], replicated
- grad_final_gain: float32 [768], replicated
- grad_final_shift: float32 [768], replicated
Inputs may be any that keep to these rules, and one draw needn't show every extreme that they name: Text rows 0 .. text_count - 1 of a page are valid, the rest of its 512 text rows are masked; some page has every text row valid and some has 128.
All inputs are finite; a program needn't handle non-finite values.
Results may differ from a plain program's by a relative error of at most 0.017.
The roundings to bfloat16 on the way count: a program that leaves them out, or rounds other values in their place, can miss the bound.
Values may be sent and summed in bfloat16 or wider, within the bound.
No kernel may reach another device: no remote copies, remote signals or barrier semaphores. Data moves between devices by JAX's collectives and lax.ppermute only.
A program may use at most 256 MiB of HBM per device.

v0:
```python
import jax
import jax.numpy as jnp
from jax import lax
from jax.sharding import PartitionSpec as P

TEXT = 512
GRID = 7
SPAN = 16


EPS = 1e-06
SCALE = 0.125
NEG = -1e30


def padded_2(value, sides, width):
    for axis, dim in sides:
        peers, length = (lax.axis_size(axis), value.shape[dim])
        up = [(i, (i + 1) % peers) for i in range(peers - 1)]
        down = [(j, i) for i, j in up]
        last = lax.slice_in_dim(value, length - width, length, axis=dim)
        leading = lax.slice_in_dim(value, 0, width, axis=dim)
        before = lax.ppermute(last, axis, up)
        after = lax.ppermute(leading, axis, down)
        value = jnp.concatenate([before, value, after], axis=dim)
    return value


def layer_norm(inputs, gain_vec, shift_vec):
    average = jnp.mean(inputs, axis=-1, keepdims=True)
    centred = inputs - average
    variance = jnp.mean(centred * centred, axis=-1, keepdims=True)
    return centred * lax.rsqrt(variance + EPS) * gain_vec + shift_vec


def gelu_exact(inputs):
    return jax.nn.gelu(inputs, approximate=False)


def text_conv(padded, conv_text, length):
    running = jnp.zeros(padded.shape[:1] + (length,) + padded.shape[2:], jnp.float32)
    for dilation in range(1, 4):
        for tap_index in range(3):
            offset = (tap_index - 1) * dilation
            running = (
                running
                + conv_text[dilation - 1, tap_index] * padded[:, 3 + offset : 3 + offset + length]
            )
    return running


def patch_conv(patch_rows, conv_patch):
    side = patch_rows.shape[1]
    grid_pad = jnp.pad(patch_rows, ((0, 0), (1, 1), (1, 1), (0, 0)))
    running = jnp.zeros_like(patch_rows)
    for across in range(3):
        for down_index in range(3):
            running = (
                running
                + conv_patch[across, down_index]
                * grid_pad[:, across : across + side, down_index : down_index + side]
            )
    return running


def bucket_index(first_pos, second_pos):
    return jnp.clip(second_pos[..., None, :] - first_pos[..., :, None], -SPAN, SPAN) + SPAN


def bucket_hot(bucket_ids, bucket_count):
    return (bucket_ids[..., None] == jnp.arange(bucket_count, dtype=jnp.int32)).astype(jnp.bfloat16)


def bucket_exact(bucket_ids, bucket_count):
    return (bucket_ids[..., None] == jnp.arange(bucket_count, dtype=jnp.int32)).astype(jnp.float32)


def bias_terms(order_bucket, left_bucket, top_bucket, rel_order, rel_horiz, rel_vert):
    bucket_count = rel_order.shape[1]
    order_term = jnp.einsum(
        "ijb,hb->hij",
        bucket_exact(order_bucket, bucket_count),
        rel_order,
        precision=lax.Precision.HIGHEST,
    )
    horiz_term = jnp.einsum(
        "pijb,hb->phij",
        bucket_exact(left_bucket, bucket_count),
        rel_horiz,
        precision=lax.Precision.HIGHEST,
    )
    vert_term = jnp.einsum(
        "pijb,hb->phij",
        bucket_exact(top_bucket, bucket_count),
        rel_vert,
        precision=lax.Precision.HIGHEST,
    )
    return order_term[None] + horiz_term + vert_term


def scores_of(query_heads, key_heads, rel_terms, key_ok):
    raw_scores = (
        jnp.einsum("pihd,pjhd->phij", query_heads, key_heads, preferred_element_type=jnp.float32)
        * SCALE
    )
    return jnp.where(key_ok[:, None, None, :], raw_scores + rel_terms, NEG)


def per_device(
    tokens,
    cotangent,
    conv_text,
    conv_patch,
    proj_query,
    bias_query,
    proj_key,
    proj_value,
    bias_value,
    proj_output,
    bias_output,
    rel_order,
    rel_horiz,
    rel_vert,
    norm_gain,
    norm_shift,
    expand_weight,
    expand_bias,
    reduce_weight,
    reduce_bias,
    final_gain,
    final_shift,
    text_count,
    box_left,
    box_top,
):
    pages_here, stretch_rows, model_width = tokens.shape
    cycle_size = lax.axis_size("seq")
    cycle_place = lax.axis_index("seq")
    length = stretch_rows * cycle_size
    head_count = rel_order.shape[0]
    head_size = model_width // head_count
    bucket_count = rel_order.shape[1]
    row_count = pages_here * stretch_rows
    patches = GRID * GRID
    patch_start = TEXT - (cycle_size - 1) * stretch_rows
    first_row = cycle_place * stretch_rows
    local_pos = first_row + jnp.arange(stretch_rows, dtype=jnp.int32)
    all_pos = jnp.arange(length, dtype=jnp.int32)
    text_keep = (local_pos[None, :] < text_count[:, None]).astype(jnp.float32)[..., None]
    patch_any = (all_pos >= TEXT) & (all_pos < TEXT + patches)
    key_ok = (all_pos[None, :] < text_count[:, None]) | patch_any[None, :]
    is_last = (cycle_place == cycle_size - 1).astype(jnp.float32)
    token_float = tokens.astype(jnp.float32)
    masked = (token_float * text_keep).astype(jnp.bfloat16)
    padded = padded_2(masked, (("seq", 1),), 3)
    padded_float = padded.astype(jnp.float32)
    text_term = text_conv(padded_float, conv_text, stretch_rows)
    patch_rows = lax.slice_in_dim(token_float, patch_start, patch_start + patches, axis=1)
    patch_rows = patch_rows.reshape(pages_here, GRID, GRID, model_width)
    patch_term = (
        patch_conv(patch_rows, conv_patch).reshape(pages_here, patches, model_width) * is_last
    )
    before_zeros = jnp.zeros((pages_here, patch_start, model_width), jnp.float32)
    after_zeros = jnp.zeros(
        (pages_here, stretch_rows - patch_start - patches, model_width), jnp.float32
    )
    patch_full = jnp.concatenate([before_zeros, patch_term, after_zeros], axis=1)
    settled = (token_float + text_keep * text_term + patch_full).reshape(row_count, model_width)
    entry_low = settled.astype(jnp.bfloat16)
    query_low = (
        jnp.dot(entry_low, proj_query, preferred_element_type=jnp.float32) + bias_query
    ).astype(jnp.bfloat16)
    key_low = jnp.dot(entry_low, proj_key, preferred_element_type=jnp.float32).astype(jnp.bfloat16)
    value_low = (
        jnp.dot(entry_low, proj_value, preferred_element_type=jnp.float32) + bias_value
    ).astype(jnp.bfloat16)
    key_block = key_low.reshape(pages_here, stretch_rows, model_width)
    value_block = value_low.reshape(pages_here, stretch_rows, model_width)
    keys_all, values_all = (
        lax.all_gather(key_block, "seq", axis=1, tiled=True),
        lax.all_gather(value_block, "seq", axis=1, tiled=True),
    )
    left_here = lax.dynamic_slice_in_dim(box_left, first_row, stretch_rows, 1)
    top_here = lax.dynamic_slice_in_dim(box_top, first_row, stretch_rows, 1)
    order_bucket = bucket_index(local_pos, all_pos)
    left_bucket = bucket_index(left_here, box_left)
    top_bucket = bucket_index(top_here, box_top)
    rel_terms = bias_terms(order_bucket, left_bucket, top_bucket, rel_order, rel_horiz, rel_vert)
    query_heads = query_low.reshape(pages_here, stretch_rows, head_count, head_size)
    key_heads = keys_all.reshape(pages_here, length, head_count, head_size)
    value_heads = values_all.reshape(pages_here, length, head_count, head_size)
    scores = scores_of(query_heads, key_heads, rel_terms, key_ok)
    row_max = jnp.max(scores, axis=-1, keepdims=True)
    expo_terms = jnp.exp(scores - row_max)
    row_total = jnp.sum(expo_terms, axis=-1, keepdims=True)
    probs_low = (expo_terms / row_total).astype(jnp.bfloat16)
    log_total = row_max + jnp.log(row_total)
    heads_out = jnp.einsum(
        "phij,pjhd->pihd", probs_low, value_heads, preferred_element_type=jnp.float32
    )
    attended = heads_out.astype(jnp.bfloat16).reshape(row_count, model_width)
    branch = jnp.dot(attended, proj_output, preferred_element_type=jnp.float32) + bias_output
    first_norm, norm_pull = jax.vjp(layer_norm, settled + branch, norm_gain, norm_shift)
    first_low = first_norm.astype(jnp.bfloat16)
    expanded = jnp.dot(first_low, expand_weight, preferred_element_type=jnp.float32) + expand_bias
    activated_float, gelu_pull = jax.vjp(gelu_exact, expanded)
    activated = activated_float.astype(jnp.bfloat16)
    reduced = jnp.dot(activated, reduce_weight, preferred_element_type=jnp.float32) + reduce_bias
    mixed_float, final_pull = jax.vjp(layer_norm, first_norm + reduced, final_gain, final_shift)
    mixed_out = mixed_float.astype(jnp.bfloat16).reshape(pages_here, stretch_rows, model_width)
    d_out = cotangent.astype(jnp.float32).reshape(row_count, model_width)
    d_second, g_final_gain, g_final_shift = final_pull(d_out)
    d_reduced = d_second.astype(jnp.bfloat16)
    g_reduce_bias = jnp.sum(d_reduced, axis=0, dtype=jnp.float32)
    g_reduce = jnp.einsum("rf,rd->fd", activated, d_reduced, preferred_element_type=jnp.float32)
    d_activated = jnp.einsum(
        "rd,fd->rf", d_reduced, reduce_weight, preferred_element_type=jnp.float32
    )
    d_expanded = gelu_pull(d_activated)[0].astype(jnp.bfloat16)
    g_expand_bias = jnp.sum(d_expanded, axis=0, dtype=jnp.float32)
    g_expand = jnp.einsum("rd,rf->df", first_low, d_expanded, preferred_element_type=jnp.float32)
    d_first = d_second + jnp.einsum(
        "rf,df->rd", d_expanded, expand_weight, preferred_element_type=jnp.float32
    )
    d_first_in, g_norm_gain, g_norm_shift = norm_pull(d_first)
    d_branch = d_first_in.astype(jnp.bfloat16)
    g_output_bias = jnp.sum(d_branch, axis=0, dtype=jnp.float32)
    g_output = jnp.einsum("re,rd->ed", attended, d_branch, preferred_element_type=jnp.float32)
    d_attended_low = jnp.einsum(
        "rd,ed->re", d_branch, proj_output, preferred_element_type=jnp.float32
    ).astype(jnp.bfloat16)
    d_attended = d_attended_low.reshape(pages_here, stretch_rows, head_count, head_size)
    keys_back, values_back = (keys_all, values_all)
    key_heads_back = keys_back.reshape(pages_here, length, head_count, head_size)
    value_heads_back = values_back.reshape(pages_here, length, head_count, head_size)
    scores_back = scores_of(query_heads, key_heads_back, rel_terms, key_ok)
    probs_back = jnp.exp(scores_back - log_total)
    d_probs = jnp.einsum(
        "pihd,pjhd->phij", d_attended, value_heads_back, preferred_element_type=jnp.float32
    )
    inner_sum = jnp.sum(probs_back * d_probs, axis=-1, keepdims=True)
    d_scores = (probs_back * (d_probs - inner_sum)).astype(jnp.bfloat16)
    g_order = jnp.einsum(
        "phij,ijb->hb",
        d_scores,
        bucket_hot(order_bucket, bucket_count),
        preferred_element_type=jnp.float32,
    )
    g_horiz = jnp.einsum(
        "phij,pijb->hb",
        d_scores,
        bucket_hot(left_bucket, bucket_count),
        preferred_element_type=jnp.float32,
    )
    g_vert = jnp.einsum(
        "phij,pijb->hb",
        d_scores,
        bucket_hot(top_bucket, bucket_count),
        preferred_element_type=jnp.float32,
    )
    d_query = (
        jnp.einsum("phij,pjhd->pihd", d_scores, key_heads_back, preferred_element_type=jnp.float32)
        * SCALE
    ).astype(jnp.bfloat16)
    d_key_part = (
        jnp.einsum("phij,pihd->pjhd", d_scores, query_heads, preferred_element_type=jnp.float32)
        * SCALE
    )
    d_value_part = jnp.einsum(
        "phij,pihd->pjhd", probs_low, d_attended, preferred_element_type=jnp.float32
    )
    d_key_sum, d_value_sum = (
        lax.psum_scatter(
            d_key_part.reshape(pages_here, length, model_width),
            "seq",
            scatter_dimension=1,
            tiled=True,
        ),
        lax.psum_scatter(
            d_value_part.reshape(pages_here, length, model_width),
            "seq",
            scatter_dimension=1,
            tiled=True,
        ),
    )
    d_key_rows = d_key_sum.astype(jnp.bfloat16).reshape(row_count, model_width)
    d_value_rows = d_value_sum.astype(jnp.bfloat16).reshape(row_count, model_width)
    d_query_rows = d_query.reshape(row_count, model_width)
    g_query_bias = jnp.sum(d_query_rows, axis=0, dtype=jnp.float32)
    g_value_bias = jnp.sum(d_value_rows, axis=0, dtype=jnp.float32)
    g_query = jnp.einsum("re,rd->ed", entry_low, d_query_rows, preferred_element_type=jnp.float32)
    g_key = jnp.einsum("re,rd->ed", entry_low, d_key_rows, preferred_element_type=jnp.float32)
    g_value = jnp.einsum("re,rd->ed", entry_low, d_value_rows, preferred_element_type=jnp.float32)
    d_entry = (
        jnp.einsum("rd,ed->re", d_query_rows, proj_query, preferred_element_type=jnp.float32)
        + jnp.einsum("rd,ed->re", d_key_rows, proj_key, preferred_element_type=jnp.float32)
        + jnp.einsum("rd,ed->re", d_value_rows, proj_value, preferred_element_type=jnp.float32)
    )
    d_settled = (d_first_in + d_entry).reshape(pages_here, stretch_rows, model_width)
    text_grad = d_settled * text_keep
    grad_pad = padded_2(text_grad.astype(jnp.bfloat16), (("seq", 1),), 3).astype(text_grad.dtype)
    d_masked = jnp.zeros_like(text_grad)
    tap_sums = []
    for dilation in range(1, 4):
        for tap_index in range(3):
            offset = (tap_index - 1) * dilation
            d_masked = (
                d_masked
                + conv_text[dilation - 1, tap_index]
                * grad_pad[:, 3 - offset : 3 - offset + stretch_rows]
            )
            tap_sums.append(
                jnp.sum(
                    text_grad * padded_float[:, 3 + offset : 3 + offset + stretch_rows], axis=(0, 1)
                )
            )
    g_conv_text = jnp.stack(tap_sums).reshape(3, 3, model_width)
    patch_grad = lax.slice_in_dim(d_settled, patch_start, patch_start + patches, axis=1)
    patch_grad = patch_grad.reshape(pages_here, GRID, GRID, model_width) * is_last
    unused_out, patch_pull = jax.vjp(patch_conv, patch_rows, conv_patch)
    d_patch_rows, g_conv_patch = patch_pull(patch_grad)
    d_patch_full = jnp.concatenate(
        [before_zeros, d_patch_rows.reshape(pages_here, patches, model_width), after_zeros], axis=1
    )
    grad_tokens = d_settled + text_keep * d_masked + d_patch_full
    part_query, part_key, part_value, part_output, part_expand, part_reduce = (
        lax.psum_scatter(g_query, "pages", scatter_dimension=0, tiled=True),
        lax.psum_scatter(g_key, "pages", scatter_dimension=0, tiled=True),
        lax.psum_scatter(g_value, "pages", scatter_dimension=0, tiled=True),
        lax.psum_scatter(g_output, "pages", scatter_dimension=0, tiled=True),
        lax.psum_scatter(g_expand, "pages", scatter_dimension=0, tiled=True),
        lax.psum_scatter(g_reduce, "pages", scatter_dimension=0, tiled=True),
    )
    sum_query, sum_key, sum_value, sum_output, sum_expand, sum_reduce = lax.psum(
        (part_query, part_key, part_value, part_output, part_expand, part_reduce), "seq"
    )
    (
        s_conv_text,
        s_conv_patch,
        s_query_bias,
        s_value_bias,
        s_output_bias,
        s_order,
        s_horiz,
        s_vert,
        s_norm_gain,
        s_norm_shift,
        s_expand_bias,
        s_reduce_bias,
        s_final_gain,
        s_final_shift,
    ) = lax.psum(
        (
            g_conv_text,
            g_conv_patch,
            g_query_bias,
            g_value_bias,
            g_output_bias,
            g_order,
            g_horiz,
            g_vert,
            g_norm_gain,
            g_norm_shift,
            g_expand_bias,
            g_reduce_bias,
            g_final_gain,
            g_final_shift,
        ),
        ("pages", "seq"),
    )
    return (
        mixed_out,
        grad_tokens,
        s_conv_text,
        s_conv_patch,
        sum_query,
        s_query_bias,
        sum_key,
        sum_value,
        s_value_bias,
        sum_output,
        s_output_bias,
        s_order,
        s_horiz,
        s_vert,
        s_norm_gain,
        s_norm_shift,
        sum_expand,
        s_expand_bias,
        sum_reduce,
        s_reduce_bias,
        s_final_gain,
        s_final_shift,
    )


def solution(mesh):
    placed = (
        P("pages", "seq", None),
        P("pages", "seq", None),
        P(),
        P(),
        P(),
        P(),
        P(),
        P(),
        P(),
        P(),
        P(),
        P(),
        P(),
        P(),
        P(),
        P(),
        P(),
        P(),
        P(),
        P(),
        P(),
        P(),
        P("pages"),
        P("pages", None),
        P("pages", None),
    )
    return jax.shard_map(
        per_device,
        mesh=mesh,
        in_specs=placed,
        out_specs=(
            P("pages", "seq", None),
            P("pages", "seq", None),
            P(),
            P(),
            P("pages", None),
            P(),
            P("pages", None),
            P("pages", None),
            P(),
            P("pages", None),
            P(),
            P(),
            P(),
            P(),
            P(),
            P(),
            P("pages", None),
            P(),
            P("pages", None),
            P(),
            P(),
            P(),
        ),
        check_vma=False,
    )
```

profile of v0, /device:TPU:0, one launch (start us, length us, event | category | flops | bytes accessed | tf_op | source)
XLA Modules:
  0.0 1190.1 jit_solution(17617919925770286832)
XLA Ops:
  38.9 5.8 fusion.22
  51.1 25.0 %fusion = f32[4,144,576,12]{2,3,1,0:T(8,128)} fusion(f32[12,33]{1,0:T(8,128)S(1)} %copy-done.93, s32[4,144,576]{2,0,1:T(4,128)S(1)} %clamp_add_fusion), kind=kOutput, calls=%fused_computation.2 | convolution fusion | flops 1587548160 | bytes 17253936 | tf_op jit(solution)/shard_map/pijb,hb->phij/dot_general | solution.py:92
  76.2 25.2 %fusion.2 = f32[4,144,576,12]{2,3,1,0:T(8,128)} fusion(f32[12,33]{1,0:T(8,128)S(1)} %copy-done.94, s32[4,144,576]{2,0,1:T(4,128)S(1)} %clamp_add_fusion.1), kind=kOutput, calls=%fused_computation.4 | convolution fusion | flops 1587548160 | bytes 17253936 | tf_op jit(solution)/shard_map/pijb,hb->phij/dot_general | solution.py:86
  112.4 6.1 copy.93
  118.5 32.7 %fusion.63 = (f32[4,12,144]{2,1,0:T(8,128)S(1)}, f32[4,12,144,576]{3,2,1,0:T(8,128)}) fusion(f32[4,144,576,12]{2,3,1,0:T(8,128)} %fusion, f32[4,144,576,12]{2,3,1,0:T(8,128)} %fusion.2, f32[12,144,576]{2,1,0:T(8,128)} %copy.95, bf16[4,144,12,64]{1,3,2,0:T(8,128)(2,1)S(1)} %copy.94, bf16[4,576,12,64]{1,3,2,0:T(8,128)(2,1)} %bitcast.121, ...), kind=kOutput, calls=%fused_computation.200 | convolution fusion | flops 533488896 | bytes 56210688 | tf_op jit(solution)/shard_map/pihd,pjhd->phij/dot_general | solution.py:103
  151.2 9.4 fusion.6
  167.8 16.9 %all-gather.3.cloned.1.call-done = bf16[4,576,768]{2,1,0:T(8,128)(2,1)} async-done(((bf16[4,144,768]{2,1,0:T(8,128)(2,1)}), bf16[4,576,768]{2,1,0:T(8,128)(2,1)}) %all-gather.3.cloned.1.call-update) | async-done | bytes 3538960 | tf_op jit(solution)/shard_map/all_gather | solution.py:181
  184.7 6.0 copy.91
  190.7 8.3 fusion.35
  205.9 21.6 %multiply_convert_fusion.1 = (bf16[576,3072]{1,0:T(8,128)(2,1)S(1)}, f32[576,3072]{1,0:T(8,128)}, f32[576,3072]{1,0:T(8,128)}) fusion(f32[3072]{0:T(1024)S(1)} %copy-done.110, bf16[768,3072]{1,0:T(8,128)(2,1)} %param.41, f32[576,768]{1,0:T(8,128)S(1)} %get-tuple-element.117, f32[768]{0:T(1024)S(1)} %copy-done.52, f32[768]{0:T(1024)S(1)} %copy-done.51, ...), kind=kOutput, calls=%fused_computation.30 | convolution fusion | flops 2836905984 | bytes 24205824 | tf_op jit(solution)/shard_map/dot_general | solution.py:205
  239.2 10.8 convert_reduce_fusion.1
  250.1 7.7 multiply_reduce_fusion.1
  271.7 8.6 fusion.68
  280.3 8.8 copy.109
  289.2 17.5 %multiply_reduce_fusion = (f32[4,12,144]{2,1,0:T(8,128)S(1)}, f32[4,12,144,576]{3,2,1,0:T(8,128)}) fusion(f32[4,12,144,576]{3,2,1,0:T(8,128)} %get-tuple-element.115, f32[4,12,144]{2,1,0:T(8,128)S(1)} %log_add_fusion, bf16[4,144,12,64]{1,3,2,0:T(8,128)(2,1)} %copy.104, bf16[4,576,12,64]{1,3,2,0:T(8,128)(2,1)} %bitcast.124), kind=kOutput, calls=%fused_computation.12 | convolution fusion | flops 521544960 | bytes 36329472 | tf_op jit(solution)/shard_map/pihd,pjhd->phij/dot_general | solution.py:238
  306.8 14.8 %convert_reduce_fusion = (bf16[12,144,576]{2,1,0:T(8,128)(2,1)}, bf16[4,12,144,576]{3,2,1,0:T(8,128)(2,1)S(1)}) fusion(f32[4,12,144,576]{3,2,1,0:T(8,128)} %get-tuple-element.123, f32[4,12,144]{2,1,0:T(8,128)S(1)} %get-tuple-element.122, f32[4,12,144,576]{3,2,1,0:T(8,128)} %get-tuple-element.115, f32[4,12,144]{2,1,0:T(8,128)S(1)} %log_add_fusion), kind=kLoop, calls=%fused_computation.10 | loop fusion | flops 22892544 | bytes 41859072 | tf_op jit(solution)/shard_map/phij,ijb->hb/reduce_sum | solution.py:243
  327.4 8.8 copy.107
  341.3 8.6 convert_reduce_fusion.2
  360.5 8.7 fusion.71
  369.3 8.6 fusion.54
  377.9 33.5 %reduce-scatter.11.cloned.1.call-done = f32[4,144,768]{2,1,0:T(8,128)} async-done(((f32[4,576,768]{2,1,0:T(8,128)}), f32[4,144,768]{2,1,0:T(8,128)}) %reduce-scatter.11.cloned.1.call-update) | async-done | bytes 1769488 | tf_op jit(solution)/shard_map/reduce_scatter | solution.py:279
  422.8 12.8 %fusion.38 = f32[12,33]{1,0:T(8,128)} fusion(bf16[4,12,144,576]{3,2,1,0:T(8,128)(2,1)} %copy-done.9, s32[4,144,576]{2,0,1:T(4,128)S(1)} %copy-done.8), kind=kOutput, calls=%fused_computation.117 | convolution fusion | flops 273715200 | bytes 9291312 | tf_op jit(solution)/shard_map/phij,pijb->hb/dot_general | solution.py:249
  435.6 102.0 %reduce-scatter.9.cloned.1.call-done = f32[4,144,768]{2,1,0:T(8,128)} async-done(((f32[4,576,768]{2,1,0:T(8,128)}), f32[4,144,768]{2,1,0:T(8,128)}) %reduce-scatter.9.cloned.1.call-update) | async-done | bytes 1769488 | tf_op jit(solution)/shard_map/reduce_scatter | solution.py:273
  547.2 13.4 %fusion.41 = f32[12,33]{1,0:T(8,128)} fusion(bf16[4,12,144,576]{3,2,1,0:T(8,128)(2,1)} %copy-done.9, s32[4,144,576]{2,0,1:T(4,128)S(1)} %copy-done.6), kind=kOutput, calls=%fused_computation.118 | convolution fusion | flops 273715200 | bytes 9291312 | tf_op jit(solution)/shard_map/phij,pijb->hb/dot_general | solution.py:255
  571.9 11.9 %reduce-scatter.19.cloned.1.call-done = f32[96,768]{1,0:T(8,128)} async-done(((f32[768,768]{1,0:T(8,128)}), f32[96,768]{1,0:T(8,128)}) %reduce-scatter.19.cloned.1.call-update) | async-done | bytes 294928 | tf_op jit(solution)/shard_map/reduce_scatter | solution.py:330
  583.9 46.1 %reduce-scatter.13.cloned.1.call-done = f32[96,768]{1,0:T(8,128)} async-done(((f32[768,768]{1,0:T(8,128)}), f32[96,768]{1,0:T(8,128)}) %reduce-scatter.13.cloned.1.call-update) | async-done | bytes 294928 | tf_op jit(solution)/shard_map/reduce_scatter | solution.py:327
  630.0 80.0 %reduce-scatter.23.cloned.1.call-done = f32[384,768]{1,0:T(8,128)} async-done(((f32[3072,768]{1,0:T(8,128)}), f32[384,768]{1,0:T(8,128)}) %reduce-scatter.23.cloned.1.call-update) | async-done | bytes 1179664 | tf_op jit(solution)/shard_map/reduce_scatter | solution.py:332
  710.0 80.0 %reduce-scatter.21.cloned.1.call-done = f32[96,3072]{1,0:T(8,128)} async-done(((f32[768,3072]{1,0:T(8,128)}), f32[96,3072]{1,0:T(8,128)}) %reduce-scatter.21.cloned.1.call-update) | async-done | bytes 1179664 | tf_op jit(solution)/shard_map/reduce_scatter | solution.py:331
  790.0 45.9 %reduce-scatter.17.cloned.1.call-done = f32[96,768]{1,0:T(8,128)} async-done(((f32[768,768]{1,0:T(8,128)}), f32[96,768]{1,0:T(8,128)}) %reduce-scatter.17.cloned.1.call-update) | async-done | bytes 294928 | tf_op jit(solution)/shard_map/reduce_scatter | solution.py:329
  835.9 46.1 %reduce-scatter.15.cloned.1.call-done = f32[96,768]{1,0:T(8,128)} async-done(((f32[768,768]{1,0:T(8,128)}), f32[96,768]{1,0:T(8,128)}) %reduce-scatter.15.cloned.1.call-update) | async-done | bytes 294928 | tf_op jit(solution)/shard_map/reduce_scatter | solution.py:328
  894.8 128.4 %all-reduce.24.cloned.1.call-done = (f32[3,3,768]{2,1,0:T(4,128)}, f32[3,3,768]{2,1,0:T(4,128)}, f32[768]{0:T(1024)}, f32[768]{0:T(1024)}, f32[768]{0:T(1024)}, ...) async-done(((f32[3,3,768]{2,1,0:T(4,128)}, ...) | async-done | bytes 96928 | tf_op jit(solution)/shard_map/psum | solution.py:352
  1023.2 140.9 %all-reduce.26.cloned.1.call-done = (f32[96,768]{1,0:T(8,128)}, f32[96,768]{1,0:T(8,128)}, f32[96,768]{1,0:T(8,128)}, f32[96,768]{1,0:T(8,128)}, f32[96,3072]{1,0:T(8,128)}, /*index=5*/f32[384,768]{1,0:T(8,128)}) async-done(((f32[96,768]{1,0:T(8,128)}, f32[96,768]{1,0:T(8,128)}, f32[96,768]{1,0:T(8,128)}, f32[96,768]{1,0:T(8,128)}, f32[96,3072]{1,0:T(8,128)}, /*index=5*/f32[384,768]{1,0:T(8,128)}), ...) | async-done | bytes 3538960 | tf_op jit(solution)/shard_map/psum | solution.py:334
  (392 shorter events, 173.1 us)
Async XLA Ops:
  7.2 195.0 %copy-start = (bf16[768,768]{1,0:T(8,128)(2,1)S(1)}, bf16[768,768]{1,0:T(8,128)(2,1)}, u32[]{:S(2)}) copy-start(bf16[768,768]{1,0:T(8,128)(2,1)} %param.34) | copy-start | bytes 3538948
  7.2 105.2 %all-gather.5.cloned.1.call-start = ((), (), s32[]{:S(2)}) async-start(), calls=%async_computation.9 | async-start | bytes 4423680 | tf_op jit(solution)/shard_map/all_gather | solution.py:180
  10.2 20.4 %collective-permute-start = (bf16[4,3,768]{2,1,0:T(4,128)(2,1)}, bf16[4,3,768]{2,1,0:T(4,128)(2,1)}, u32[]{:S(2)}, u32[]{:S(2)}) collective-permute-start(bf16[4,3,768]{2,1,0:T(4,128)(2,1)} %get-tuple-element.103), channel_id=1, source_target_pairs={{0,1},{1,2},{2,3},{4,5},{5,6},{6,7},{8,9},{9,10},{10,11},{12,13},{... | collective-permute-start | bytes 55304 | tf_op jit(solution)/shard_map/ppermute | solution.py:23
  15.7 14.9 %collective-permute-start.1 = (bf16[4,3,768]{2,1,0:T(4,128)(2,1)}, bf16[4,3,768]{2,1,0:T(4,128)(2,1)}, u32[]{:S(2)}, u32[]{:S(2)}) collective-permute-start(bf16[4,3,768]{2,1,0:T(4,128)(2,1)} %get-tuple-element.104), channel_id=1, source_target_pairs={{1,0},{2,1},{3,2},{5,4},{6,5},{7,6},{9,8},{10,9},{11,10},{13,12},{... | collective-permute-start | bytes 55304 | tf_op jit(solution)/shard_map/ppermute | solution.py:24
  36.8 64.6 %copy-start.45 = (bf16[576,768]{1,0:T(8,128)(2,1)}, bf16[576,768]{1,0:T(8,128)(2,1)S(1)}, u32[]{:S(2)}) copy-start(bf16[576,768]{1,0:T(8,128)(2,1)S(1)} %bitcast_convert_fusion) | copy-start | bytes 2654212
  38.6 146.1 %all-gather.3.cloned.1.call-start = ((), (), s32[]{:S(2)}) async-start(), calls=%async_computation.8 | async-start | bytes 4423680 | tf_op jit(solution)/shard_map/all_gather | solution.py:181
  49.5 26.6 %copy-start.7 = (s32[4,144,576]{2,0,1:T(4,128)}, s32[4,144,576]{2,0,1:T(4,128)S(1)}, u32[]{:S(2)}) copy-start(s32[4,144,576]{2,0,1:T(4,128)S(1)} %clamp_add_fusion.1) | copy-start | bytes 3981316
  51.1 25.0 %copy-start.94 = (f32[12,33]{1,0:T(8,128)S(1)}, f32[12,33]{1,0:T(8,128)}, u32[]{:S(2)}) copy-start(f32[12,33]{1,0:T(8,128)} %param.37) | copy-start | bytes 4756
  76.1 25.2 %copy-start.107 = (bf16[768,768]{1,0:T(8,128)(2,1)S(1)}, bf16[768,768]{1,0:T(8,128)(2,1)}, u32[]{:S(2)}) copy-start(bf16[768,768]{1,0:T(8,128)(2,1)} %param.29) | copy-start | bytes 3538948
  76.1 25.2 %copy-start.111 = (f32[768]{0:T(1024)S(1)}, f32[768]{0:T(1024)}, u32[]{:S(2)}) copy-start(f32[768]{0:T(1024)} %param.30) | copy-start | bytes 9220
  112.3 299.1 %reduce-scatter.11.cloned.1.call-start = ((), (), s32[]{:S(2)}) async-start(), calls=%async_computation.11 | async-start | bytes 8847360 | tf_op jit(solution)/shard_map/reduce_scatter | solution.py:279
  202.3 25.3 %slice-start = ((s8[4718592]{0:T(1024)(128)(4,1)}), s8[4194304]{0:T(1024)(128)(4,1)S(1)}, s32[]{:S(2)}) async-start(s8[4718592]{0:T(1024)(128)(4,1)} %bitcast.142), calls=%async_computation.20 | async-start | bytes 8388608
  289.1 248.5 %reduce-scatter.9.cloned.1.call-start = ((), (), s32[]{:S(2)}) async-start(), calls=%async_computation.10 | async-start | bytes 8847360 | tf_op jit(solution)/shard_map/reduce_scatter | solution.py:273
  336.3 247.6 %reduce-scatter.19.cloned.1.call-start = ((), (), s32[]{:S(2)}) async-start(), calls=%async_computation.15 | async-start | bytes 2654208 | tf_op jit(solution)/shard_map/reduce_scatter | solution.py:330
  341.2 288.7 %reduce-scatter.13.cloned.1.call-start = ((), (), s32[]{:S(2)}) async-start(), calls=%async_computation.12 | async-start | bytes 2654208 | tf_op jit(solution)/shard_map/reduce_scatter | solution.py:327
  359.4 350.6 %reduce-scatter.23.cloned.1.call-start = ((), (), s32[]{:S(2)}) async-start(), calls=%async_computation.17 | async-start | bytes 10616832 | tf_op jit(solution)/shard_map/reduce_scatter | solution.py:332
  369.2 420.8 %reduce-scatter.21.cloned.1.call-start = ((), (), s32[]{:S(2)}) async-start(), calls=%async_computation.16 | async-start | bytes 10616832 | tf_op jit(solution)/shard_map/reduce_scatter | solution.py:331
  377.9 35.8 %copy-start.46 = (bf16[4,144,768]{2,1,0:T(8,128)(2,1)S(1)}, bf16[4,144,768]{2,1,0:T(8,128)(2,1)}, u32[]{:S(2)}) copy-start(bf16[4,144,768]{2,1,0:T(8,128)(2,1)} %get-tuple-element.80) | copy-start | bytes 2654212
  377.9 458.0 %reduce-scatter.17.cloned.1.call-start = ((), (), s32[]{:S(2)}) async-start(), calls=%async_computation.14 | async-start | bytes 2654208 | tf_op jit(solution)/shard_map/reduce_scatter | solution.py:329
  416.2 465.7 %reduce-scatter.15.cloned.1.call-start = ((), (), s32[]{:S(2)}) async-start(), calls=%async_computation.13 | async-start | bytes 2654208 | tf_op jit(solution)/shard_map/reduce_scatter | solution.py:328
  435.6 103.6 %copy-start.47 = (bf16[4,144,768]{2,1,0:T(8,128)(2,1)S(1)}, bf16[4,144,768]{2,1,0:T(8,128)(2,1)}, u32[]{:S(2)}) copy-start(bf16[4,144,768]{2,1,0:T(8,128)(2,1)} %get-tuple-element.80) | copy-start | bytes 2654212
  541.8 481.3 %all-reduce.24.cloned.1.call-start = ((), (), s32[]{:S(2)}) async-start(), calls=%async_computation.18 | async-start | bytes 286720 | tf_op jit(solution)/shard_map/psum | solution.py:352
  571.9 592.3 %all-reduce.26.cloned.1.call-start = ((), (), s32[]{:S(2)}) async-start(), calls=%async_computation.19 | async-start | bytes 7077888 | tf_op jit(solution)/shard_map/psum | solution.py:334
  882.0 8.4 collective-permute-start.2
  885.6 5.7 collective-permute-start.3
  1023.2 150.3 %copy-start.105 = (f32[768]{0:T(1024)S(1)}, f32[768]{0:T(1024)}, u32[]{:S(2)}) copy-start(f32[768]{0:T(1024)} %get-tuple-element.136) | copy-start | bytes 9220
  1023.2 151.6 %copy-start.104 = (f32[768]{0:T(1024)S(1)}, f32[768]{0:T(1024)}, u32[]{:S(2)}) copy-start(f32[768]{0:T(1024)} %get-tuple-element.138) | copy-start | bytes 9220
  1023.2 152.2 %copy-start.97 = (f32[12,33]{1,0:T(8,128)S(1)}, f32[12,33]{1,0:T(8,128)}, u32[]{:S(2)}) copy-start(f32[12,33]{1,0:T(8,128)} %get-tuple-element.139) | copy-start | bytes 4756
  1023.2 152.8 %copy-start.96 = (f32[12,33]{1,0:T(8,128)S(1)}, f32[12,33]{1,0:T(8,128)}, u32[]{:S(2)}) copy-start(f32[12,33]{1,0:T(8,128)} %get-tuple-element.140) | copy-start | bytes 4756
  1023.2 153.4 %copy-start.95 = (f32[12,33]{1,0:T(8,128)S(1)}, f32[12,33]{1,0:T(8,128)}, u32[]{:S(2)}) copy-start(f32[12,33]{1,0:T(8,128)} %get-tuple-element.141) | copy-start | bytes 4756
  1023.2 154.0 %copy-start.103 = (f32[768]{0:T(1024)S(1)}, f32[768]{0:T(1024)}, u32[]{:S(2)}) copy-start(f32[768]{0:T(1024)} %get-tuple-element.142) | copy-start | bytes 9220
  1023.2 154.6 %copy-start.102 = (f32[768]{0:T(1024)S(1)}, f32[768]{0:T(1024)}, u32[]{:S(2)}) copy-start(f32[768]{0:T(1024)} %get-tuple-element.143) | copy-start | bytes 9220
  (102 other events, 418.9 us)
Sparse Core Ops, SparseCore 0:
  38.7 72.2 all-gather.4
  113.2 71.5 all-gather.2
  289.3 122.1 reduce-scatter.10
  413.6 124.0 reduce-scatter.8
  540.8 42.9 reduce-scatter.18
  587.4 42.4 reduce-scatter.12
  633.5 76.4 reduce-scatter.22
  713.5 76.4 reduce-scatter.20
  793.3 42.5 reduce-scatter.16
  839.4 42.4 reduce-scatter.14
  890.1 133.0 all-reduce.23
  1025.9 138.2 all-reduce.25
where the time goes:
time: 1200 us; the launch traced here: 1190 us
  waiting for transfers between devices  733 us (61%)
  matrix products  255 us (21%)
  local copies, waits for them, and re-layouts  103 us (9%)
  other arithmetic  70 us (6%)
  between operations  16.2 us (1%)
  starting transfers between devices  12.3 us (1%)
    psum x1, waiting for transfers between devices, per_device(): lax.psum((part_query, part_key, part_value, part_output, part_expand, par...  141 us
    psum x1, waiting for transfers between devices, per_device(): lax.psum((g_conv_text, g_conv_patch, g_query_bias, g_value_bias, g_output...  128 us
    reduce_scatter x1, waiting for transfers between devices, per_device(): lax.psum_scatter(d_key_part.reshape(pages_here, length, model_width), 'se...  102 us
    reduce_scatter x1, waiting for transfers between devices, per_device(): lax.psum_scatter(g_expand, 'pages', scatter_dimension=0, tiled=True)  80 us
    reduce_scatter x1, waiting for transfers between devices, per_device(): lax.psum_scatter(g_reduce, 'pages', scatter_dimension=0, tiled=True)  80 us
    reduce_scatter x1, waiting for transfers between devices, per_device(): lax.psum_scatter(g_query, 'pages', scatter_dimension=0, tiled=True)  46.1 us
    reduce_scatter x1, waiting for transfers between devices, per_device(): lax.psum_scatter(g_key, 'pages', scatter_dimension=0, tiled=True)  46.1 us
    reduce_scatter x1, waiting for transfers between devices, per_device(): lax.psum_scatter(g_value, 'pages', scatter_dimension=0, tiled=True)  45.9 us
  transfers between devices with their start and end apart: 16, of which 12 were waited for; matrix products, arithmetic and copies ran while one was open for 24% of the time, Pallas kernels for 0%

commit v1 on v0

v1 whole, which is shorter than its diff:
```python
import jax
import jax.numpy as jnp
from jax import lax
from jax.experimental import pallas as pl
from jax.experimental.pallas import tpu as pltpu
from jax.sharding import PartitionSpec as P

BF = jnp.bfloat16
F32 = jnp.float32
TEXT = 512
GRID = 7
SPAN = 16
EPS = 1e-06
SCALE = 0.125
NEG = -1e30
RT = 64
BOX = 64


def order_offsets():
    return (-128,-64,0,64)

def table_prep(rel_order, rel_horiz, rel_vert):
    heads, nb = rel_order.shape
    a=jnp.arange(64)[:,None]; c=jnp.arange(64)[None,:]
    b=jnp.clip(c-a,-SPAN,SPAN)+SPAN
    oh=(b.reshape(-1)[None,:]==jnp.arange(nb)[:,None]).astype(F32)
    th=jnp.dot(rel_horiz,oh,precision=lax.Precision.HIGHEST).reshape(heads,64,64)
    tv=jnp.dot(rel_vert,oh,precision=lax.Precision.HIGHEST).reshape(heads,64,64)
    z=jnp.zeros_like(th)
    def hl(x):
        hi=lax.reduce_precision(x,8,7)
        return hi, x-hi
    hh,hlo=hl(th); vh,vlo=hl(tv)
    top=jnp.concatenate([hh,z,hlo,z],2); bot=jnp.concatenate([z,vh,z,vlo],2)
    wt=jnp.concatenate([top,bot],1).astype(BF)
    i=jnp.arange(RT)[:,None]; j=jnp.arange(128)[None,:]
    ob=jnp.stack([jnp.clip(d+j-i,-SPAN,SPAN)+SPAN for d in order_offsets()])
    ohd=(ob.reshape(-1)[None,:]==jnp.arange(nb)[:,None]).astype(F32)
    od=jnp.dot(rel_order,ohd,precision=lax.Precision.HIGHEST).reshape(heads,4,RT,128)
    return wt, od

def fwd_kernel(edge_ref,q_ref,k_ref,v_ref,oh_ref,wt_ref,ord_ref,mask_ref,p_ref,o_ref,qa_ref,ka_ref,s_ref):
    g=pl.program_id(0)
    L=q_ref.shape[0]
    @pl.when(g==0)
    def _():
        ka_ref[:,128:256]=oh_ref[...]
        ka_ref[:,256:384]=oh_ref[...]
    ka_ref[:,0:128]=k_ref[...]
    lane=lax.broadcasted_iota(jnp.int32,(L,128),1)
    for e in range(2):
        keep=(lane<64) if e==0 else (lane>=64)
        qa_ref[e,:,0:128]=jnp.where(keep,q_ref[...],jnp.zeros((),BF))
        qa_ref[e,:,128:384]=jnp.dot(oh_ref[...],wt_ref[e],preferred_element_type=F32).astype(BF)
        s_ref[e]=lax.dot_general(qa_ref[e],ka_ref[...],(((1,),(1,)),((),())),preferred_element_type=F32)
    outs=[]
    nj=(L+127)//128
    for e in range(2):
        h=2*g+e
        left=edge_ref[h,0]; right=edge_ref[h,1]
        for a in range(L//RT):
            r0=a*RT
            cols=[]
            for b in range(nj):
                w=min(128,L-128*b); d=128*b-RT*a
                t=s_ref[e,r0:r0+RT,128*b:128*b+w]+mask_ref[:,128*b:128*b+w]
                if d in order_offsets():
                    t=t+ord_ref[e,order_offsets().index(d)][:,:w]
                elif d<0: t=t+left
                else: t=t+right
                cols.append(t)
            t=jnp.concatenate(cols,1)
            m=jnp.max(t,axis=1,keepdims=True)
            ex=jnp.exp(t-m)
            tot=jnp.sum(ex,axis=1,keepdims=True)
            p_ref[e,r0:r0+RT,:]=(ex*(1.0/tot)).astype(BF)
        outs.append(jnp.dot(p_ref[e],v_ref[...],preferred_element_type=F32))
    o_ref[...]=jnp.where(lane<64,outs[0],outs[1]).astype(BF)

def attn_fwd(q,k,v,oh,wt,od,edge,mask):
    L,D=q.shape; H=wt.shape[0]
    col=pl.BlockSpec((L,128),lambda g,*_:(0,g))
    full=lambda shp: pl.BlockSpec(shp,lambda g,*_:(0,)*len(shp))
    return pl.pallas_call(fwd_kernel,
        out_shape=(jax.ShapeDtypeStruct((H,L,L),BF),jax.ShapeDtypeStruct((L,D),BF)),
        grid_spec=pltpu.PrefetchScalarGridSpec(num_scalar_prefetch=1,grid=(H//2,),
            in_specs=[col,col,col,full((L,128)),pl.BlockSpec((2,128,256),lambda g,*_:(g,0,0)),
                      pl.BlockSpec((2,4,RT,128),lambda g,*_:(g,0,0,0)),full((1,L))],
            out_specs=[pl.BlockSpec((2,L,L),lambda g,*_:(g,0,0)),col],
            scratch_shapes=[pltpu.VMEM((2,L,384),BF),pltpu.VMEM((L,384),BF),pltpu.VMEM((2,L,L),F32)]),
        name="attn_fwd",
    )(edge,q,k,v,oh,wt,od,mask)

def bwd_kernel(p_ref,q_ref,k_ref,v_ref,do_ref,o_ref,oh_ref,oht_ref,
               dq_ref,dk_ref,dv_ref,hist_ref,ord_ref,va_ref,rhs_ref,ds_ref,dp_ref):
    g=pl.program_id(0)
    L=q_ref.shape[0]
    lane=lax.broadcasted_iota(jnp.int32,(L,128),1)
    @pl.when(g==0)
    def _():
        va_ref[:,128:256]=jnp.where(lane<2,1.0,0.0).astype(BF)
        rhs_ref[:,128:256]=oh_ref[...]
    va_ref[:,0:128]=v_ref[...]
    rhs_ref[:,0:128]=k_ref[...]
    nj=(L+127)//128
    do=do_ref[...]
    prod=do.astype(F32)*o_ref[...].astype(F32)
    res=[]
    for e in range(2):
        keep=(lane<64) if e==0 else (lane>=64)
        inner=-jnp.sum(jnp.where(keep,prod,0.0),axis=1,keepdims=True)
        hi=inner.astype(BF); lo=(inner-hi.astype(F32)).astype(BF)
        ext=jnp.where(lane==0,jnp.broadcast_to(hi.astype(F32),(L,128)),jnp.where(lane==1,jnp.broadcast_to(lo.astype(F32),(L,128)),0.0)).astype(BF)
        da=jnp.concatenate([jnp.where(keep,do,jnp.zeros((),BF)),ext],1)
        dp_ref[e]=lax.dot_general(da,va_ref[...],(((1,),(1,)),((),())),preferred_element_type=F32)
    for e in range(2):
        accs={}
        for a in range(L//RT):
            r0=a*RT
            pf=p_ref[e,r0:r0+RT,:].astype(F32)
            ds=pf*dp_ref[e,r0:r0+RT,:]
            ds_ref[e,r0:r0+RT,:]=ds.astype(BF)
            for b in range(nj):
                w=min(128,L-128*b); d=128*b-RT*a
                t=ds[:,128*b:128*b+w]
                if w<128: t=jnp.concatenate([t,jnp.zeros((RT,128-w),F32)],1)
                key=order_offsets().index(d) if d in order_offsets() else (4 if d<0 else 5)
                accs[key]=t if key not in accs else accs[key]+t
        for key in range(6):
            ord_ref[e,key]=accs[key]
        r=jnp.dot(ds_ref[e],rhs_ref[...],preferred_element_type=F32)
        gg=r[:,128:256]
        ghi=gg.astype(BF); glo=(gg-ghi.astype(F32)).astype(BF)
        hh=jnp.dot(oht_ref[...],jnp.concatenate([ghi,glo],1),preferred_element_type=F32)
        hist_ref[e]=hh[:,0:128]+hh[:,128:256]
        dk=lax.dot_general(ds_ref[e],q_ref[...],(((0,),(0,)),((),())),preferred_element_type=F32)
        dv=lax.dot_general(p_ref[e],do,(((0,),(0,)),((),())),preferred_element_type=F32)
        res.append((r[:,0:128],dk,dv))
    first=lane<64
    dq_ref[...]=(jnp.where(first,res[0][0],res[1][0])*0.125).astype(BF)
    dk_ref[...]=jnp.where(first,res[0][1],res[1][1]).astype(BF)
    dv_ref[...]=jnp.where(first,res[0][2],res[1][2]).astype(BF)

def attn_bwd(p,q,k,v,do,o,oh,oht):
    L,D=q.shape; H=p.shape[0]
    col=pl.BlockSpec((L,128),lambda g:(0,g))
    full=lambda shp: pl.BlockSpec(shp,lambda g:(0,)*len(shp))
    return pl.pallas_call(bwd_kernel,
        out_shape=(jax.ShapeDtypeStruct((L,D),BF),)*3+(jax.ShapeDtypeStruct((H,128,128),F32),jax.ShapeDtypeStruct((H,6,RT,128),F32)),
        grid=(H//2,),
        in_specs=[pl.BlockSpec((2,L,L),lambda g:(g,0,0)),col,col,col,col,col,full((L,128)),full((128,L))],
        out_specs=[col,col,col,pl.BlockSpec((2,128,128),lambda g:(g,0,0)),pl.BlockSpec((2,6,RT,128),lambda g:(g,0,0,0))],
        scratch_shapes=[pltpu.VMEM((L,256),BF),pltpu.VMEM((L,256),BF),pltpu.VMEM((2,L,L),BF),pltpu.VMEM((2,L,L),F32)],
        name="attn_bwd",
    )(p,q,k,v,do,o,oh,oht)


def xor_pairs(n, bit):
    return [(i, i ^ bit) for i in range(n)]


def swap(value, axis, bit):
    return lax.ppermute(value, axis, xor_pairs(lax.axis_size(axis), bit))


def page_in(blocks):
    n = lax.axis_size("seq")
    place = lax.axis_index("seq")
    got = [lax.dynamic_index_in_dim(blocks, place, 0, keepdims=True)]
    for d in range(1, n):
        part = lax.dynamic_index_in_dim(blocks, lax.rem(place + d, n), 0, keepdims=True)
        got.append(lax.ppermute(part, "seq", [(i, (i + d) % n) for i in range(n)]))
    ring = jnp.concatenate(got[::-1] * 2, axis=0)
    return lax.dynamic_slice_in_dim(ring, n - 1 - place, n, 0)


def halve(value, ids, bit):
    pos = [i for i, x in enumerate(ids) if not x & bit]
    kept = [x for x in ids if not x & bit]
    low = jnp.concatenate([value[i : i + 1] for i in pos], 0) if len(pos) > 1 else value[pos[0] : pos[0] + 1]
    pos1 = [i for i, x in enumerate(ids) if x & bit]
    high = jnp.concatenate([value[i : i + 1] for i in pos1], 0) if len(pos1) > 1 else value[pos1[0] : pos1[0] + 1]
    mine = (lax.axis_index("pages") & bit) != 0
    keep = jnp.where(mine, high, low)
    send = jnp.where(mine, low, high)
    got = swap(send, "pages", bit)
    return (keep.astype(F32) + got.astype(F32)).astype(BF), kept


def scatter_pages(value):
    n = value.shape[0]
    bits = []
    b = 1
    while b < n:
        bits.append(b)
        b *= 2
    ids = list(range(n))
    value, ids = halve(value, ids, bits[0])
    half = value.shape[2] // 2
    parts = []
    for order, piece in ((bits[1:], value[:, :, :half]), (bits[1:][::-1], value[:, :, half:])):
        left = ids
        for bit in order:
            piece, left = halve(piece, left, bit)
        parts.append(piece)
    return jnp.concatenate(parts, 2)[0]


def sum_seq(value):
    n = lax.axis_size("seq")
    place = lax.axis_index("seq")
    rows, cols = value.shape
    quarters = value.reshape(n, rows // n, cols)
    total = lax.dynamic_index_in_dim(quarters, place, 0, keepdims=False).astype(F32)
    for d in range(1, n):
        part = lax.dynamic_index_in_dim(quarters, lax.rem(place + d, n), 0, keepdims=False)
        total = total + lax.ppermute(part, "seq", [(i, (i + d) % n) for i in range(n)]).astype(F32)
    total = total.astype(BF)[None]
    got = [total] + [lax.ppermute(total, "seq", [(i, (i + d) % n) for i in range(n)]) for d in range(1, n)]
    ring = jnp.concatenate(got[::-1] * 2, axis=0)
    return lax.dynamic_slice_in_dim(ring, n - 1 - place, n, 0).reshape(rows, cols)


def sum_all(value):
    b = 1
    while b < lax.axis_size("pages"):
        value = value + swap(value, "pages", b)
        b *= 2
    b = 1
    while b < lax.axis_size("seq"):
        value = value + swap(value, "seq", b)
        b *= 2
    return value


def layer_norm(inputs, gain_vec, shift_vec):
    average = jnp.mean(inputs, axis=-1, keepdims=True)
    centred = inputs - average
    variance = jnp.mean(centred * centred, axis=-1, keepdims=True)
    return centred * lax.rsqrt(variance + EPS) * gain_vec + shift_vec


def gelu_exact(inputs):
    return jax.nn.gelu(inputs, approximate=False)


def shifted(value, offset):
    rows = value.shape[0]
    if offset == 0:
        return value
    zeros = jnp.zeros((abs(offset),) + value.shape[1:], value.dtype)
    if offset > 0:
        return jnp.concatenate([value[offset:], zeros], 0)
    return jnp.concatenate([zeros, value[: rows + offset]], 0)


def patch_conv(patch_rows, conv_patch):
    side = patch_rows.shape[0]
    grid_pad = jnp.pad(patch_rows, ((1, 1), (1, 1), (0, 0)))
    running = jnp.zeros_like(patch_rows)
    for across in range(3):
        for down_index in range(3):
            running = running + conv_patch[across, down_index] * grid_pad[across : across + side, down_index : down_index + side]
    return running


def per_device(
    tokens, cotangent, conv_text, conv_patch, proj_query, bias_query, proj_key, proj_value, bias_value,
    proj_output, bias_output, rel_order, rel_horiz, rel_vert, norm_gain, norm_shift, expand_weight,
    expand_bias, reduce_weight, reduce_bias, final_gain, final_shift, text_count, box_left, box_top,
):
    pages_here, stretch, width = tokens.shape
    n_seq = lax.axis_size("seq")
    n_pages = lax.axis_size("pages")
    place = lax.axis_index("seq")
    length = stretch * n_seq
    heads = rel_order.shape[0]
    patches = GRID * GRID
    pick = lambda a: lax.dynamic_index_in_dim(a, place, 0, keepdims=False)
    count, left, top = pick(text_count), pick(box_left), pick(box_top)
    pos = jnp.arange(length, dtype=jnp.int32)
    keep = (pos < count).astype(F32)[:, None]
    key_ok = (pos < count) | ((pos >= TEXT) & (pos < TEXT + patches))
    mask = jnp.where(key_ok, 0.0, NEG).astype(F32)[None]
    cells = jnp.arange(BOX, dtype=jnp.int32)
    oh = jnp.concatenate([left[:, None] == cells[None], top[:, None] == cells[None]], 1).astype(BF)
    oht = jnp.concatenate([left[None] == cells[:, None], top[None] == cells[:, None]], 0).astype(BF)
    edge = jnp.stack([rel_order[:, 0], rel_order[:, -1]], 1)
    wt, od = table_prep(rel_order, rel_horiz, rel_vert)

    page = page_in(tokens).reshape(length, width).astype(F32)
    d_out = page_in(cotangent).reshape(length, width).astype(F32)

    masked = page * keep
    text_term = jnp.zeros_like(page)
    for s in range(1, 4):
        for t in range(3):
            text_term = text_term + conv_text[s - 1, t] * shifted(masked, (t - 1) * s)
    patch_rows = page[TEXT : TEXT + patches].reshape(GRID, GRID, width)
    patch_term = patch_conv(patch_rows, conv_patch).reshape(patches, width)
    above = jnp.zeros((TEXT, width), F32)
    below = jnp.zeros((length - TEXT - patches, width), F32)
    settled = page + keep * text_term + jnp.concatenate([above, patch_term, below], 0)
    entry = settled.astype(BF)
    query = (jnp.dot(entry, proj_query, preferred_element_type=F32) + bias_query).astype(BF)
    key = jnp.dot(entry, proj_key, preferred_element_type=F32).astype(BF)
    value = (jnp.dot(entry, proj_value, preferred_element_type=F32) + bias_value).astype(BF)
    query = query * jnp.asarray(SCALE, BF)
    probs, attended = attn_fwd(query, key, value, oh, wt, od, edge, mask)
    branch = jnp.dot(attended, proj_output, preferred_element_type=F32) + bias_output
    first_norm, norm_pull = jax.vjp(layer_norm, settled + branch, norm_gain, norm_shift)
    first_low = first_norm.astype(BF)
    expanded = jnp.dot(first_low, expand_weight, preferred_element_type=F32) + expand_bias
    activated_float, gelu_pull = jax.vjp(gelu_exact, expanded)
    activated = activated_float.astype(BF)
    reduced = jnp.dot(activated, reduce_weight, preferred_element_type=F32) + reduce_bias
    mixed_float, final_pull = jax.vjp(layer_norm, first_norm + reduced, final_gain, final_shift)
    mixed_out = page_in(mixed_float.astype(BF).reshape(n_seq, stretch, width))
    d_second, g_final_gain, g_final_shift = final_pull(d_out)
    d_reduced = d_second.astype(BF)
    g_reduce_bias = jnp.sum(d_reduced, axis=0, dtype=F32)
    g_reduce = jnp.einsum("rf,rd->fd", activated, d_reduced, preferred_element_type=F32).astype(BF)
    d_activated = jnp.einsum("rd,fd->rf", d_reduced, reduce_weight, preferred_element_type=F32)
    d_expanded = gelu_pull(d_activated)[0].astype(BF)
    g_expand_bias = jnp.sum(d_expanded, axis=0, dtype=F32)
    g_expand = jnp.einsum("rd,rf->df", first_low, d_expanded, preferred_element_type=F32).astype(BF)
    d_first = d_second + jnp.einsum("rf,df->rd", d_expanded, expand_weight, preferred_element_type=F32)
    d_first_in, g_norm_gain, g_norm_shift = norm_pull(d_first)
    d_branch = d_first_in.astype(BF)
    g_output_bias = jnp.sum(d_branch, axis=0, dtype=F32)
    g_output = jnp.einsum("re,rd->ed", attended, d_branch, preferred_element_type=F32).astype(BF)
    d_attended = jnp.einsum("rd,ed->re", d_branch, proj_output, preferred_element_type=F32).astype(BF)

    d_query, d_key, d_value, hist, ords = attn_bwd(probs, query, key, value, d_attended, attended, oh, oht)

    g_query_bias = jnp.sum(d_query, axis=0, dtype=F32)
    g_value_bias = jnp.sum(d_value, axis=0, dtype=F32)
    g_query, g_key, g_value = (
        jnp.einsum("re,rd->ed", entry, d, preferred_element_type=F32).astype(BF) for d in (d_query, d_key, d_value)
    )
    d_entry = (
        jnp.einsum("rd,ed->re", d_query, proj_query, preferred_element_type=F32)
        + jnp.einsum("rd,ed->re", d_key, proj_key, preferred_element_type=F32)
        + jnp.einsum("rd,ed->re", d_value, proj_value, preferred_element_type=F32)
    )
    d_settled = d_first_in + d_entry
    text_grad = d_settled * keep
    d_masked = jnp.zeros_like(text_grad)
    tap_sums = []
    for s in range(1, 4):
        for t in range(3):
            offset = (t - 1) * s
            d_masked = d_masked + conv_text[s - 1, t] * shifted(text_grad, -offset)
            tap_sums.append(jnp.sum(text_grad * shifted(masked, offset), axis=0))
    g_conv_text = jnp.stack(tap_sums).reshape(9, width)
    patch_grad = d_settled[TEXT : TEXT + patches].reshape(GRID, GRID, width)
    unused_out, patch_pull = jax.vjp(patch_conv, patch_rows, conv_patch)
    d_patch_rows, g_conv_patch = patch_pull(patch_grad)
    grad_tokens = d_settled + keep * d_masked + jnp.concatenate([above, d_patch_rows.reshape(patches, width), below], 0)
    grad_tokens = page_in(grad_tokens.astype(BF).reshape(n_seq, stretch, width)).astype(F32)

    a = jnp.arange(BOX)[:, None]
    c = jnp.arange(BOX)[None]
    nb = rel_order.shape[1]
    cell_hot = (jnp.clip(c - a, -SPAN, SPAN).reshape(-1, 1) + SPAN == jnp.arange(nb)).astype(F32)
    i = jnp.arange(RT)[:, None]
    j = jnp.arange(128)[None]
    band = jnp.stack([jnp.clip(d + j - i, -SPAN, SPAN) for d in order_offsets()] + [jnp.full((RT, 128), -SPAN), jnp.full((RT, 128), SPAN)])
    band_hot = (band.reshape(-1, 1) + SPAN == jnp.arange(nb)).astype(F32)
    high = lax.Precision.HIGHEST
    g_horiz = jnp.dot(hist[:, :BOX, :BOX].reshape(heads, -1), cell_hot, precision=high)
    g_vert = jnp.dot(hist[:, BOX:, BOX:].reshape(heads, -1), cell_hot, precision=high)
    g_order = jnp.dot(ords.reshape(heads, -1), band_hot, precision=high)

    def reduced_matrix(g):
        return scatter_pages(g.reshape(n_pages, g.shape[0] // n_pages, g.shape[1]))

    o_reduce = sum_seq(reduced_matrix(g_reduce)).astype(F32)
    o_expand = sum_seq(reduced_matrix(g_expand)).astype(F32)
    four = jnp.concatenate([g.reshape(n_pages, width // n_pages, width) for g in (g_output, g_query, g_key, g_value)], 1)
    o_four = sum_seq(scatter_pages(four)).astype(F32)
    rb = width // n_pages
    o_output, o_query, o_key, o_value = (o_four[k * rb : (k + 1) * rb] for k in range(4))

    small = [
        g_conv_text, g_conv_patch.reshape(9, width), g_query_bias, g_value_bias, g_output_bias,
        g_order, g_horiz, g_vert, g_norm_gain, g_norm_shift, g_expand_bias, g_reduce_bias, g_final_gain, g_final_shift,
    ]
    sizes = [x.size for x in small]
    flat = jnp.concatenate([x.reshape(-1) for x in small])
    pad = -flat.size % 1024
    flat = sum_all(jnp.pad(flat, (0, pad)).reshape(-1, 128)).reshape(-1)
    shapes = [(3, 3, width), (3, 3, width)] + [x.shape for x in small[2:]]
    outs, at = [], 0
    for size, shape in zip(sizes, shapes):
        outs.append(flat[at : at + size].reshape(shape))
        at += size
    (s_conv_text, s_conv_patch, s_query_bias, s_value_bias, s_output_bias, s_order, s_horiz, s_vert,
     s_norm_gain, s_norm_shift, s_expand_bias, s_reduce_bias, s_final_gain, s_final_shift) = outs
    return (
        mixed_out, grad_tokens, s_conv_text, s_conv_patch, o_query, s_query_bias, o_key, o_value, s_value_bias,
        o_output, s_output_bias, s_order, s_horiz, s_vert, s_norm_gain, s_norm_shift, o_expand, s_expand_bias,
        o_reduce, s_reduce_bias, s_final_gain, s_final_shift,
    )


def solution(mesh):
    placed = (
        P("pages", "seq", None),
        P("pages", "seq", None),
        P(),
        P(),
        P(),
        P(),
        P(),
        P(),
        P(),
        P(),
        P(),
        P(),
        P(),
        P(),
        P(),
        P(),
        P(),
        P(),
        P(),
        P(),
        P(),
        P(),
        P("pages"),
        P("pages", None),
        P("pages", None),
    )
    return jax.shard_map(
        per_device,
        mesh=mesh,
        in_specs=placed,
        out_specs=(
            P("pages", "seq", None),
            P("pages", "seq", None),
            P(),
            P(),
            P("pages", None),
            P(),
            P("pages", None),
            P("pages", None),
            P(),
            P("pages", None),
            P(),
            P(),
            P(),
            P(),
            P(),
            P(),
            P("pages", None),
            P(),
            P("pages", None),
            P(),
            P(),
            P(),
        ),
        check_vma=False,
    )
```

time: 1200 us -> 497 us (0.41)
  waiting for transfers between devices: 733 us -> 85 us
  matrix products: 255 us -> 90.8 us
  starting transfers between devices: 12.3 us -> 88.4 us
  Pallas kernels: 0 us -> 39 us
  between operations: 16.2 us -> 3.77 us
    reduce_scatter x8 -> x0, waiting for transfers between devices: 445 us -> none  [the longest x1 102 us: per_device(): lax.psum_scatter(d_key_part.reshape(pages_here, length, model_width), 'se...]
    psum x2 -> x0, waiting for transfers between devices: 269 us -> none  [the longest x1 141 us: per_device(): lax.psum((part_query, part_key, part_value, part_output, part_expand, par...]
    dot_general x28 -> x22, matrix products: 237 us -> 74 us  [the longest x1 21.8 us: per_device(): jnp.dot(first_low, expand_weight, preferred_element_type=F32) + expand_bias]
    ppermute x4 -> x50, waiting for transfers between devices: 0.83 us -> 85 us  [the longest x20 35.6 us: swap(): return lax.ppermute(value, axis, xor_pairs(lax.axis_size(axis), bit))]
    ppermute x4 -> x50, starting transfers between devices: 11.6 us -> 88.4 us  [the longest x12 32.5 us: page_in(): got.append(lax.ppermute(part, 'seq', [(i, (i + d) % n) for i in range(n)]))]
    pallas_call x0 -> x2, Pallas kernels: none -> 39 us  [the longest x1 21.5 us: attn_bwd(): pl.pallas_call(bwd_kernel, out_shape=(jax.ShapeDtypeStruct((L, D), BF),)...]
    reduce_sum x6 -> x4, other arithmetic: 31.4 us -> 4.62 us  [the longest x1 2.29 us: per_device(): g_reduce_bias = jnp.sum(d_reduced, axis=0, dtype=F32)]
    slice x5 -> x22, local copies, waits for them, and re-layouts: 4.65 us -> 28.9 us  [the longest x6 9.33 us: halve(): value[i:i + 1]]
  transfers between devices with their start and end apart: 16 -> 50, of which waited for: 12 -> 17; matrix products, arithmetic and copies ran while one was open for 24% -> 29% of each run, Pallas kernels for 0% -> 0%
where the time goes in v1:
time: 497 us; the launch traced here: 489 us
  local copies, waits for them, and re-layouts  104 us (21%)
  matrix products  90.8 us (18%)
  starting transfers between devices  88.4 us (18%)
  waiting for transfers between devices  85 us (17%)
  other arithmetic  77.9 us (16%)
  Pallas kernels  39 us (8%)
    ppermute x20, waiting for transfers between devices, swap(): return lax.ppermute(value, axis, xor_pairs(lax.axis_size(axis), bit))  35.6 us
    ppermute x12, starting transfers between devices, page_in(): got.append(lax.ppermute(part, 'seq', [(i, (i + d) % n) for i in range(n)]))  32.5 us
    unnamed x347, local copies, waits for them, and re-layouts  27.1 us
    ppermute x20, starting transfers between devices, swap(): return lax.ppermute(value, axis, xor_pairs(lax.axis_size(axis), bit))  24 us
    dot_general x1, matrix products, per_device(): jnp.dot(first_low, expand_weight, preferred_element_type=F32) + expand_bias  21.8 us
    pallas_call x1, Pallas kernels, attn_bwd(): pl.pallas_call(bwd_kernel, out_shape=(jax.ShapeDtypeStruct((L, D), BF),)...  21.5 us
    pallas_call x1, Pallas kernels, attn_fwd(): pl.pallas_call(fwd_kernel, out_shape=(jax.ShapeDtypeStruct((H, L, L), BF)...  17.6 us
    ppermute x9, waiting for transfers between devices, sum_seq(): lax.ppermute(part, 'seq', [(i, (i + d) % n) for i in range(n)]).astype(F32)  16.9 us
  transfers between devices with their start and end apart: 50, of which 17 were waited for; matrix products, arithmetic and copies ran while one was open for 29% of the time, Pallas kernels for 0%

profile of v1, /device:TPU:0, one launch (start us, length us, event | category | flops | bytes accessed | tf_op | source)
XLA Modules:
  0.0 488.9 jit_solution(6310467684348732174)
XLA Ops:
  11.4 3.1 collective-permute-start.6
  38.9 8.4 %collective-permute-done.7 = bf16[1,144,768]{2,1,0:T(8,128)(2,1)S(1)} collective-permute-done((bf16[1,144,768]{2,1,0:T(8,128)(2,1)S(1)}, bf16[1,144,768]{2,1,0:T(8,128)(2,1)S(1)}, u32[]{:S(2)}, u32[]{:S(2)}) %collective-permute-start.7) | collective-permute-done | bytes 221216 | tf_op jit(solution)/shard_map/ppermute | solution.py:173
  65.3 6.4 %fusion.49 = (bf16[576,768]{1,0:T(8,128)(2,1)S(1)}, f32[576,768]{1,0:T(8,128)}) fusion(f32[576]{0:T(1024)S(1)} %copy-done.97, f32[49,768]{1,0:T(8,128)S(1)} %reshape.607, f32[576]{0:T(1024)S(1)} %copy-done.112, f32[573,768]{1,0:T(8,128)} %get-tuple-element.138, f32[768]{0:T(1024)S(1)} %copy-done.110, f32[768]{0:T(1024)S(1)} %copy-done.111, ...), kind=kLoop, calls=%fused_computation.359 | loop fusion | flops 11059200 | bytes 14304000 | tf_op jit(solution)/shard_map/convert_element_type | solution.py:305
  77.1 17.6 %attn_fwd.1 = (bf16[12,576,576]{2,1,0:T(8,128)(2,1)}, bf16[576,768]{1,0:T(8,128)(2,1)}) custom-call(f32[12,2]{1,0:T(8,128)} %copy.82.edge_ref, bf16[576,768]{1,0:T(8,128)(2,1)} %fusion.13.q_ref, bf16[576,768]{1,0:T(8,128)(2,1)} %convolution_convert_fusion.7.k_ref, bf16[576,768]{1,0:T(8,128)(2,1)} %add_convert_fusion.5.v_ref, ...), custom_call_target="tpu_custom_call" | custom-call | tf_op jit(solution)/shard_map/attn_fwd/pallas_call | solution.py:85
  98.4 21.8 %multiply_convert_fusion = (bf16[576,3072]{1,0:T(8,128)(2,1)S(1)}, f32[576,3072]{1,0:T(8,128)}, f32[576,3072]{1,0:T(8,128)}) fusion(f32[3072]{0:T(1024)S(1)} %copy-done.133, bf16[768,3072]{1,0:T(8,128)(2,1)} %param.41, f32[576,768]{1,0:T(8,128)S(1)} %get-tuple-element.201, f32[768]{0:T(1024)S(1)} %copy-done.138, f32[768]{0:T(1024)S(1)} %copy-done.125, ...), kind=kOutput, calls=%fused_computation.6 | convolution fusion | flops 2836905984 | bytes 24205824 | tf_op jit(solution)/shard_map/dot_general | solution.py:314
  132.3 10.3 %convert_reduce_fusion = (f32[3072]{0:T(1024)}, bf16[576,3072]{1,0:T(8,128)(2,1)S(1)}) fusion(f32[576,3072]{1,0:T(8,128)} %get-tuple-element.83, f32[576,3072]{1,0:T(8,128)} %get-tuple-element.202, f32[3072]{0:T(1024)S(1)} %copy-done.133, bf16[576,768]{1,0:T(8,128)(2,1)S(1)} %get-tuple-element.75, bf16[3072,768]{1,0:T(8,128)(2,1)} %param.43), kind=kOutput, calls=%fused_computation.4 | convolution fusion | flops 2747986944 | bytes 23322624 | tf_op jit(solution)/shard_map/rd,fd->rf/dot_general | solution.py:324
  142.7 6.4 %multiply_reduce_fusion = (f32[768]{0:T(1024)}, f32[576]{0:T(1024)S(1)}, f32[768]{0:T(1024)}, f32[576,768]{1,0:T(8,128)S(1)}) fusion(f32[576,768]{1,0:T(8,128)S(1)} %copy-done.15, f32[576]{0:T(1024)S(1)} %fusion.39, f32[576]{0:T(1024)S(1)} %broadcast_multiply_fusion.11, f32[768]{0:T(1024)S(1)} %copy-done.125, bf16[576,3072]{1,0:T(8,128)(2,1)S(1)} %get-tuple-element.77, ...), kind=kOutput, calls=%fused_computation.51 | convolution fusion | flops 2722330624 | bytes 13584384 | tf_op jit(solution)/shard_map/rf,df->rd/dot_general | solution.py:328
  149.1 6.5 %convolution_convert_fusion.1 = bf16[768,3072]{1,0:T(8,128)(2,1)} fusion(bf16[576,3072]{1,0:T(8,128)(2,1)S(1)} %get-tuple-element.77, f32[576,768]{1,0:T(8,128)S(1)} %copy-done.15, f32[768]{0:T(1024)S(1)} %copy-done.138, f32[768]{0:T(1024)S(1)} %copy-done.125, f32[576]{0:T(1024)S(1)} %fusion.39, f32[576]{0:T(1024)S(1)} %broadcast_multiply_fusion.11), kind=kOutput, calls=%fused_computation.23 | convolution fusion | flops 2722480128 | bytes 10037760 | tf_op jit(solution)/shard_map/rd,rf->df/dot_general | solution.py:327
  162.3 21.5 %attn_bwd.1 = (bf16[576,768]{1,0:T(8,128)(2,1)}, bf16[576,768]{1,0:T(8,128)(2,1)}, bf16[576,768]{1,0:T(8,128)(2,1)}, f32[12,128,128]{2,1,0:T(8,128)}, f32[12,6,64,128]{3,2,1,0:T(8,128)}) custom-call(bf16[12,576,576]{2,1,0:T(8,128)(2,1)} %get-tuple-element.30.p_ref, bf16[576,768]{1,0:T(8,128)(2,1)} %fusion.13.q_ref, ...), custom_call_target="tpu_custom_call" | custom-call | tf_op jit(solution)/shard_map/attn_bwd/pallas_call | solution.py:149
  183.7 3.7 convolution_convert_fusion.3
  195.8 5.7 %convolution_convert_fusion = bf16[3072,768]{0,1:T(8,128)(2,1)} fusion(bf16[576,3072]{1,0:T(8,128)(2,1)S(1)} %copy-done.141, bf16[576,768]{1,0:T(8,128)(2,1)S(1)} %copy-done.68), kind=kOutput, calls=%fused_computation.22 | convolution fusion | flops 2720268288 | bytes 9142272 | tf_op jit(solution)/shard_map/rf,rd->fd/dot_general | solution.py:323
  201.6 5.0 %multiply_reduce_fusion.1 = (f32[768]{0:T(1024)}, f32[768]{0:T(1024)}, f32[768]{0:T(1024)}, f32[768]{0:T(1024)}, f32[768]{0:T(1024)}, /*index=5*/f32[768]{0:T(10...) fusion(f32[573,768]{1,0:T(8,128)S(1)} %copy-done.7, f32[576]{0:T(1024)S(1)} %fusion.38, ...), kind=kOutput, calls=%fused_computation.55 | convolution fusion | flops 688761600 | bytes 22402560 | tf_op jit(solution)/shard_map/rd,ed->re/dot_general | solution.py:345
  214.1 3.4 collective-permute-start.4
  225.2 3.9 fusion
  247.4 5.7 %pad_maximum_fusion = bf16[8,384,768]{1,2,0:T(8,128)(2,1)S(1)} fusion(bf16[8,96,768]{1,2,0:T(8,128)(2,1)} %copy.86, bf16[8,96,768]{1,2,0:T(8,128)(2,1)} %copy.85, bf16[8,96,768]{1,2,0:T(8,128)(2,1)} %copy.84, bf16[8,96,768]{1,2,0:T(8,128)(2,1)S(1)} %copy.83), kind=kLoop, calls=%fused_computation.24 | loop fusion | flops 18874368 | bytes 9437184 | tf_op jit(solution)/shard_map/concatenate | solution.py:381
  266.5 4.7 slice_bitcast_fusion.7
  282.5 3.6 broadcast_select_fusion
  287.7 4.7 fusion.10
  300.0 3.7 collective-permute-done.13
  312.6 6.0 %collective-permute-done.9 = bf16[1,144,768]{2,1,0:T(8,128)(2,1)S(1)} collective-permute-done((bf16[1,144,768]{2,1,0:T(8,128)(2,1)S(1)}, bf16[1,144,768]{2,1,0:T(8,128)(2,1)S(1)}, u32[]{:S(2)}, u32[]{:S(2)}) %collective-permute-start.9) | collective-permute-done | bytes 221216 | tf_op jit(solution)/shard_map/ppermute | solution.py:173
  318.6 10.7 %collective-permute-start.11 = (bf16[1,144,768]{2,1,0:T(8,128)(2,1)S(1)}, bf16[1,144,768]{2,1,0:T(8,128)(2,1)S(1)}, u32[]{:S(2)}, u32[]{:S(2)}) collective-permute-start(bf16[1,144,768]{2,1,0:T(8,128)(2,1)S(1)} %get-tuple-element.143), channel_id=1, source_target_pairs={{0,1},{1,2},{2,3},{3,0},{4,5},{5,6},{6,7},{7,4},{8,9},{9,10},{10,1... | collective-permute-start | bytes 663560 | tf_op jit(solution)/shard_map/ppermute | solution.py:173
  371.7 4.7 collective-permute-done.31
  379.9 9.1 %collective-permute-done.20 = bf16[2,384,384]{1,2,0:T(8,128)(2,1)S(1)} collective-permute-done((bf16[2,384,384]{1,2,0:T(8,128)(2,1)S(1)}, bf16[2,384,384]{1,2,0:T(8,128)(2,1)S(1)}, u32[]{:S(2)}, u32[]{:S(2)}) %collective-permute-start.20) | collective-permute-done | bytes 589856 | tf_op jit(solution)/shard_map/ppermute | solution.py:164
  392.7 9.0 %collective-permute-done.42 = bf16[2,384,384]{1,2,0:T(8,128)(2,1)S(1)} collective-permute-done((bf16[2,384,384]{1,2,0:T(8,128)(2,1)S(1)}, bf16[2,384,384]{1,2,0:T(8,128)(2,1)S(1)}, u32[]{:S(2)}, u32[]{:S(2)}) %collective-permute-start.42) | collective-permute-done | bytes 589856 | tf_op jit(solution)/shard_map/ppermute | solution.py:164
  427.7 5.3 %collective-permute-done.34 = bf16[24,3072]{1,0:T(8,128)(2,1)} collective-permute-done((bf16[24,3072]{1,0:T(8,128)(2,1)}, bf16[24,3072]{1,0:T(8,128)(2,1)}, u32[]{:S(2)}, u32[]{:S(2)}) %collective-permute-start.34) | collective-permute-done | bytes 147488 | tf_op jit(solution)/shard_map/ppermute | solution.py:218
  434.2 5.7 %collective-permute-start.45 = (bf16[96,768]{1,0:T(8,128)(2,1)S(1)}, bf16[96,768]{1,0:T(8,128)(2,1)S(1)}, u32[]{:S(2)}, u32[]{:S(2)}) collective-permute-start(bf16[96,768]{1,0:T(8,128)(2,1)S(1)} %get-tuple-element.159), channel_id=1, source_target_pairs={{0,2},{1,3},{2,0},{3,1},{4,6},{5,7},{6,4},{7,5},{8,10},{9,11},{10,... | collective-permute-start | bytes 442376 | tf_op jit(solution)/shard_map/ppermute | solution.py:218
  439.9 6.2 %collective-permute-start.38 = (bf16[1,24,3072]{2,1,0:T(8,128)(2,1)S(1)}, bf16[1,24,3072]{2,1,0:T(8,128)(2,1)S(1)}, u32[]{:S(2)}, u32[]{:S(2)}) collective-permute-start(bf16[1,24,3072]{2,1,0:T(8,128)(2,1)S(1)} %fusion.32), channel_id=1, source_target_pairs={{0,1},{1,2},{2,3},{3,0},{4,5},{5,6},{6,7},{7,4},{8,9},{9,10},{10,1... | collective-permute-start | bytes 442376 | tf_op jit(solution)/shard_map/ppermute | solution.py:220
  446.1 8.9 %collective-permute-done.23 = bf16[96,768]{1,0:T(8,128)(2,1)S(1)} collective-permute-done((bf16[96,768]{1,0:T(8,128)(2,1)}, bf16[96,768]{1,0:T(8,128)(2,1)S(1)}, u32[]{:S(2)}, u32[]{:S(2)}) %collective-permute-start.23) | collective-permute-done | bytes 147488 | tf_op jit(solution)/shard_map/ppermute | solution.py:218
  461.5 7.5 %collective-permute-done.36 = bf16[1,24,3072]{2,1,0:T(8,128)(2,1)S(1)} collective-permute-done((bf16[1,24,3072]{2,1,0:T(8,128)(2,1)S(1)}, bf16[1,24,3072]{2,1,0:T(8,128)(2,1)S(1)}, u32[]{:S(2)}, u32[]{:S(2)}) %collective-permute-start.36) | collective-permute-done | bytes 147488 | tf_op jit(solution)/shard_map/ppermute | solution.py:220
  469.0 5.6 %collective-permute-start.49 = (bf16[1,96,768]{2,1,0:T(8,128)(2,1)S(1)}, bf16[1,96,768]{2,1,0:T(8,128)(2,1)S(1)}, u32[]{:S(2)}, u32[]{:S(2)}) collective-permute-start(bf16[1,96,768]{2,1,0:T(8,128)(2,1)S(1)} %fusion.33), channel_id=1, source_target_pairs={{0,1},{1,2},{2,3},{3,0},{4,5},{5,6},{6,7},{7,4},{8,9},{9,10},{10,1... | collective-permute-start | bytes 442376 | tf_op jit(solution)/shard_map/ppermute | solution.py:220
  477.6 4.3 collective-permute-done.25
  483.1 4.0 collective-permute-done.47
  (634 shorter events, 252.0 us)
Async XLA Ops:
  2.9 45.5 %collective-permute-start.2 = (bf16[1,144,768]{2,1,0:T(8,128)(2,1)}, bf16[1,144,768]{2,1,0:T(8,128)(2,1)}, u32[]{:S(2)}, u32[]{:S(2)}) collective-permute-start(bf16[1,144,768]{2,1,0:T(8,128)(2,1)} %get-tuple-element.152), channel_id=1, source_target_pairs={{0,1},{1,2},{2,3},{3,0},{4,5},{5,6},{6,7},{7,4},{8,9},{9,10},{10,1... | collective-permute-start | bytes 663560 | tf_op jit(solution)/shard_map/ppermute | solution.py:173
  5.9 41.5 %collective-permute-start.1 = (bf16[1,144,768]{2,1,0:T(8,128)(2,1)}, bf16[1,144,768]{2,1,0:T(8,128)(2,1)}, u32[]{:S(2)}, u32[]{:S(2)}) collective-permute-start(bf16[1,144,768]{2,1,0:T(8,128)(2,1)} %get-tuple-element.153), channel_id=1, source_target_pairs={{0,2},{1,3},{2,0},{3,1},{4,6},{5,7},{6,4},{7,5},{8,10},{9,11},{10,... | collective-permute-start | bytes 663560 | tf_op jit(solution)/shard_map/ppermute | solution.py:173
  8.5 29.5 %collective-permute-start = (bf16[1,144,768]{2,1,0:T(8,128)(2,1)}, bf16[1,144,768]{2,1,0:T(8,128)(2,1)}, u32[]{:S(2)}, u32[]{:S(2)}) collective-permute-start(bf16[1,144,768]{2,1,0:T(8,128)(2,1)} %get-tuple-element.154), channel_id=1, source_target_pairs={{0,3},{1,0},{2,1},{3,2},{4,7},{5,4},{6,5},{7,6},{8,11},{9,8},{10,9... | collective-permute-start | bytes 663560 | tf_op jit(solution)/shard_map/ppermute | solution.py:173
  10.7 36.7 %collective-permute-start.8 = (bf16[1,144,768]{2,1,0:T(8,128)(2,1)}, bf16[1,144,768]{2,1,0:T(8,128)(2,1)S(1)}, u32[]{:S(2)}, u32[]{:S(2)}) collective-permute-start(bf16[1,144,768]{2,1,0:T(8,128)(2,1)} %get-tuple-element.146), channel_id=1, source_target_pairs={{0,1},{1,2},{2,3},{3,0},{4,5},{5,6},{6,7},{7,4},{8,9},{9,10},{10,1... | collective-permute-start | bytes 663560 | tf_op jit(solution)/shard_map/ppermute | solution.py:173
  11.4 23.1 %collective-permute-start.6 = (bf16[1,144,768]{2,1,0:T(8,128)(2,1)}, bf16[1,144,768]{2,1,0:T(8,128)(2,1)}, u32[]{:S(2)}, u32[]{:S(2)}) collective-permute-start(bf16[1,144,768]{2,1,0:T(8,128)(2,1)} %get-tuple-element.148), channel_id=1, source_target_pairs={{0,3},{1,0},{2,1},{3,2},{4,7},{5,4},{6,5},{7,6},{8,11},{9,8},{10,9... | collective-permute-start | bytes 663560 | tf_op jit(solution)/shard_map/ppermute | solution.py:173
  213.5 95.5 %collective-permute-start.5 = (bf16[1,144,768]{2,1,0:T(8,128)(2,1)}, bf16[1,144,768]{2,1,0:T(8,128)(2,1)}, u32[]{:S(2)}, u32[]{:S(2)}) collective-permute-start(bf16[1,144,768]{2,1,0:T(8,128)(2,1)} %get-tuple-element.149), channel_id=1, source_target_pairs={{0,1},{1,2},{2,3},{3,0},{4,5},{5,6},{6,7},{7,4},{8,9},{9,10},{10,1... | collective-permute-start | bytes 663560 | tf_op jit(solution)/shard_map/ppermute | solution.py:173
  214.1 92.1 %collective-permute-start.4 = (bf16[1,144,768]{2,1,0:T(8,128)(2,1)}, bf16[1,144,768]{2,1,0:T(8,128)(2,1)}, u32[]{:S(2)}, u32[]{:S(2)}) collective-permute-start(bf16[1,144,768]{2,1,0:T(8,128)(2,1)} %get-tuple-element.150), channel_id=1, source_target_pairs={{0,2},{1,3},{2,0},{3,1},{4,6},{5,7},{6,4},{7,5},{8,10},{9,11},{10,... | collective-permute-start | bytes 663560 | tf_op jit(solution)/shard_map/ppermute | solution.py:173
  217.5 87.1 %collective-permute-start.3 = (bf16[1,144,768]{2,1,0:T(8,128)(2,1)}, bf16[1,144,768]{2,1,0:T(8,128)(2,1)}, u32[]{:S(2)}, u32[]{:S(2)}) collective-permute-start(bf16[1,144,768]{2,1,0:T(8,128)(2,1)} %get-tuple-element.151), channel_id=1, source_target_pairs={{0,3},{1,0},{2,1},{3,2},{4,7},{5,4},{6,5},{7,6},{8,11},{9,8},{10,9... | collective-permute-start | bytes 663560 | tf_op jit(solution)/shard_map/ppermute | solution.py:173
  277.6 19.8 %collective-permute-start.12 = (f32[192,128]{1,0:T(8,128)}, f32[192,128]{1,0:T(8,128)}, u32[]{:S(2)}, u32[]{:S(2)}) collective-permute-start(f32[192,128]{1,0:T(8,128)} %pad_bitcast_fusion), channel_id=1, source_target_pairs={{0,4},{4,0},{8,12},{12,8},{16,20},{20,16},{24,28},{28,24},{1,5},{5... | collective-permute-start | bytes 294920 | tf_op jit(solution)/shard_map/ppermute | solution.py:164
  286.1 70.7 %collective-permute-start.28 = (bf16[4,96,3072]{2,1,0:T(8,128)(2,1)}, bf16[4,96,3072]{2,1,0:T(8,128)(2,1)}, u32[]{:S(2)}, u32[]{:S(2)}) collective-permute-start(bf16[4,96,3072]{2,1,0:T(8,128)(2,1)} %broadcast_select_fusion), channel_id=1, source_target_pairs={{0,4},{4,0},{8,12},{12,8},{16,20},{20,16},{24,28},{28,24},{1,5},{5... | collective-permute-start | bytes 7077896 | tf_op jit(solution)/shard_map/ppermute | solution.py:164
  303.7 59.7 %collective-permute-start.17 = (bf16[4,384,768]{1,2,0:T(8,128)(2,1)}, bf16[4,384,768]{1,2,0:T(8,128)(2,1)}, u32[]{:S(2)}, u32[]{:S(2)}) collective-permute-start(bf16[4,384,768]{1,2,0:T(8,128)(2,1)} %broadcast_select_fusion.2), channel_id=1, source_target_pairs={{0,4},{4,0},{8,12},{12,8},{16,20},{20,16},{24,28},{28,24},{1,5},{5... | collective-permute-start | bytes 7077896 | tf_op jit(solution)/shard_map/ppermute | solution.py:164
  304.6 63.5 %collective-permute-start.39 = (bf16[4,384,768]{1,2,0:T(8,128)(2,1)}, bf16[4,384,768]{1,2,0:T(8,128)(2,1)}, u32[]{:S(2)}, u32[]{:S(2)}) collective-permute-start(bf16[4,384,768]{1,2,0:T(8,128)(2,1)} %broadcast_select_fusion.1), channel_id=1, source_target_pairs={{0,4},{4,0},{8,12},{12,8},{16,20},{20,16},{24,28},{28,24},{1,5},{5... | collective-permute-start | bytes 7077896 | tf_op jit(solution)/shard_map/ppermute | solution.py:164
  306.1 23.2 %collective-permute-start.10 = (bf16[1,144,768]{2,1,0:T(8,128)(2,1)S(1)}, bf16[1,144,768]{2,1,0:T(8,128)(2,1)S(1)}, u32[]{:S(2)}, u32[]{:S(2)}) collective-permute-start(bf16[1,144,768]{2,1,0:T(8,128)(2,1)S(1)} %get-tuple-element.144), channel_id=1, source_target_pairs={{0,2},{1,3},{2,0},{3,1},{4,6},{5,7},{6,4},{7,5},{8,10},{9,11},{10,... | collective-permute-start | bytes 663560 | tf_op jit(solution)/shard_map/ppermute | solution.py:173
  361.9 16.3 %collective-permute-start.29 = (bf16[2,96,1536]{2,1,0:T(8,128)(2,1)S(1)}, bf16[2,96,1536]{2,1,0:T(8,128)(2,1)S(1)}, u32[]{:S(2)}, u32[]{:S(2)}) collective-permute-start(bf16[2,96,1536]{2,1,0:T(8,128)(2,1)S(1)} %broadcast_select_fusion.4), channel_id=1, source_target_pairs={{0,8},{4,12},{8,0},{12,4},{16,24},{20,28},{24,16},{28,20},{1,9},{5... | collective-permute-start | bytes 1769480 | tf_op jit(solution)/shard_map/ppermute | solution.py:164
  366.0 23.1 %collective-permute-start.20 = (bf16[2,384,384]{1,2,0:T(8,128)(2,1)S(1)}, bf16[2,384,384]{1,2,0:T(8,128)(2,1)S(1)}, u32[]{:S(2)}, u32[]{:S(2)}) collective-permute-start(bf16[2,384,384]{1,2,0:T(8,128)(2,1)S(1)} %broadcast_select_fusion.6), channel_id=1, source_target_pairs={{0,16},{4,20},{8,24},{12,28},{16,0},{20,4},{24,8},{28,12},{1,17},{... | collective-permute-start | bytes 1769480 | tf_op jit(solution)/shard_map/ppermute | solution.py:164
  366.8 24.0 %collective-permute-start.18 = (bf16[2,384,384]{1,2,0:T(8,128)(2,1)S(1)}, bf16[2,384,384]{1,2,0:T(8,128)(2,1)S(1)}, u32[]{:S(2)}, u32[]{:S(2)}) collective-permute-start(bf16[2,384,384]{1,2,0:T(8,128)(2,1)S(1)} %broadcast_select_fusion.8), channel_id=1, source_target_pairs={{0,8},{4,12},{8,0},{12,4},{16,24},{20,28},{24,16},{28,20},{1,9},{5... | collective-permute-start | bytes 1769480 | tf_op jit(solution)/shard_map/ppermute | solution.py:164
  370.6 31.1 %collective-permute-start.42 = (bf16[2,384,384]{1,2,0:T(8,128)(2,1)S(1)}, bf16[2,384,384]{1,2,0:T(8,128)(2,1)S(1)}, u32[]{:S(2)}, u32[]{:S(2)}) collective-permute-start(bf16[2,384,384]{1,2,0:T(8,128)(2,1)S(1)} %broadcast_select_fusion.5), channel_id=1, source_target_pairs={{0,16},{4,20},{8,24},{12,28},{16,0},{20,4},{24,8},{28,12},{1,17},{... | collective-permute-start | bytes 1769480 | tf_op jit(solution)/shard_map/ppermute | solution.py:164
  376.4 27.8 %collective-permute-start.40 = (bf16[2,384,384]{1,2,0:T(8,128)(2,1)S(1)}, bf16[2,384,384]{1,2,0:T(8,128)(2,1)S(1)}, u32[]{:S(2)}, u32[]{:S(2)}) collective-permute-start(bf16[2,384,384]{1,2,0:T(8,128)(2,1)S(1)} %broadcast_select_fusion.7), channel_id=1, source_target_pairs={{0,8},{4,12},{8,0},{12,4},{16,24},{20,28},{24,16},{28,20},{1,9},{5... | collective-permute-start | bytes 1769480 | tf_op jit(solution)/shard_map/ppermute | solution.py:164
  378.2 31.6 %collective-permute-start.32 = (bf16[1,96,1536]{2,1,0:T(8,128)(2,1)S(1)}, bf16[1,96,1536]{2,1,0:T(8,128)(2,1)S(1)}, u32[]{:S(2)}, u32[]{:S(2)}) collective-permute-start(bf16[1,96,1536]{2,1,0:T(8,128)(2,1)S(1)} %broadcast_select_fusion.9), channel_id=1, source_target_pairs={{0,8},{4,12},{8,0},{12,4},{16,24},{20,28},{24,16},{28,20},{1,9},{5... | collective-permute-start | bytes 884744 | tf_op jit(solution)/shard_map/ppermute | solution.py:164
  389.0 21.4 %collective-permute-start.30 = (bf16[1,96,1536]{2,1,0:T(8,128)(2,1)S(1)}, bf16[1,96,1536]{2,1,0:T(8,128)(2,1)S(1)}, u32[]{:S(2)}, u32[]{:S(2)}) collective-permute-start(bf16[1,96,1536]{2,1,0:T(8,128)(2,1)S(1)} %broadcast_select_fusion.10), channel_id=1, source_target_pairs={{0,16},{4,20},{8,24},{12,28},{16,0},{20,4},{24,8},{28,12},{1,17},{... | collective-permute-start | bytes 884744 | tf_op jit(solution)/shard_map/ppermute | solution.py:164
  390.8 23.3 %collective-permute-start.21 = (bf16[1,384,384]{1,2,0:T(8,128)(2,1)S(1)}, bf16[1,384,384]{1,2,0:T(8,128)(2,1)S(1)}, u32[]{:S(2)}, u32[]{:S(2)}) collective-permute-start(bf16[1,384,384]{1,2,0:T(8,128)(2,1)S(1)} %broadcast_select_fusion.12), channel_id=1, source_target_pairs={{0,8},{4,12},{8,0},{12,4},{16,24},{20,28},{24,16},{28,20},{1,9},{5... | collective-permute-start | bytes 884744 | tf_op jit(solution)/shard_map/ppermute | solution.py:164
  404.2 16.5 %collective-permute-start.43 = (bf16[1,384,384]{1,2,0:T(8,128)(2,1)}, bf16[1,384,384]{1,2,0:T(8,128)(2,1)}, u32[]{:S(2)}, u32[]{:S(2)}) collective-permute-start(bf16[1,384,384]{1,2,0:T(8,128)(2,1)} %broadcast_select_fusion.11), channel_id=1, source_target_pairs={{0,8},{4,12},{8,0},{12,4},{16,24},{20,28},{24,16},{28,20},{1,9},{5... | collective-permute-start | bytes 884744 | tf_op jit(solution)/shard_map/ppermute | solution.py:164
  415.8 17.3 %collective-permute-start.34 = (bf16[24,3072]{1,0:T(8,128)(2,1)}, bf16[24,3072]{1,0:T(8,128)(2,1)}, u32[]{:S(2)}, u32[]{:S(2)}) collective-permute-start(bf16[24,3072]{1,0:T(8,128)(2,1)} %get-tuple-element.162), channel_id=1, source_target_pairs={{0,2},{1,3},{2,0},{3,1},{4,6},{5,7},{6,4},{7,5},{8,10},{9,11},{10,... | collective-permute-start | bytes 442376 | tf_op jit(solution)/shard_map/ppermute | solution.py:218
  422.5 17.4 %collective-permute-start.24 = (bf16[96,768]{1,0:T(8,128)(2,1)}, bf16[96,768]{1,0:T(8,128)(2,1)}, u32[]{:S(2)}, u32[]{:S(2)}) collective-permute-start(bf16[96,768]{1,0:T(8,128)(2,1)} %get-tuple-element.164), channel_id=1, source_target_pairs={{0,3},{1,0},{2,1},{3,2},{4,7},{5,4},{6,5},{7,6},{8,11},{9,8},{10,9... | collective-permute-start | bytes 442376 | tf_op jit(solution)/shard_map/ppermute | solution.py:218
  427.1 27.9 %collective-permute-start.23 = (bf16[96,768]{1,0:T(8,128)(2,1)}, bf16[96,768]{1,0:T(8,128)(2,1)S(1)}, u32[]{:S(2)}, u32[]{:S(2)}) collective-permute-start(bf16[96,768]{1,0:T(8,128)(2,1)} %get-tuple-element.165), channel_id=1, source_target_pairs={{0,2},{1,3},{2,0},{3,1},{4,6},{5,7},{6,4},{7,5},{8,10},{9,11},{10,... | collective-permute-start | bytes 442376 | tf_op jit(solution)/shard_map/ppermute | solution.py:218
  427.2 28.9 %collective-permute-start.44 = (bf16[96,768]{1,0:T(8,128)(2,1)S(1)}, bf16[96,768]{1,0:T(8,128)(2,1)S(1)}, u32[]{:S(2)}, u32[]{:S(2)}) collective-permute-start(bf16[96,768]{1,0:T(8,128)(2,1)S(1)} %get-tuple-element.157), channel_id=1, source_target_pairs={{0,1},{1,2},{2,3},{3,0},{4,5},{5,6},{6,7},{7,4},{8,9},{9,10},{10,1... | collective-permute-start | bytes 442376 | tf_op jit(solution)/shard_map/ppermute | solution.py:218
  433.0 23.1 %collective-permute-start.46 = (bf16[96,768]{1,0:T(8,128)(2,1)S(1)}, bf16[96,768]{1,0:T(8,128)(2,1)S(1)}, u32[]{:S(2)}, u32[]{:S(2)}) collective-permute-start(bf16[96,768]{1,0:T(8,128)(2,1)S(1)} %get-tuple-element.158), channel_id=1, source_target_pairs={{0,3},{1,0},{2,1},{3,2},{4,7},{5,4},{6,5},{7,6},{8,11},{9,8},{10,9... | collective-permute-start | bytes 442376 | tf_op jit(solution)/shard_map/ppermute | solution.py:218
  434.2 27.3 %collective-permute-start.45 = (bf16[96,768]{1,0:T(8,128)(2,1)S(1)}, bf16[96,768]{1,0:T(8,128)(2,1)S(1)}, u32[]{:S(2)}, u32[]{:S(2)}) collective-permute-start(bf16[96,768]{1,0:T(8,128)(2,1)S(1)} %get-tuple-element.159), channel_id=1, source_target_pairs={{0,2},{1,3},{2,0},{3,1},{4,6},{5,7},{6,4},{7,5},{8,10},{9,11},{10,... | collective-permute-start | bytes 442376 | tf_op jit(solution)/shard_map/ppermute | solution.py:218
  439.9 34.8 %collective-permute-start.38 = (bf16[1,24,3072]{2,1,0:T(8,128)(2,1)S(1)}, bf16[1,24,3072]{2,1,0:T(8,128)(2,1)S(1)}, u32[]{:S(2)}, u32[]{:S(2)}) collective-permute-start(bf16[1,24,3072]{2,1,0:T(8,128)(2,1)S(1)} %fusion.32), channel_id=1, source_target_pairs={{0,1},{1,2},{2,3},{3,0},{4,5},{5,6},{6,7},{7,4},{8,9},{9,10},{10,1... | collective-permute-start | bytes 442376 | tf_op jit(solution)/shard_map/ppermute | solution.py:220
  456.2 25.7 %collective-permute-start.27 = (bf16[1,96,768]{2,1,0:T(8,128)(2,1)S(1)}, bf16[1,96,768]{2,1,0:T(8,128)(2,1)S(1)}, u32[]{:S(2)}, u32[]{:S(2)}) collective-permute-start(bf16[1,96,768]{2,1,0:T(8,128)(2,1)S(1)} %fusion.31), channel_id=1, source_target_pairs={{0,1},{1,2},{2,3},{3,0},{4,5},{5,6},{6,7},{7,4},{8,9},{9,10},{10,1... | collective-permute-start | bytes 442376 | tf_op jit(solution)/shard_map/ppermute | solution.py:220
  461.4 20.4 %collective-permute-start.26 = (bf16[1,96,768]{2,1,0:T(8,128)(2,1)S(1)}, bf16[1,96,768]{2,1,0:T(8,128)(2,1)S(1)}, u32[]{:S(2)}, u32[]{:S(2)}) collective-permute-start(bf16[1,96,768]{2,1,0:T(8,128)(2,1)S(1)} %fusion.31), channel_id=1, source_target_pairs={{0,2},{1,3},{2,0},{3,1},{4,6},{5,7},{6,4},{7,5},{8,10},{9,11},{10,... | collective-permute-start | bytes 442376 | tf_op jit(solution)/shard_map/ppermute | solution.py:220
  469.0 18.1 %collective-permute-start.49 = (bf16[1,96,768]{2,1,0:T(8,128)(2,1)S(1)}, bf16[1,96,768]{2,1,0:T(8,128)(2,1)S(1)}, u32[]{:S(2)}, u32[]{:S(2)}) collective-permute-start(bf16[1,96,768]{2,1,0:T(8,128)(2,1)S(1)} %fusion.33), channel_id=1, source_target_pairs={{0,1},{1,2},{2,3},{3,0},{4,5},{5,6},{6,7},{7,4},{8,9},{9,10},{10,1... | collective-permute-start | bytes 442376 | tf_op jit(solution)/shard_map/ppermute | solution.py:220
  (164 other events, 1275.7 us)

commit v2 on v1

v2 whole, which is shorter than its diff:
```python
import functools
import jax
import jax.numpy as jnp
from jax import lax
from jax.experimental import pallas as pl
from jax.experimental.pallas import tpu as pltpu
from jax.sharding import PartitionSpec as P

BF = jnp.bfloat16
F32 = jnp.float32
TEXT = 512
GRID = 7
SPAN = 16
EPS = 1e-06
SCALE = 0.125
NEG = -1e30
BOX = 64
RT = 64
EDGE = 16
CELLS = 56
OFFSETS = (-128, -64, 0, 64)
TAPS = (-3, -2, -1, 0, 1, 2, 3)
ERF_P = 0.33
ERF_Q = (0.18635791540145874, 0.1829543262720108, 0.20123349130153656, 0.047190189361572266,
         0.4085558354854584, -0.35120898485183716, 0.4602709114551544, -0.1353536993265152)


def dot(a, b):
    return jnp.dot(a, b, preferred_element_type=F32)


def dot_t(a, b):
    return lax.dot_general(a, b, (((1,), (1,)), ((), ())), preferred_element_type=F32)


def t_dot(a, b):
    return lax.dot_general(a, b, (((0,), (0,)), ((), ())), preferred_element_type=F32)


def whole(shape, buffers=1):
    return pl.BlockSpec(shape, lambda *_: (0,) * len(shape), pipeline_mode=pl.Buffered(buffers))


def whole_out(shape):
    return pl.BlockSpec(shape, lambda *_: (0,) * len(shape))


def lanes(n):
    return [slice(128 * c, 128 * (c + 1)) for c in range(n // 128)]


def row_sum(x):
    return jnp.sum(x, axis=0, keepdims=True)


def shift_rows(window, offset, rows):
    if offset == 0:
        return window[8 : 8 + rows]
    return pltpu.roll(window, (-offset) % window.shape[0], 0)[8 : 8 + rows]


def gather_page(dest, row0, place, n_seq, own, others):
    stretch = own.shape[0]
    for d, block in enumerate((own,) + tuple(others)):
        source = lax.rem(place - d + n_seq, n_seq)
        dest[pl.ds(pl.multiple_of(row0 + source * stretch, 16), stretch), :] = block[...].astype(dest.dtype)


def front_kernel(info_ref, edge_ref, *refs, n_seq):
    blocks = refs[:n_seq]
    (ct_ref, cp_ref, pm_ref, turn_ref, wq_ref, bq_ref, wk_ref, wv_ref, bv_ref, oh_ref, wt_ref, ord_ref,
     set_ref, et_ref, q_ref, k_ref, v_ref, p_ref, o_ref,
     entry_ref, xs_ref, ms_ref, ka_ref, qa_ref, s_ref) = refs[n_seq:]
    g = pl.program_id(0)
    length, width = entry_ref.shape
    place, count = info_ref[0], info_ref[1]

    @pl.when(g == 0)
    def _():
        zero = jnp.zeros((EDGE, width), F32)
        xs_ref[0:EDGE, :] = zero
        xs_ref[EDGE + length :, :] = zero
        ms_ref[0:EDGE, :] = zero
        ms_ref[EDGE + length :, :] = zero
        gather_page(xs_ref, EDGE, place, n_seq, blocks[0], blocks[1:])

        def mask_chunk(i, carry):
            r0 = pl.multiple_of(i * RT, RT)
            keep = (r0 + lax.broadcasted_iota(jnp.int32, (RT, 128), 0)) < count
            for c in lanes(width):
                ms_ref[pl.ds(r0 + EDGE, RT), c] = jnp.where(keep, xs_ref[pl.ds(r0 + EDGE, RT), c], 0.0)
            return carry

        lax.fori_loop(0, length // RT, mask_chunk, 0)

        def conv_chunk(i, carry):
            r0 = pl.multiple_of(i * RT, RT)
            keep = (r0 + lax.broadcasted_iota(jnp.int32, (RT, 128), 0)) < count
            for c in lanes(width):
                window = ms_ref[pl.ds(r0 + EDGE - 8, RT + 16), c]
                term = None
                for n, d in enumerate(TAPS):
                    part = shift_rows(window, d, RT) * ct_ref[n : n + 1, c]
                    term = part if term is None else term + part
                set_ref[pl.ds(r0, RT), c] = xs_ref[pl.ds(r0 + EDGE, RT), c] + jnp.where(keep, term, 0.0)
            return carry

        lax.fori_loop(0, length // RT, conv_chunk, 0)
        for c in lanes(width):
            window = xs_ref[EDGE + TEXT - 8 : EDGE + TEXT + CELLS + 8, c]
            term = jnp.zeros((CELLS, 128), F32)
            for n in range(9):
                off = (n // 3 - 1) * GRID + n % 3 - 1
                term = term + shift_rows(window, off, CELLS) * (cp_ref[n : n + 1, c] * pm_ref[:, n : n + 1])
            set_ref[TEXT : TEXT + CELLS, c] = set_ref[TEXT : TEXT + CELLS, c] + term
        entry_ref[...] = set_ref[...].astype(BF)
        et_ref[...] = dot_t(turn_ref[...], entry_ref[...]).astype(BF)
        for c in range(width // 256):
            s = slice(256 * c, 256 * (c + 1))
            q_ref[:, s] = (dot(entry_ref[...], wq_ref[:, s]) + bq_ref[:, s]).astype(BF) * jnp.asarray(SCALE, BF)
            k_ref[:, s] = dot(entry_ref[...], wk_ref[:, s]).astype(BF)
            v_ref[:, s] = (dot(entry_ref[...], wv_ref[:, s]) + bv_ref[:, s]).astype(BF)
        ka_ref[:, 128:256] = oh_ref[...]
        ka_ref[:, 256:384] = oh_ref[...]

    pair = pl.ds(pl.multiple_of(g * 128, 128), 128)
    ka_ref[:, 0:128] = k_ref[:, pair]
    lane = lax.broadcasted_iota(jnp.int32, (length, 128), 1)
    for e in range(2):
        mine = (lane < 64) if e == 0 else (lane >= 64)
        qa_ref[e, :, 0:128] = jnp.where(mine, q_ref[:, pair], jnp.zeros((), BF))
        qa_ref[e, :, 128:384] = dot(oh_ref[...], wt_ref[e]).astype(BF)
        s_ref[e] = dot_t(qa_ref[e], ka_ref[...])
    cols = (length + 127) // 128
    at = lax.broadcasted_iota(jnp.int32, (1, length), 1)
    ok = (at < count) | ((at >= TEXT) & (at < TEXT + GRID * GRID))
    bar = jnp.where(ok, 0.0, NEG)
    outs = []
    for e in range(2):
        left, right = edge_ref[2 * g + e, 0], edge_ref[2 * g + e, 1]
        for a in range(length // RT):
            r0 = a * RT
            parts = []
            for b in range(cols):
                w = min(128, length - 128 * b)
                d = 128 * b - r0
                t = s_ref[e, r0 : r0 + RT, 128 * b : 128 * b + w]
                m = bar[:, 128 * b : 128 * b + w]
                if d in OFFSETS:
                    t = t + ord_ref[e, OFFSETS.index(d)][:, :w] + m
                else:
                    t = t + (m + (left if d < 0 else right))
                parts.append(t)
            t = jnp.concatenate(parts, 1)
            top = jnp.max(t, axis=1, keepdims=True)
            ex = jnp.exp(t - top)
            total = jnp.sum(ex, axis=1, keepdims=True)
            p_ref[e, r0 : r0 + RT, :] = (ex * (1.0 / total)).astype(BF)
        outs.append(dot(p_ref[e], v_ref[:, pair]))
    o_ref[...] = jnp.where(lane < 64, outs[0], outs[1]).astype(BF)


def front(info, edge, blocks, ct, cp, pm, turn, wq, bq, wk, wv, bv, oh, wt, od):
    n_seq = len(blocks)
    stretch, width = blocks[0].shape
    length = n_seq * stretch
    heads = wt.shape[0]
    sds = jax.ShapeDtypeStruct
    flops = 2 * length * width * width * 3 + heads * 2 * length * length * (384 + 128)
    return pl.pallas_call(
        functools.partial(front_kernel, n_seq=n_seq),
        out_shape=(sds((length, width), F32), sds((width, length), BF)) + (sds((length, width), BF),) * 3
        + (sds((heads, length, length), BF), sds((length, width), BF)),
        grid_spec=pltpu.PrefetchScalarGridSpec(
            num_scalar_prefetch=2, grid=(heads // 2,),
            in_specs=[whole((stretch, width))] * n_seq
            + [whole(ct.shape), whole(cp.shape), whole(pm.shape), whole(turn.shape), whole(wq.shape), whole(bq.shape), whole(wk.shape),
               whole(wv.shape), whole(bv.shape), whole(oh.shape),
               pl.BlockSpec((2, 128, 256), lambda g, *_: (g, 0, 0)),
               pl.BlockSpec((2, len(OFFSETS), RT, 128), lambda g, *_: (g, 0, 0, 0))],
            out_specs=[whole_out((length, width)), whole_out((width, length))] + [whole_out((length, width))] * 3
            + [pl.BlockSpec((2, length, length), lambda g, *_: (g, 0, 0)), pl.BlockSpec((length, 128), lambda g, *_: (0, g))],
            scratch_shapes=[pltpu.VMEM((length, width), BF), pltpu.VMEM((length + 2 * EDGE, width), F32), pltpu.VMEM((length + 2 * EDGE, width), F32),
                            pltpu.VMEM((length, 384), BF), pltpu.VMEM((2, length, 384), BF), pltpu.VMEM((2, length, length), F32)],
        ),
        cost_estimate=pl.CostEstimate(flops=25_000_000_000, bytes_accessed=8 << 20, transcendentals=0),
        name="front",
    )(info, edge, *blocks, ct, cp, pm, turn, wq, bq, wk, wv, bv, oh, wt, od)


def norm_stats(u):
    mean = jnp.mean(u, axis=1, keepdims=True)
    c = u - mean
    rs = lax.rsqrt(jnp.mean(c * c, axis=1, keepdims=True) + EPS)
    return c * rs, rs


def norm_back(u, xhat, rs):
    return rs * (u - jnp.mean(u, axis=1, keepdims=True) - xhat * jnp.mean(u * xhat, axis=1, keepdims=True))


def gelu_pair(x):
    t = 1.0 / (1.0 + jnp.abs(x) * (ERF_P * 0.7071067811865476))
    bell = jnp.exp(x * x * -0.5)
    q = jnp.full_like(t, 0.5 * ERF_Q[7])
    for k in range(6, -1, -1):
        q = q * t + 0.5 * ERF_Q[k]
    tail = q * t * bell
    cdf = jnp.where(x < 0, tail, 1.0 - tail)
    return x * cdf, cdf + x * (bell * 0.3989422804014327)


def middle_kernel(info_ref, *refs, n_seq, tiles, tile, block):
    cots = refs[:n_seq]
    (att_ref, set_ref, wo_ref, bo_ref, ng_ref, ns_ref, w1_ref, b1_ref, w2_ref, b2_ref, fg_ref, fs_ref, turn_ref) = refs[n_seq : n_seq + 13]
    outs = refs[n_seq + 13 :]
    mixed = outs[:n_seq]
    (xh_ref, rs_ref, fl_ref, gp_ref, ds_ref, dr_ref, gk_ref, gs_ref, sm_ref, act_ref, fn_ref, acc_ref, cot_ref, mix_ref, e_ref, g_ref) = outs[n_seq:]
    i = pl.program_id(0)
    length, width = fl_ref.shape
    place = info_ref[0]

    @pl.when(i == 0)
    def _():
        for c in range(width // 256):
            s = slice(256 * c, 256 * (c + 1))
            acc_ref[:, s] = dot(att_ref[...], wo_ref[:, s])

        def chunk(j, carry):
            r = pl.ds(pl.multiple_of(j * RT, RT), RT)
            u = set_ref[r, :] + (acc_ref[r, :] + bo_ref[...])
            xhat, rs = norm_stats(u)
            xh_ref[r, :] = xhat
            rs_ref[r, :] = jnp.broadcast_to(rs, (RT, 128))
            fn = xhat * ng_ref[...] + ns_ref[...]
            fn_ref[r, :] = fn
            fl_ref[r, :] = fn.astype(BF)
            return carry

        lax.fori_loop(0, length // RT, chunk, 0)
        gather_page(cot_ref, 0, place, n_seq, cots[0], cots[1:])

    @pl.when(i < tiles)
    def _():
        half = tile // 3
        for n in range(3):
            e_ref[n] = dot(fl_ref[...], w1_ref[:, n * half : (n + 1) * half])
        for n in range(3):
            s = slice(n * half, (n + 1) * half)
            act, gp = gelu_pair(e_ref[n] + b1_ref[:, s])
            act_ref[i, :, s] = act.astype(BF)
            gp_ref[:, s] = gp.astype(gp_ref.dtype)
        part = dot(act_ref[i], w2_ref[...])

        @pl.when(i == 0)
        def _():
            acc_ref[...] = part

        @pl.when(i > 0)
        def _():
            acc_ref[...] += part

    @pl.when(i == tiles - 1)
    def _():
        def chunk(j, sums):
            r0 = pl.multiple_of(j * RT, RT)
            r = pl.ds(r0, RT)
            second = fn_ref[r, :] + (acc_ref[r, :] + b2_ref[...])
            xhat, rs = norm_stats(second)
            mix_ref[r, :] = (xhat * fg_ref[...] + fs_ref[...]).astype(BF)
            cot = cot_ref[r, :].astype(F32)
            back = norm_back(cot * fg_ref[...], xhat, rs)
            ds_ref[r, :] = back
            low = back.astype(BF)
            dr_ref[r, :] = low
            return (sums[0] + row_sum(cot * xhat), sums[1] + row_sum(cot), sums[2] + row_sum(low.astype(F32)))

        sums = lax.fori_loop(0, length // RT, chunk, (jnp.zeros((1, width), F32),) * 3)
        for n in range(3):
            sm_ref[n : n + 1, :] = sums[n]
        stretch = length // n_seq
        for d in range(n_seq):
            dest = lax.rem(place + d, n_seq)
            mixed[d][...] = mix_ref[pl.ds(pl.multiple_of(dest * stretch, 16), stretch), :]

    @pl.when(i >= tiles)
    def _():
        grad = t_dot(act_ref[i - tiles], dr_ref[...]).astype(BF)
        if 2 * block == tile:
            g_ref[...] = grad
            core = info_ref[2]
            gk_ref[...] = g_ref[pl.ds(pl.multiple_of(core * block, block), block), :]
            gs_ref[...] = g_ref[pl.ds(pl.multiple_of((1 - core) * block, block), block), :]
        else:
            turned = dot(turn_ref[...], grad).astype(BF)
            gk_ref[...] = turned[: tile // 2]
            gs_ref[...] = turned[tile // 2 :]


def middle(info, cots, att, settled, wo, bo, ng, ns, w1, b1, w2, b2, fg, fs, turn, block):
    tile = w1.shape[0]
    n_seq = len(cots)
    stretch, width = cots[0].shape
    length = n_seq * stretch
    ff = w1.shape[1]
    tiles = ff // tile
    sds = jax.ShapeDtypeStruct
    early = lambda i: jnp.minimum(i, tiles - 1)
    late = lambda i: jnp.maximum(i - tiles, 0)
    return pl.pallas_call(
        functools.partial(middle_kernel, n_seq=n_seq, tiles=tiles, tile=tile, block=block),
        out_shape=(sds((stretch, width), BF),) * n_seq
        + (sds((length, width), F32), sds((length, 128), F32), sds((length, width), BF), sds((length, ff), BF),
           sds((length, width), F32), sds((length, width), BF), sds((ff // 2, width), BF), sds((ff // 2, width), BF), sds((8, width), F32)),
        grid_spec=pltpu.PrefetchScalarGridSpec(
            num_scalar_prefetch=1, grid=(2 * tiles,),
            in_specs=[whole((stretch, width))] * n_seq
            + [whole(att.shape), whole(settled.shape), whole(wo.shape), whole(bo.shape), whole(ng.shape), whole(ns.shape),
               pl.BlockSpec((width, tile), lambda i, *_: (0, early(i))), pl.BlockSpec((1, tile), lambda i, *_: (0, early(i))),
               pl.BlockSpec((tile, width), lambda i, *_: (early(i), 0)), whole(b2.shape), whole(fg.shape), whole(fs.shape), whole(turn.shape)],
            out_specs=[whole_out((stretch, width))] * n_seq
            + [whole_out((length, width)), whole_out((length, 128)), whole_out((length, width)),
               pl.BlockSpec((length, tile), lambda i, *_: (0, early(i))),
               whole_out((length, width)), whole_out((length, width)),
               pl.BlockSpec((tile // 2, width), lambda i, *_: (late(i), 0)), pl.BlockSpec((tile // 2, width), lambda i, *_: (late(i), 0)),
               whole_out((8, width))],
            scratch_shapes=[pltpu.VMEM((tiles, length, tile), BF), pltpu.VMEM((length, width), F32), pltpu.VMEM((length, width), F32),
                            pltpu.VMEM((length, width), BF), pltpu.VMEM((length, width), BF), pltpu.VMEM((3, length, tile // 3), F32),
                            pltpu.VMEM((tile, width), BF)],
        ),
        cost_estimate=pl.CostEstimate(flops=35_000_000_000, bytes_accessed=8 << 20, transcendentals=0),
        name="middle",
    )(info, *cots, att, settled, wo, bo, ng, ns, w1, b1, w2, b2, fg, fs, turn)


def back_kernel(*refs, tiles, last):
    if last:
        (dr_ref, in_ref, w2_ref, gp_ref, w1_ref, fl_ref, turn_ref, xh_ref, rs_ref, ng_ref, att_ref, wo_ref) = refs[:12]
        (gk_ref, gs_ref, be_ref, df_ref, da_ref, sm_ref, flt_ref, acc_ref, db_ref) = refs[-9:]
    else:
        (dr_ref, in_ref, w2_ref, gp_ref, w1_ref, fl_ref, turn_ref) = refs[:7]
        (gk_ref, gs_ref, be_ref, acc_ref, flt_ref) = refs[-5:]
    i = pl.program_id(0)
    length, width = dr_ref.shape

    @pl.when(i == 0)
    def _():
        flt_ref[...] = dot_t(turn_ref[...], fl_ref[...]).astype(BF)
        acc_ref[...] = in_ref[...]

    @pl.when(i < tiles)
    def _():
        de = dot_t(dr_ref[...], w2_ref[...]) * gp_ref[...].astype(F32)
        de = de.astype(BF)
        be_ref[...] = row_sum(de.astype(F32))
        grad = dot(flt_ref[...], de).astype(BF)
        gk_ref[...] = grad[: width // 2]
        gs_ref[...] = grad[width // 2 :]
        acc_ref[...] += dot_t(de, w1_ref[...])

    if not last:
        return

    @pl.when(i == tiles)
    def _():
        def chunk(j, sums):
            r = pl.ds(pl.multiple_of(j * RT, RT), RT)
            first = acc_ref[r, :]
            xhat = xh_ref[r, :]
            back = norm_back(first * ng_ref[...], xhat, rs_ref[r, 0:1])
            df_ref[r, :] = back
            low = back.astype(BF)
            db_ref[r, :] = low
            return (sums[0] + row_sum(first * xhat), sums[1] + row_sum(first), sums[2] + row_sum(low.astype(F32)))

        sums = lax.fori_loop(0, length // RT, chunk, (jnp.zeros((1, width), F32),) * 3)
        for n in range(3):
            sm_ref[n : n + 1, :] = sums[n]
        da_ref[...] = dot_t(db_ref[...], wo_ref[...]).astype(BF)
        grad = dot(dot_t(turn_ref[...], att_ref[...]).astype(BF), db_ref[...]).astype(BF)
        gk_ref[...] = grad[: width // 2]
        gs_ref[...] = grad[width // 2 :]


def back(first, tiles, dr, acc, w2, gp, w1, fl, turn, filled=(), norm=None):
    length, width = dr.shape
    ff = w1.shape[1]
    last = norm is not None
    sds = jax.ShapeDtypeStruct
    at = lambda i: jnp.minimum(i, tiles - 1) + first
    grad = pl.BlockSpec((width // 2, width), lambda i: (0, i + first))
    args = [dr, acc, w2, gp, w1, fl, turn] + list(norm or ())
    out_shape = [sds((width // 2, ff + width), BF), sds((width // 2, ff + width), BF), sds((1, ff), F32), sds((length, width), F32)]
    out_specs = [grad, grad, pl.BlockSpec((1, width), lambda i: (0, at(i))), whole_out((length, width))]
    scratch = [pltpu.VMEM((width, length), BF)]
    if last:
        out_shape += [sds((length, width), BF), sds((8, width), F32)]
        out_specs += [whole_out((length, width)), whole_out((8, width))]
        scratch += [pltpu.VMEM((length, width), F32), pltpu.VMEM((length, width), BF)]
    return pl.pallas_call(
        functools.partial(back_kernel, tiles=tiles, last=last),
        out_shape=tuple(out_shape),
        grid=(tiles + last,),
        in_specs=[whole(dr.shape), whole(acc.shape), pl.BlockSpec((width, width), lambda i: (at(i), 0)),
                  pl.BlockSpec((length, width), lambda i: (0, at(i))), pl.BlockSpec((width, width), lambda i: (0, at(i)))]
        + [whole(x.shape) for x in args[5:]] + [pl.BlockSpec(memory_space=pl.ANY)] * len(filled),
        out_specs=out_specs,
        scratch_shapes=scratch,
        input_output_aliases={len(args) + n: n for n in range(len(filled))},
        cost_estimate=pl.CostEstimate(flops=12_000_000_000, bytes_accessed=8 << 20, transcendentals=0),
        name="back",
    )(*args, *filled)


def diagonals(x):
    wide = jnp.concatenate([x, jnp.zeros_like(x)], 1)
    return row_sum(pltpu.roll(wide, 0, 1, stride=1, stride_axis=0))


def hi_lo(x):
    hi = x.astype(BF)
    return jnp.concatenate([hi, (x - hi.astype(F32)).astype(BF)], 1)


def heads_kernel(*refs):
    (p_ref, q_ref, k_ref, v_ref, do_ref, o_ref, oh_ref, oht_ref, et_ref, wq_ref, wk_ref, wv_ref, in_ref) = refs[:13]
    (gk_ref, gs_ref, qb_ref, diag_ref, acc_ref, va_ref, rhs_ref, dsc_ref, dp_ref, w_ref, d_ref) = refs[-11:]
    g = pl.program_id(0)
    length = q_ref.shape[0]
    lane = lax.broadcasted_iota(jnp.int32, (length, 128), 1)

    @pl.when(g == 0)
    def _():
        va_ref[:, 128:256] = jnp.where(lane < 2, 1.0, 0.0).astype(BF)
        rhs_ref[:, 128:256] = oh_ref[...]
        acc_ref[...] = in_ref[...]

    va_ref[:, 0:128] = v_ref[...]
    rhs_ref[:, 0:128] = k_ref[...]
    cols = (length + 127) // 128
    flip = (lax.broadcasted_iota(jnp.int32, (RT, RT), 0) + lax.broadcasted_iota(jnp.int32, (RT, RT), 1) == RT - 1).astype(F32).astype(BF)
    do = do_ref[...]
    prod = do.astype(F32) * o_ref[...].astype(F32)
    res = []
    for e in range(2):
        mine = (lane < 64) if e == 0 else (lane >= 64)
        inner = -jnp.sum(jnp.where(mine, prod, 0.0), axis=1, keepdims=True)
        hi = inner.astype(BF)
        lo = inner - hi.astype(F32)
        ext = jnp.where(lane == 0, hi.astype(F32), jnp.where(lane == 1, lo, 0.0)).astype(BF)
        da = jnp.concatenate([jnp.where(mine, do, jnp.zeros((), BF)), ext], 1)
        dp_ref[e] = dot_t(da, va_ref[...])
    for e in range(2):
        sums = {}
        for a in range(length // RT):
            r0 = a * RT
            ds = p_ref[e, r0 : r0 + RT, :].astype(F32) * dp_ref[e, r0 : r0 + RT, :]
            dsc_ref[e, r0 : r0 + RT, :] = ds.astype(BF)
            for b in range(cols):
                w = min(128, length - 128 * b)
                d = 128 * b - r0
                t = ds[:, 128 * b : 128 * b + w]
                if w < 128:
                    t = jnp.concatenate([t, jnp.zeros((RT, 128 - w), F32)], 1)
                key = OFFSETS.index(d) if d in OFFSETS else (4 if d < 0 else 5)
                sums[key] = sums[key] + t if key in sums else t
        for n in range(4):
            turned = dot(flip, hi_lo(sums[n]))
            diag_ref[e, n : n + 1, :] = diagonals(turned[:, 0:128] + turned[:, 128:256])
        diag_ref[e, 4:5, 0:128] = row_sum(sums[4])
        diag_ref[e, 4:5, 128:256] = row_sum(sums[5])
        r = dot(dsc_ref[e], rhs_ref[...])
        hh = dot(oht_ref[...], hi_lo(r[:, 128:256]))
        hist = hh[:, 0:128] + hh[:, 128:256]
        half = lane[:BOX] < BOX
        diag_ref[e, 5:6, :] = diagonals(jnp.where(half, hist[:BOX], 0.0))
        diag_ref[e, 6:7, :] = diagonals(jnp.where(half, 0.0, hist[BOX:]))
        diag_ref[e, 7:8, :] = jnp.zeros((1, 256), F32)
        dk = t_dot(dsc_ref[e], q_ref[...])
        dv = t_dot(p_ref[e], do)
        res.append((r[:, 0:128], dk, dv))
    first = lane < 64
    dq = (jnp.where(first, res[0][0], res[1][0]) * SCALE).astype(BF)
    dk = jnp.where(first, res[0][1], res[1][1]).astype(BF)
    dv = jnp.where(first, res[0][2], res[1][2]).astype(BF)
    d_ref[:, 0:128] = dq
    d_ref[:, 128:256] = dk
    d_ref[:, 256:384] = dv
    qb_ref[0:1, :] = row_sum(dq.astype(F32))
    qb_ref[1:2, :] = row_sum(dv.astype(F32))
    w_ref[:, 0:128] = wq_ref[...]
    w_ref[:, 128:256] = wk_ref[...]
    w_ref[:, 256:384] = wv_ref[...]
    grad = dot(et_ref[...], d_ref[...]).astype(BF)
    gk_ref[...] = grad[: grad.shape[0] // 2]
    gs_ref[...] = grad[grad.shape[0] // 2 :]
    acc_ref[...] += dot_t(d_ref[...], w_ref[...])


def heads_back(first, count, probs, q, k, v, do, o, oh, oht, et, wq, wk, wv, acc, filled=()):
    heads = probs.shape[0]
    length, width = q.shape
    steps = count // 2
    base = first // 2
    sds = jax.ShapeDtypeStruct
    col = pl.BlockSpec((length, 128), lambda g: (0, g + base))
    wcol = pl.BlockSpec((width, 128), lambda g: (0, g + base))
    flops = 2 * length * width * 64 * count * 6 + count * 2 * length * length * (256 + 256 + 128 + 128)
    return pl.pallas_call(
        heads_kernel,
        out_shape=(sds((width // 2, 3 * width), BF), sds((width // 2, 3 * width), BF), sds((8, width), F32), sds((heads, 8, 256), F32), sds((length, width), F32)),
        grid=(steps,),
        in_specs=[pl.BlockSpec((2, length, length), lambda g: (g + base, 0, 0)), col, col, col, col, col, whole(oh.shape), whole(oht.shape),
                  whole(et.shape), wcol, wcol, wcol, whole(acc.shape)] + [pl.BlockSpec(memory_space=pl.ANY)] * len(filled),
        out_specs=[pl.BlockSpec((width // 2, 384), lambda g: (0, g + base)), pl.BlockSpec((width // 2, 384), lambda g: (0, g + base)),
                   pl.BlockSpec((8, 128), lambda g: (0, g + base)), pl.BlockSpec((2, 8, 256), lambda g: (g + base, 0, 0)), whole_out((length, width))],
        input_output_aliases={13 + n: n for n in range(len(filled))},
        scratch_shapes=[pltpu.VMEM((length, 256), BF), pltpu.VMEM((length, 256), BF), pltpu.VMEM((2, length, length), BF),
                        pltpu.VMEM((2, length, length), F32), pltpu.VMEM((width, 384), BF), pltpu.VMEM((length, 384), BF)],
        cost_estimate=pl.CostEstimate(flops=20_000_000_000, bytes_accessed=8 << 20, transcendentals=0),
        name="heads_back",
    )(probs, q, k, v, do, o, oh, oht, et, wq, wk, wv, acc, *filled)


def encode_kernel(info_ref, *refs, n_seq):
    blocks = refs[:n_seq]
    in_ref, ct_ref, cp_ref, pm_ref, sm_ref, sm2_ref, be_ref, qb_ref = refs[n_seq : n_seq + 8]
    outs = refs[n_seq + 8 :]
    grads = outs[:n_seq]
    small_ref, acc_ref, gs_ref, ms_ref, gt_ref = outs[n_seq:]
    length, width = in_ref.shape
    place, count = info_ref[0], info_ref[1]
    acc_ref[...] = in_ref[...]
    small_ref[...] = jnp.zeros_like(small_ref)
    small_ref[0:3, :] = sm_ref[0:3, :]
    small_ref[3:6, :] = sm2_ref[0:3, :]
    small_ref[6:8, :] = qb_ref[0:2, :]
    tiles = be_ref.shape[1] // width
    for t in range(tiles):
        small_ref[8 + t : 9 + t, :] = be_ref[:, t * width : (t + 1) * width]
    taps, cells = 8 + tiles, 15 + tiles
    zero = jnp.zeros((EDGE, width), F32)
    gs_ref[0:EDGE, :] = zero
    gs_ref[EDGE + length :, :] = zero
    ms_ref[0:EDGE, :] = zero
    ms_ref[EDGE + length :, :] = zero
    gather_page(ms_ref, EDGE, place, n_seq, blocks[0], blocks[1:])
    for c in lanes(width):
        tok = ms_ref[EDGE + TEXT - 8 : EDGE + TEXT + CELLS + 8, c]
        own = acc_ref[TEXT : TEXT + CELLS, c]
        window = jnp.concatenate([acc_ref[TEXT - 8 : TEXT + CELLS, c], jnp.zeros((8, 128), F32)], 0)
        term = jnp.zeros((CELLS, 128), F32)
        for n in range(9):
            off = (n // 3 - 1) * GRID + n % 3 - 1
            term = term + shift_rows(window, -off, CELLS) * (cp_ref[n : n + 1, c] * pm_ref[:, 8 - n : 9 - n])
            small_ref[cells + n : cells + n + 1, c] = row_sum(own * shift_rows(tok, off, CELLS) * pm_ref[:, n : n + 1])
        gt_ref[:, c] = term

    def split_chunk(j, carry):
        r0 = pl.multiple_of(j * RT, RT)
        keep = (r0 + lax.broadcasted_iota(jnp.int32, (RT, 128), 0)) < count
        for c in lanes(width):
            dset = acc_ref[pl.ds(r0, RT), c]
            gs_ref[pl.ds(r0 + EDGE, RT), c] = jnp.where(keep, dset, 0.0)
            ms_ref[pl.ds(r0 + EDGE, RT), c] = jnp.where(keep, ms_ref[pl.ds(r0 + EDGE, RT), c], 0.0)
        return carry

    lax.fori_loop(0, length // RT, split_chunk, 0)
    for c in lanes(width):
        acc_ref[TEXT : TEXT + CELLS, c] = acc_ref[TEXT : TEXT + CELLS, c] + gt_ref[:, c]

    def conv_chunk(j, sums):
        r0 = pl.multiple_of(j * RT, RT)
        keep = (r0 + lax.broadcasted_iota(jnp.int32, (RT, 128), 0)) < count
        out = []
        for n, c in enumerate(lanes(width)):
            window = gs_ref[pl.ds(r0 + EDGE - 8, RT + 16), c]
            own = ms_ref[pl.ds(r0 + EDGE, RT), c]
            term = None
            for m, d in enumerate(TAPS):
                moved = shift_rows(window, -d, RT)
                part = moved * ct_ref[m : m + 1, c]
                term = part if term is None else term + part
                out.append(sums[n * len(TAPS) + m] + row_sum(moved * own))
            acc_ref[pl.ds(r0, RT), c] = acc_ref[pl.ds(r0, RT), c] + jnp.where(keep, term, 0.0)
        return tuple(out)

    zeros = (jnp.zeros((1, 128), F32),) * (len(TAPS) * (width // 128))
    sums = lax.fori_loop(0, length // RT, conv_chunk, zeros)
    for n, c in enumerate(lanes(width)):
        for m in range(len(TAPS)):
            small_ref[taps + m : taps + m + 1, c] = sums[n * len(TAPS) + m]
    stretch = length // n_seq
    for d in range(n_seq):
        dest = lax.rem(place + d, n_seq)
        grads[d][...] = acc_ref[pl.ds(pl.multiple_of(dest * stretch, 16), stretch), :].astype(BF)


def encode_back(info, blocks, d_settled, ct, cp, pm, sm, sm2, be, qb):
    n_seq = len(blocks)
    stretch, width = blocks[0].shape
    length = n_seq * stretch
    sds = jax.ShapeDtypeStruct
    rows = 24 + be.shape[1] // width
    rows += 8 - rows % 8
    return pl.pallas_call(
        functools.partial(encode_kernel, n_seq=n_seq),
        out_shape=(sds((stretch, width), BF),) * n_seq + (sds((rows, width), F32),),
        grid_spec=pltpu.PrefetchScalarGridSpec(
            num_scalar_prefetch=1, grid=(1,),
            in_specs=[whole((stretch, width))] * n_seq + [whole(d_settled.shape), whole(ct.shape), whole(cp.shape), whole(pm.shape), whole(sm.shape), whole(sm2.shape), whole(be.shape), whole(qb.shape)],
            out_specs=[whole_out((stretch, width))] * n_seq + [whole_out((rows, width))],
            scratch_shapes=[pltpu.VMEM((length, width), F32), pltpu.VMEM((length + 2 * EDGE, width), F32),
                            pltpu.VMEM((length + 2 * EDGE, width), F32), pltpu.VMEM((CELLS, width), F32)],
        ),
        cost_estimate=pl.CostEstimate(flops=10_000_000_000, bytes_accessed=8 << 20, transcendentals=0),
        name="encode_back",
    )(info, *blocks, d_settled, ct, cp, pm, sm, sm2, be, qb)


def turn_matrix(width, n, core):
    block, half = width // n, width // 2
    r = jnp.arange(width, dtype=jnp.int32)
    inner = jnp.where(r < half, r, r - half)
    parity = jnp.where(r < half, core, 1 - core)
    source = (2 * (inner // block) + parity) * block + inner % block
    return (source[:, None] == r[None]).astype(BF)


def restack_kernel(info_ref, *refs):
    out_ref = refs[-1]
    n = len(refs) - 1
    for d, part in enumerate(refs[:-1]):
        out_ref[lax.rem(info_ref[0] - d + n, n)] = part[...].astype(out_ref.dtype)


def restack(info, parts, dtype):
    n = len(parts)
    rows, cols = parts[0].shape
    return pl.pallas_call(
        restack_kernel, out_shape=jax.ShapeDtypeStruct((n, rows, cols), dtype),
        in_specs=[pl.BlockSpec(memory_space=pltpu.SMEM)] + [pl.BlockSpec(memory_space=pltpu.VMEM)] * n,
        out_specs=pl.BlockSpec(memory_space=pltpu.VMEM),
        cost_estimate=pl.CostEstimate(flops=1000, bytes_accessed=1000, transcendentals=0),
        name="restack",
    )(info, *parts)


def one_hot_rows(ids, size):
    return (ids.reshape(1, -1) == jnp.arange(size, dtype=jnp.int32)[:, None]).astype(F32)


def tables(rel_order, rel_horiz, rel_vert):
    heads, nb = rel_order.shape
    high = lax.Precision.HIGHEST
    a = jnp.arange(BOX, dtype=jnp.int32)
    cell = one_hot_rows(jnp.clip(a[None, :] - a[:, None], -SPAN, SPAN) + SPAN, nb)

    def split(table):
        x = jnp.dot(table, cell, precision=high).reshape(heads, BOX, BOX)
        top = lax.reduce_precision(x, 8, 7)
        return top, x - top

    (hh, hl), (vh, vl) = split(rel_horiz), split(rel_vert)
    zero = jnp.zeros_like(hh)
    wt = jnp.concatenate([jnp.concatenate([hh, zero, hl, zero], 2), jnp.concatenate([zero, vh, zero, vl], 2)], 1).astype(BF)
    i = jnp.arange(RT, dtype=jnp.int32)[:, None]
    j = jnp.arange(128, dtype=jnp.int32)[None]
    band = jnp.stack([jnp.clip(d + j - i, -SPAN, SPAN) + SPAN for d in OFFSETS])
    od = jnp.dot(rel_order, one_hot_rows(band, nb), precision=high).reshape(heads, len(OFFSETS), RT, 128)
    edge = jnp.stack([rel_order[:, 0], rel_order[:, -1]], 1)
    return wt, od, edge


def bias_grads(diag, nb):
    heads = diag.shape[0]
    high = lax.Precision.HIGHEST
    at = jnp.arange(256, dtype=jnp.int32)
    step = at - (RT - 1)
    order_bins = jnp.stack([jnp.clip(d + step, -SPAN, SPAN) for d in OFFSETS] + [jnp.where(at < 128, -SPAN, SPAN)]) + SPAN
    order = jnp.dot(diag[:, :5].reshape(heads, -1), one_hot_rows(order_bins, nb).T, precision=high)
    flat = jnp.clip(step, -SPAN, SPAN) + SPAN
    horiz = jnp.dot(diag[:, 5], one_hot_rows(flat, nb).T, precision=high)
    low = jnp.clip(step - BOX, -SPAN, SPAN) + SPAN
    vert = jnp.dot(diag[:, 6], one_hot_rows(low, nb).T, precision=high)
    return order, horiz, vert


def patch_masks():
    g = jnp.arange(CELLS, dtype=jnp.int32)
    i, j = g // GRID, g % GRID
    cols = []
    for n in range(9):
        a, b = i + n // 3 - 1, j + n % 3 - 1
        cols.append((g < GRID * GRID) & (a >= 0) & (a < GRID) & (b >= 0) & (b < GRID))
    return jnp.pad(jnp.stack(cols, 1).astype(F32), ((0, 0), (0, 128 - 9)))


def text_taps(conv_text):
    rows = []
    for d in TAPS:
        if d == 0:
            rows.append(conv_text[0, 1] + conv_text[1, 1] + conv_text[2, 1])
        else:
            rows.append(conv_text[abs(d) - 1, 2 if d > 0 else 0])
    rows.append(jnp.zeros_like(rows[0]))
    return jnp.stack(rows)


def text_tap_grads(rows):
    return jnp.stack([jnp.stack([rows[3 - s], rows[3], rows[3 + s]]) for s in (1, 2, 3)])


def xor_pairs(n, bit):
    return [(i, i ^ bit) for i in range(n)]


def swap(value, axis, bit):
    return lax.ppermute(value, axis, xor_pairs(lax.axis_size(axis), bit))


def spread(blocks, after=None):
    n = lax.axis_size("seq")
    out = [blocks[0]]
    for d in range(1, n):
        out.append(lax.ppermute(blocks[d], "seq", [(i, (i + d) % n) for i in range(n)]))
    return out


def rotated(pages):
    n = lax.axis_size("seq")
    place = lax.axis_index("seq")
    return [lax.dynamic_index_in_dim(pages, lax.rem(place + d, n), 0, keepdims=False) for d in range(n)]


def total(terms):
    out = terms[0].astype(F32)
    for t in terms[1:]:
        out = out + t.astype(F32)
    return out.astype(BF)


class Reduction:
    def __init__(self, keep, send):
        n = lax.axis_size("pages")
        self.bits = [1 << b for b in range(n.bit_length() - 1)][:0:-1]
        self.shape = [2] * len(self.bits) + [keep.shape[0] * 2 // n]
        cols = keep.shape[1]
        self.cols = cols // 2
        self.orders = (self.bits[::-1], list(self.bits))
        self.at = 0
        self.send = send
        self.terms = [(tuple(self.bits), keep.reshape(self.shape + [cols]))]
        self.own = ([], [])
        self.fresh = []

    def pick(self, term, side, closed, sent=None):
        bits, value = term
        starts = [0] * value.ndim
        sizes = list(value.shape)
        for axis, bit in enumerate(bits):
            if bit in closed:
                mine = jnp.minimum(lax.axis_index("pages") & bit, 1)
                starts[axis] = 1 - mine if bit == sent else mine
                sizes[axis] = 1
        if value.shape[-1] > self.cols:
            starts[-1] = side * self.cols
            sizes[-1] = self.cols
        out = lax.dynamic_slice(value, starts, sizes)
        return out.reshape([n for axis, n in enumerate(sizes) if axis >= len(bits) or bits[axis] not in closed])

    def parts(self, side, closed, sent=None):
        return total([self.pick(t, side, closed, sent) for t in self.terms + self.own[side]])

    def step(self):
        at, last = self.at, len(self.bits)
        self.at += 1
        n = lax.axis_size("seq")
        ring = lambda d: [(i, (i + d) % n) for i in range(n)]
        place = lax.axis_index("seq")
        if at == 0:
            got = swap(self.send, "pages", 1)
            self.fresh = [got]
        elif at <= last:
            self.settle()
            self.fresh = []
            for side in range(2):
                closed = self.orders[side][:at]
                send = self.parts(side, closed, closed[-1])
                self.fresh.append(swap(send, "pages", closed[-1]))
        elif at == last + 1:
            self.settle()
            value = jnp.concatenate([self.parts(side, self.bits) for side in range(2)], 1)
            rows, cols = value.shape
            quarters = value.reshape(n, rows // n, cols)
            piece = lambda d: lax.dynamic_index_in_dim(quarters, lax.rem(place + d, n), 0, keepdims=False)
            self.own = [(), piece(0)]
            self.fresh = [lax.ppermute(piece(d), "seq", ring(d)) for d in range(1, n)]
        else:
            self.own = total([self.own[1]] + self.fresh)
            self.fresh = [lax.ppermute(self.own, "seq", ring(d)) for d in range(1, n)]

    def settle(self):
        at, last = self.at - 1, len(self.bits)
        if at == 1:
            self.terms.append((tuple(self.bits), self.fresh[0].reshape(self.terms[0][1].shape)))
        elif at > 1:
            for side in range(2):
                closed = self.orders[side][: at - 1]
                self.own[side].append((tuple(b for b in self.bits if b not in closed), self.fresh[side]))

    def over(self):
        return self.at == len(self.bits) + 3

    def result(self, info):
        out = restack(info, [self.own] + self.fresh, F32)
        return out.reshape(-1, out.shape[-1])


def tie(value, *reductions):
    value, fresh, held = lax.optimization_barrier(
        (value, tuple(r.fresh for r in reductions), tuple(r.send for r in reductions)))
    for r, f, h in zip(reductions, fresh, held):
        r.fresh, r.send = f, h
    return value


def per_device(
    tokens, cotangent, conv_text, conv_patch, proj_query, bias_query, proj_key, proj_value, bias_value,
    proj_output, bias_output, rel_order, rel_horiz, rel_vert, norm_gain, norm_shift, expand_weight,
    expand_bias, reduce_weight, reduce_bias, final_gain, final_shift, text_count, box_left, box_top,
):
    pages_here, stretch, width = tokens.shape
    n_seq = lax.axis_size("seq")
    n_pages = lax.axis_size("pages")
    assert pages_here == n_seq and n_pages & (n_pages - 1) == 0
    place = lax.axis_index("seq")
    heads, nb = rel_order.shape
    ff = expand_weight.shape[1]
    pick = lambda a: lax.dynamic_index_in_dim(a, place, 0, keepdims=False)
    count, left, top = pick(text_count), pick(box_left), pick(box_top)
    blocks = spread(rotated(tokens))
    core = lax.axis_index("pages") & 1
    info = jnp.stack([place, count, core]).astype(jnp.int32)
    turn = turn_matrix(width, n_pages, core)
    cells = jnp.arange(BOX, dtype=jnp.int32)
    oh = jnp.concatenate([left[:, None] == cells[None], top[:, None] == cells[None]], 1).astype(BF)
    oht = jnp.concatenate([left[None] == cells[::-1, None], top[None] == cells[::-1, None]], 0).astype(BF)
    wt, od, edge = tables(rel_order, rel_horiz, rel_vert)
    pm, ct = patch_masks(), text_taps(conv_text)
    cp = jnp.pad(conv_patch.reshape(9, width), ((0, 7), (0, 0)))
    row = lambda x: x[None]

    cot_out, blocks = lax.optimization_barrier((rotated(cotangent), blocks))
    cots = spread(cot_out)
    settled, et, q, k, v, probs, att = front(
        info, edge, blocks, ct, cp, pm, turn, proj_query, row(bias_query), proj_key, proj_value, row(bias_value), oh, wt, od)
    *mixed, xh, rs, fl, gp, ds, dr, grk, grs, sm = middle(
        info, cots, att, settled, proj_output, row(bias_output), row(norm_gain), row(norm_shift), expand_weight,
        row(expand_bias), reduce_weight, row(reduce_bias), row(final_gain), row(final_shift), turn, ff // n_pages)
    c_reduce = Reduction(grk, grs)
    c_reduce.step()
    mixed = spread(mixed)
    done = back(0, 2, dr, ds, reduce_weight, gp, expand_weight, fl, turn)
    done = tie(done, c_reduce)
    c_reduce.step()
    done = back(2, ff // width - 2, dr, done[3], reduce_weight, gp, expand_weight, fl, turn, done[:3],
                (xh, rs, row(norm_gain), att, proj_output))
    done, mixed = tie((done, mixed), c_reduce)
    gek, ges, be, df, da, sm2 = done
    c_expand = Reduction(gek, ges)
    heads_of = lambda first, count, da, acc, filled=(): heads_back(
        first, count, probs, q, k, v, da, att, oh, oht, et, proj_query, proj_key, proj_value, acc, filled)
    half = heads // 2
    c_reduce.step()
    c_expand.step()
    done = heads_of(0, half, da, df)
    done, da = tie((done, da), c_reduce, c_expand)
    c_reduce.step()
    c_expand.step()
    done = heads_of(half, half, da, done[4], done[:4])
    gqk, gqs, qb, diag, acc = tie(done, c_reduce, c_expand)
    c_qkv = Reduction(gqk, gqs)
    c_reduce.step()
    c_expand.step()
    c_qkv.step()
    *gts, small = encode_back(info, blocks, acc, ct, cp, pm, sm, sm2, be, qb)
    rounds = [("pages", 1 << b) for b in range(n_pages.bit_length() - 1)] + [("seq", 1 << b) for b in range(n_seq.bit_length() - 1)]
    hop = lambda d: lax.ppermute(gts[d], "seq", [(i, (i + d) % n_seq) for i in range(n_seq)])
    work = [c_reduce, c_expand, c_qkv]
    bias = jnp.concatenate(bias_grads(diag, nb), 1)
    bias = jnp.pad(bias, ((0, 0), (0, 128 - 3 * nb))).reshape(-1, width)
    phase = 0
    while rounds or not c_qkv.over():
        gts, small, bias = tie((gts, small, bias), *work)
        if phase == 0:
            small = lax.dynamic_update_slice(small, bias, (24 + ff // width, 0))
        for r in work:
            if not r.over():
                r.step()
        for d in {1: (1,), 2: (3,), 3: (2,)}.get(phase, ()):
            gts = [hop(d) if e == d else part for e, part in enumerate(gts)]
        for axis, bit in rounds[: 1 if phase < 3 else 2]:
            small = small + swap(small, axis, bit)
        rounds = rounds[1 if phase < 3 else 2 :]
        phase += 1
    o_reduce, o_expand, o_qkv = (r.result(info) for r in work)
    mixed_out = restack(info, mixed, BF)
    grad_tokens = restack(info, gts, F32)
    g3 = o_qkv.reshape(width // n_pages, heads // 2, 3, 128)
    o_query, o_key, o_value = (g3[:, :, n].reshape(width // n_pages, width) for n in range(3))
    bias = small[24 + ff // width : 24 + ff // width + heads * 128 // width].reshape(heads, 128)

    at = 0

    def take(n):
        nonlocal at
        at += n
        return small[at - n : at]

    sm, sm2, qb, be, gct, gcp = take(3), take(3), take(2), take(ff // width), take(7), take(9)
    return (
        mixed_out, grad_tokens, text_tap_grads(gct), gcp.reshape(3, 3, width), o_query, qb[0], o_key, o_value, qb[1],
        o_expand[:, ff:], sm2[2], bias[:, :nb], bias[:, nb : 2 * nb], bias[:, 2 * nb : 3 * nb], sm2[0], sm2[1],
        o_expand[:, :ff], be.reshape(ff), o_reduce, sm[2], sm[0], sm[1],
    )


def solution(mesh):
    placed = (
        P("pages", "seq", None),
        P("pages", "seq", None),
        P(),
        P(),
        P(),
        P(),
        P(),
        P(),
        P(),
        P(),
        P(),
        P(),
        P(),
        P(),
        P(),
        P(),
        P(),
        P(),
        P(),
        P(),
        P(),
        P(),
        P("pages"),
        P("pages", None),
        P("pages", None),
    )
    return jax.shard_map(
        per_device,
        mesh=mesh,
        in_specs=placed,
        out_specs=(
            P("pages", "seq", None),
            P("pages", "seq", None),
            P(),
            P(),
            P("pages", None),
            P(),
            P("pages", None),
            P("pages", None),
            P(),
            P("pages", None),
            P(),
            P(),
            P(),
            P(),
            P(),
            P(),
            P("pages", None),
            P(),
            P("pages", None),
            P(),
            P(),
            P(),
        ),
        check_vma=False,
    )
```

time: 497 us -> 329 us (0.66)
  Pallas kernels: 39 us -> 144 us
  matrix products: 90.8 us -> 3.04 us
  local copies, waits for them, and re-layouts: 104 us -> 32.7 us
  waiting for transfers between devices: 85 us -> 37.2 us
  other arithmetic: 77.9 us -> 35.1 us
  starting transfers between devices: 88.4 us -> 69.5 us
    pallas_call x2 -> x12, Pallas kernels: 39 us -> 144 us  [the longest x2 37.1 us: heads_back(): pl.pallas_call(heads_kernel, out_shape=(sds((width // 2, 3 * width), BF),...]
    dot_general x24 -> x6, matrix products: 90.8 us -> 3.04 us  [the longest x1 1.99 us: tables(): jnp.dot(rel_order, one_hot_rows(band, nb), precision=high)]
    ppermute x20, waiting for transfers between devices: 35.6 us -> 4.98 us  [swap(): return lax.ppermute(value, axis, xor_pairs(lax.axis_size(axis), bit))]
    reshape x31 -> x7, local copies, waits for them, and re-layouts: 27.2 us -> 1.58 us  [the longest x1 0.63 us: per_device(): gcp.reshape(3, 3, width)]
    slice x23 -> x10, local copies, waits for them, and re-layouts: 29.6 us -> 6.67 us  [the longest x1 2.32 us: per_device(): g3[:, :, n].reshape(width // n_pages, width)]
    unnamed x347 -> x99, local copies, waits for them, and re-layouts: 27.1 us -> 8.85 us
    ppermute x30, waiting for transfers between devices: 49.4 us -> 32.3 us  [the longest x9 17.7 us: step(): self.fresh = [lax.ppermute(self.own, 'seq', ring(d)) for d in range(1, n)]]
    ppermute x30, starting transfers between devices: 64.4 us -> 49.9 us  [the longest x9 16.6 us: spread(): lax.ppermute(blocks[d], 'seq', [(i, (i + d) % n) for i in range(n)])]
  transfers between devices with their start and end apart: 50 -> 50, of which waited for: 17 -> 9; matrix products, arithmetic and copies ran while one was open for 29% -> 17% of each run, Pallas kernels for 0% -> 34%
where the time goes in v2:
time: 329 us; the launch traced here: 323 us
  Pallas kernels  144 us (44%)
  starting transfers between devices  69.5 us (21%)
  waiting for transfers between devices  37.2 us (11%)
  other arithmetic  35.1 us (11%)
  local copies, waits for them, and re-layouts  32.7 us (10%)
    pallas_call x2, Pallas kernels, heads_back(): pl.pallas_call(heads_kernel, out_shape=(sds((width // 2, 3 * width), BF),...  37.1 us
    pallas_call x1, Pallas kernels, middle(): pl.pallas_call(functools.partial(middle_kernel, n_seq=n_seq, tiles=tiles,...  32.5 us
    pallas_call x2, Pallas kernels, back(): pl.pallas_call(functools.partial(back_kernel, tiles=tiles, last=last), ou...  29.2 us
    pallas_call x1, Pallas kernels, front(): pl.pallas_call(functools.partial(front_kernel, n_seq=n_seq), out_shape=(s...  25.6 us
    convert_element_type x15, other arithmetic, total(): return out.astype(BF)  23.2 us
    ppermute x20, starting transfers between devices, swap(): return lax.ppermute(value, axis, xor_pairs(lax.axis_size(axis), bit))  19.5 us
    ppermute x9, waiting for transfers between devices, step(): self.fresh = [lax.ppermute(self.own, 'seq', ring(d)) for d in range(1, n)]  17.7 us
    ppermute x9, starting transfers between devices, spread(): lax.ppermute(blocks[d], 'seq', [(i, (i + d) % n) for i in range(n)])  16.6 us
  transfers between devices with their start and end apart: 50, of which 9 were waited for; matrix products, arithmetic and copies ran while one was open for 17% of the time, Pallas kernels for 34%

profile of v2, /device:TPU:0, one launch (start us, length us, event | category | flops | bytes accessed | tf_op | source)
XLA Modules:
  0.0 323.4 jit_solution(16485059433752188565)
XLA Ops:
  2.9 3.0 collective-permute-start
  5.9 2.6 collective-permute-start.1
  31.1 3.1 collective-permute-start.5
  34.2 25.6 %front.1 = (f32[576,768]{1,0:T(8,128)}, bf16[768,576]{1,0:T(8,128)(2,1)}, bf16[576,768]{1,0:T(8,128)(2,1)}, bf16[576,768]{1,0:T(8,128)(2,1)}, bf16[576,768]{1,0:...) custom-call(s32[3]{0:T(128)} %pad_add_fusion.1.info_ref, f32[12,2]{1,0:T(8,128)} %copy.69.edge_ref, ...), custom_call_target="tpu_custom_call" | custom-call | flops 24999999488 | bytes 8388608 | tf_op jit(solution)/shard_map/front/pallas_call | solution.py:170
  60.7 32.5 %middle.1 = (bf16[144,768]{1,0:T(8,128)(2,1)}, bf16[144,768]{1,0:T(8,128)(2,1)}, bf16[144,768]{1,0:T(8,128)(2,1)}, bf16[144,768]{1,0:T(8,128)(2,1)}, f32[576,768...) custom-call(s32[3]{0:T(128)} %pad_add_fusion.1.info_ref, ...), custom_call_target="tpu_custom_call" | custom-call | flops 35000000512 | bytes 8388608 | tf_op jit(solution)/shard_map/middle/pallas_call | solution.py:310
  96.0 3.4 %collective-permute-start.9 = (bf16[144,768]{1,0:T(8,128)(2,1)}, bf16[144,768]{1,0:T(8,128)(2,1)}, u32[]{:S(2)}, u32[]{:S(2)}) collective-permute-start(bf16[144,768]{1,0:T(8,128)(2,1)} %get-tuple-element.197), channel_id=1, source_target_pairs={{0,3},{1,0},{2,1},{3,2},{4,7},{5,4},{6,5},{7,6},{8,11},{9,8},{10,9... | collective-permute-start | bytes 663560 | tf_op jit(solution)/shard_map/ppermute | solution.py:726
  99.4 11.5 %back.2 = (bf16[384,3840]{1,0:T(8,128)(2,1)}, bf16[384,3840]{1,0:T(8,128)(2,1)}, f32[1,3072]{1,0:T(1,128)}, f32[576,768]{1,0:T(8,128)}) custom-call(bf16[576,768]{1,0:T(8,128)(2,1)} %get-tuple-element.173.refs_0_, f32[576,768]{1,0:T(8,128)} %get-tuple-element.174.refs_1_, bf16[3072,768]{1,0:T(8,128)(2,1)} %refs_2_.3, ...), custom_call_target="tpu_custom_call" | custom-call | flops 12000000000 | bytes 8388608 | tf_op jit(solution)/shard_map/back/pallas_call | solution.py:400
  117.3 17.7 %back.3 = (bf16[384,3840]{1,0:T(8,128)(2,1)}, bf16[384,3840]{1,0:T(8,128)(2,1)}, f32[1,3072]{1,0:T(1,128)}, f32[576,768]{1,0:T(8,128)}, bf16[576,768]{1,0:T(8,128)(2,1)}, /*index=5*/f32[8,768]{1,0:T(8,128)}) custom-call(bf16[576,768]{1,0:T(8,128)(2,1)} %get-tuple-element.173.refs_0_, ...), custom_call_target="tpu_custom_call", output_to_operand_aliasing={{0}: (12, {}), {1}: (13, {}), {2}: (14, {})} | custom-call | flops 12000000000 | bytes 8388608 | tf_op jit(solution)/shard_map/back/pallas_call | solution.py:400
  142.3 2.4 fusion.17
  145.7 18.7 %heads_back.2 = (bf16[384,2304]{1,0:T(8,128)(2,1)}, bf16[384,2304]{1,0:T(8,128)(2,1)}, f32[8,768]{1,0:T(8,128)}, f32[12,8,256]{2,1,0:T(8,128)}, f32[576,768]{1,0:T(8,128)}) custom-call(bf16[12,576,576]{2,1,0:T(8,128)(2,1)} %get-tuple-element.204.refs_0_, bf16[576,768]{1,0:T(8,128)(2,1)} %get-tuple-element.205.refs_1_, ...), custom_call_target="tpu_custom_call" | custom-call | flops 20000000000 | bytes 8388608 | tf_op jit(solution)/shard_map/heads_back/pallas_call | solution.py:509
  172.4 2.9 collective-permute-start.17
  178.3 18.4 %heads_back.3 = (bf16[384,2304]{1,0:T(8,128)(2,1)}, bf16[384,2304]{1,0:T(8,128)(2,1)}, f32[8,768]{1,0:T(8,128)}, f32[12,8,256]{2,1,0:T(8,128)}, f32[576,768]{1,0:T(8,128)}) custom-call(bf16[12,576,576]{2,1,0:T(8,128)(2,1)} %get-tuple-element.204.refs_0_, ...), custom_call_target="tpu_custom_call", output_to_operand_aliasing={{0}: (13, {}), {1}: (14, {}), {2}: (15, {}), {3}: (16, {})} | custom-call | flops 20000000000 | bytes 8388608 | tf_op jit(solution)/shard_map/heads_back/pallas_call | solution.py:509
  201.5 2.4 fusion.9
  206.2 7.9 %encode_back.1 = (bf16[144,768]{1,0:T(8,128)(2,1)}, bf16[144,768]{1,0:T(8,128)(2,1)}, bf16[144,768]{1,0:T(8,128)(2,1)}, bf16[144,768]{1,0:T(8,128)(2,1)}, f32[32,768]{1,0:T(8,128)}) custom-call(s32[3]{0:T(128)} %pad_add_fusion.1.info_ref, bf16[144,768]{1,0:T(8,128)(2,1)} %get-tuple-element.167.refs_0_, bf16[144,768]{1,0:T(8,128)(2,1)} %copy-done.35, ...), custom_call_target="tpu_custom_call" | custom-call | flops 10000000000 | bytes 8388608 | tf_op jit(solution)/shard_map/encode_back/pallas_call | solution.py:606
  214.2 3.2 collective-permute-start.22
  217.7 4.0 %collective-permute-done.22.refs_3_ = bf16[96,768]{1,0:T(8,128)(2,1)} collective-permute-done((bf16[96,768]{1,0:T(8,128)(2,1)}, bf16[96,768]{1,0:T(8,128)(2,1)}, u32[]{:S(2)}, u32[]{:S(2)}) %collective-permute-start.22) | collective-permute-done | bytes 147488 | tf_op jit(solution)/shard_map/ppermute | solution.py:801
  231.3 2.9 collective-permute-start.28
  234.3 5.0 %collective-permute-done.27 = bf16[24,3840]{1,0:T(8,128)(2,1)S(1)} collective-permute-done((bf16[24,3840]{1,0:T(8,128)(2,1)S(1)}, bf16[24,3840]{1,0:T(8,128)(2,1)S(1)}, u32[]{:S(2)}, u32[]{:S(2)}) %collective-permute-start.27) | collective-permute-done | bytes 184352 | tf_op jit(solution)/shard_map/ppermute | solution.py:798
  239.2 7.1 %collective-permute-done.28 = bf16[24,3840]{1,0:T(8,128)(2,1)S(1)} collective-permute-done((bf16[24,3840]{1,0:T(8,128)(2,1)S(1)}, bf16[24,3840]{1,0:T(8,128)(2,1)S(1)}, u32[]{:S(2)}, u32[]{:S(2)}) %collective-permute-start.28) | collective-permute-done | bytes 184352 | tf_op jit(solution)/shard_map/ppermute | solution.py:798
  246.4 4.5 %collective-permute-start.32 = (bf16[144,768]{1,0:T(8,128)(2,1)S(1)}, bf16[144,768]{1,0:T(8,128)(2,1)S(1)}, u32[]{:S(2)}, u32[]{:S(2)}) collective-permute-start(bf16[144,768]{1,0:T(8,128)(2,1)S(1)} %copy-done.40), channel_id=1, source_target_pairs={{0,1},{1,2},{2,3},{3,0},{4,5},{5,6},{6,7},{7,4},{8,9},{9,10},{10,1... | collective-permute-start | bytes 663560 | tf_op jit(solution)/shard_map/ppermute | solution.py:889
  256.2 4.6 %collective-permute-done.34.refs_1_ = bf16[24,3840]{1,0:T(8,128)(2,1)S(1)} collective-permute-done((bf16[24,3840]{1,0:T(8,128)(2,1)S(1)}, bf16[24,3840]{1,0:T(8,128)(2,1)S(1)}, u32[]{:S(2)}, u32[]{:S(2)}) %collective-permute-start.34) | collective-permute-done | bytes 184352 | tf_op jit(solution)/shard_map/ppermute | solution.py:801
  260.9 6.5 %collective-permute-done.35.refs_2_ = bf16[24,3840]{1,0:T(8,128)(2,1)S(1)} collective-permute-done((bf16[24,3840]{1,0:T(8,128)(2,1)S(1)}, bf16[24,3840]{1,0:T(8,128)(2,1)S(1)}, u32[]{:S(2)}, u32[]{:S(2)}) %collective-permute-start.35) | collective-permute-done | bytes 184352 | tf_op jit(solution)/shard_map/ppermute | solution.py:801
  267.5 2.5 collective-permute-done.36.refs_3_
  270.0 4.7 %collective-permute-start.39 = (bf16[144,768]{1,0:T(8,128)(2,1)S(1)}, bf16[144,768]{1,0:T(8,128)(2,1)S(1)}, u32[]{:S(2)}, u32[]{:S(2)}) collective-permute-start(bf16[144,768]{1,0:T(8,128)(2,1)S(1)} %copy-done.39), channel_id=1, source_target_pairs={{0,3},{1,0},{2,1},{3,2},{4,7},{5,4},{6,5},{7,6},{8,11},{9,8},{10,9... | collective-permute-start | bytes 663560 | tf_op jit(solution)/shard_map/ppermute | solution.py:889
  276.9 3.1 collective-permute-start.43
  280.5 4.1 %collective-permute-done.40 = f32[32,768]{1,0:T(8,128)S(1)} collective-permute-done((f32[32,768]{1,0:T(8,128)S(1)}, f32[32,768]{1,0:T(8,128)S(1)}, u32[]{:S(2)}, u32[]{:S(2)}) %collective-permute-start.40) | collective-permute-done | bytes 98336 | tf_op jit(solution)/shard_map/ppermute | solution.py:719
  284.7 2.4 collective-permute-done.42
  287.2 2.5 collective-permute-start.47
  289.7 3.4 %collective-permute-start.48 = (bf16[24,2304]{1,0:T(8,128)(2,1)S(1)}, bf16[24,2304]{1,0:T(8,128)(2,1)S(1)}, u32[]{:S(2)}, u32[]{:S(2)}) collective-permute-start(bf16[24,2304]{1,0:T(8,128)(2,1)S(1)} %fusion.39.refs_0_), channel_id=1, source_target_pairs={{0,2},{1,3},{2,0},{3,1},{4,6},{5,7},{6,4},{7,5},{8,10},{9,11},{10,... | collective-permute-start | bytes 331784 | tf_op jit(solution)/shard_map/ppermute | solution.py:801
  297.4 2.4 restack.8
  304.0 3.0 collective-permute-start.46
  320.6 2.6 restack.6
  (289 shorter events, 100.7 us)
Async XLA Ops:
  2.9 27.2 %collective-permute-start = (bf16[144,768]{1,0:T(8,128)(2,1)S(1)}, bf16[144,768]{1,0:T(8,128)(2,1)S(1)}, u32[]{:S(2)}, u32[]{:S(2)}) collective-permute-start(bf16[144,768]{1,0:T(8,128)(2,1)S(1)} %get-tuple-element.328), channel_id=1, source_target_pairs={{0,1},{1,2},{2,3},{3,0},{4,5},{5,6},{6,7},{7,4},{8,9},{9,10},{10,1... | collective-permute-start | bytes 663560 | tf_op jit(solution)/shard_map/ppermute | solution.py:726
  5.9 24.2 %collective-permute-start.1 = (bf16[144,768]{1,0:T(8,128)(2,1)S(1)}, bf16[144,768]{1,0:T(8,128)(2,1)S(1)}, u32[]{:S(2)}, u32[]{:S(2)}) collective-permute-start(bf16[144,768]{1,0:T(8,128)(2,1)S(1)} %get-tuple-element.330), channel_id=1, source_target_pairs={{0,2},{1,3},{2,0},{3,1},{4,6},{5,7},{6,4},{7,5},{8,10},{9,11},{10,... | collective-permute-start | bytes 663560 | tf_op jit(solution)/shard_map/ppermute | solution.py:726
  8.5 21.6 %collective-permute-start.2 = (bf16[144,768]{1,0:T(8,128)(2,1)S(1)}, bf16[144,768]{1,0:T(8,128)(2,1)S(1)}, u32[]{:S(2)}, u32[]{:S(2)}) collective-permute-start(bf16[144,768]{1,0:T(8,128)(2,1)S(1)} %get-tuple-element.327), channel_id=1, source_target_pairs={{0,3},{1,0},{2,1},{3,2},{4,7},{5,4},{6,5},{7,6},{8,11},{9,8},{10,9... | collective-permute-start | bytes 663560 | tf_op jit(solution)/shard_map/ppermute | solution.py:726
  30.1 29.8 %collective-permute-start.3 = (bf16[144,768]{1,0:T(8,128)(2,1)S(1)}, bf16[144,768]{1,0:T(8,128)(2,1)S(1)}, u32[]{:S(2)}, u32[]{:S(2)}) collective-permute-start(bf16[144,768]{1,0:T(8,128)(2,1)S(1)} %get-tuple-element.164), channel_id=1, source_target_pairs={{0,1},{1,2},{2,3},{3,0},{4,5},{5,6},{6,7},{7,4},{8,9},{9,10},{10,1... | collective-permute-start | bytes 663560 | tf_op jit(solution)/shard_map/ppermute | solution.py:726
  30.8 29.1 %collective-permute-start.4 = (bf16[144,768]{1,0:T(8,128)(2,1)S(1)}, bf16[144,768]{1,0:T(8,128)(2,1)S(1)}, u32[]{:S(2)}, u32[]{:S(2)}) collective-permute-start(bf16[144,768]{1,0:T(8,128)(2,1)S(1)} %get-tuple-element.165), channel_id=1, source_target_pairs={{0,2},{1,3},{2,0},{3,1},{4,6},{5,7},{6,4},{7,5},{8,10},{9,11},{10,... | collective-permute-start | bytes 663560 | tf_op jit(solution)/shard_map/ppermute | solution.py:726
  31.1 28.8 %collective-permute-start.5 = (bf16[144,768]{1,0:T(8,128)(2,1)S(1)}, bf16[144,768]{1,0:T(8,128)(2,1)S(1)}, u32[]{:S(2)}, u32[]{:S(2)}) collective-permute-start(bf16[144,768]{1,0:T(8,128)(2,1)S(1)} %get-tuple-element.166), channel_id=1, source_target_pairs={{0,3},{1,0},{2,1},{3,2},{4,7},{5,4},{6,5},{7,6},{8,11},{9,8},{10,9... | collective-permute-start | bytes 663560 | tf_op jit(solution)/shard_map/ppermute | solution.py:726
  93.3 17.7 %collective-permute-start.6 = (bf16[1536,768]{1,0:T(8,128)(2,1)}, bf16[1536,768]{1,0:T(8,128)(2,1)}, u32[]{:S(2)}, u32[]{:S(2)}) collective-permute-start(bf16[1536,768]{1,0:T(8,128)(2,1)} %get-tuple-element.181), channel_id=1, source_target_pairs={{0,4},{4,0},{8,12},{12,8},{16,20},{20,16},{24,28},{28,24},{1,5},{5... | collective-permute-start | bytes 7077896 | tf_op jit(solution)/shard_map/ppermute | solution.py:719
  93.9 41.1 %collective-permute-start.7 = (bf16[144,768]{1,0:T(8,128)(2,1)}, bf16[144,768]{1,0:T(8,128)(2,1)}, u32[]{:S(2)}, u32[]{:S(2)}) collective-permute-start(bf16[144,768]{1,0:T(8,128)(2,1)} %get-tuple-element.195), channel_id=1, source_target_pairs={{0,1},{1,2},{2,3},{3,0},{4,5},{5,6},{6,7},{7,4},{8,9},{9,10},{10,1... | collective-permute-start | bytes 663560 | tf_op jit(solution)/shard_map/ppermute | solution.py:726
  94.5 40.5 %collective-permute-start.8 = (bf16[144,768]{1,0:T(8,128)(2,1)}, bf16[144,768]{1,0:T(8,128)(2,1)}, u32[]{:S(2)}, u32[]{:S(2)}) collective-permute-start(bf16[144,768]{1,0:T(8,128)(2,1)} %get-tuple-element.196), channel_id=1, source_target_pairs={{0,2},{1,3},{2,0},{3,1},{4,6},{5,7},{6,4},{7,5},{8,10},{9,11},{10,... | collective-permute-start | bytes 663560 | tf_op jit(solution)/shard_map/ppermute | solution.py:726
  96.0 39.1 %collective-permute-start.9 = (bf16[144,768]{1,0:T(8,128)(2,1)}, bf16[144,768]{1,0:T(8,128)(2,1)}, u32[]{:S(2)}, u32[]{:S(2)}) collective-permute-start(bf16[144,768]{1,0:T(8,128)(2,1)} %get-tuple-element.197), channel_id=1, source_target_pairs={{0,3},{1,0},{2,1},{3,2},{4,7},{5,4},{6,5},{7,6},{8,11},{9,8},{10,9... | collective-permute-start | bytes 663560 | tf_op jit(solution)/shard_map/ppermute | solution.py:726
  112.2 22.8 %collective-permute-start.10 = (bf16[2,384,384]{2,1,0:T(8,128)(2,1)S(1)}, bf16[2,384,384]{2,1,0:T(8,128)(2,1)S(1)}, u32[]{:S(2)}, u32[]{:S(2)}) collective-permute-start(bf16[2,384,384]{2,1,0:T(8,128)(2,1)S(1)} %fusion.11), channel_id=1, source_target_pairs={{0,8},{4,12},{8,0},{12,4},{16,24},{20,28},{24,16},{28,20},{1,9},{5... | collective-permute-start | bytes 1769480 | tf_op jit(solution)/shard_map/ppermute | solution.py:719
  115.8 19.2 %collective-permute-start.11 = (bf16[2,384,384]{2,1,0:T(8,128)(2,1)}, bf16[2,384,384]{2,1,0:T(8,128)(2,1)S(1)}, u32[]{:S(2)}, u32[]{:S(2)}) collective-permute-start(bf16[2,384,384]{2,1,0:T(8,128)(2,1)} %fusion.12), channel_id=1, source_target_pairs={{0,16},{4,20},{8,24},{12,28},{16,0},{20,4},{24,8},{28,12},{1,17},{... | collective-permute-start | bytes 1769480 | tf_op jit(solution)/shard_map/ppermute | solution.py:719
  135.9 28.6 %collective-permute-start.14 = (bf16[384,3840]{1,0:T(8,128)(2,1)}, bf16[384,3840]{1,0:T(8,128)(2,1)S(1)}, u32[]{:S(2)}, u32[]{:S(2)}) collective-permute-start(bf16[384,3840]{1,0:T(8,128)(2,1)} %get-tuple-element.218), channel_id=1, source_target_pairs={{0,4},{4,0},{8,12},{12,8},{16,20},{20,16},{24,28},{28,24},{1,5},{5... | collective-permute-start | bytes 8847368 | tf_op jit(solution)/shard_map/ppermute | solution.py:719
  144.6 19.8 %collective-permute-start.12 = (bf16[384,384]{1,0:T(8,128)(2,1)}, bf16[384,384]{1,0:T(8,128)(2,1)}, u32[]{:S(2)}, u32[]{:S(2)}) collective-permute-start(bf16[384,384]{1,0:T(8,128)(2,1)} %get-tuple-element.322), channel_id=1, source_target_pairs={{0,16},{4,20},{8,24},{12,28},{16,0},{20,4},{24,8},{28,12},{1,17},{... | collective-permute-start | bytes 884744 | tf_op jit(solution)/shard_map/ppermute | solution.py:719
  145.2 19.3 %collective-permute-start.13 = (bf16[384,384]{1,0:T(8,128)(2,1)}, bf16[384,384]{1,0:T(8,128)(2,1)}, u32[]{:S(2)}, u32[]{:S(2)}) collective-permute-start(bf16[384,384]{1,0:T(8,128)(2,1)} %get-tuple-element.321), channel_id=1, source_target_pairs={{0,8},{4,12},{8,0},{12,4},{16,24},{20,28},{24,16},{28,20},{1,9},{5... | collective-permute-start | bytes 884744 | tf_op jit(solution)/shard_map/ppermute | solution.py:719
  171.5 25.3 %collective-permute-start.15 = (bf16[96,768]{1,0:T(8,128)(2,1)}, bf16[96,768]{1,0:T(8,128)(2,1)}, u32[]{:S(2)}, u32[]{:S(2)}) collective-permute-start(bf16[96,768]{1,0:T(8,128)(2,1)} %get-tuple-element.340), channel_id=1, source_target_pairs={{0,1},{1,2},{2,3},{3,0},{4,5},{5,6},{6,7},{7,4},{8,9},{9,10},{10,1... | collective-permute-start | bytes 442376 | tf_op jit(solution)/shard_map/ppermute | solution.py:798
  171.5 25.3 %collective-permute-start.16 = (bf16[96,768]{1,0:T(8,128)(2,1)}, bf16[96,768]{1,0:T(8,128)(2,1)}, u32[]{:S(2)}, u32[]{:S(2)}) collective-permute-start(bf16[96,768]{1,0:T(8,128)(2,1)} %get-tuple-element.339), channel_id=1, source_target_pairs={{0,2},{1,3},{2,0},{3,1},{4,6},{5,7},{6,4},{7,5},{8,10},{9,11},{10,... | collective-permute-start | bytes 442376 | tf_op jit(solution)/shard_map/ppermute | solution.py:798
  172.4 24.4 %collective-permute-start.17 = (bf16[96,768]{1,0:T(8,128)(2,1)}, bf16[96,768]{1,0:T(8,128)(2,1)}, u32[]{:S(2)}, u32[]{:S(2)}) collective-permute-start(bf16[96,768]{1,0:T(8,128)(2,1)} %get-tuple-element.338), channel_id=1, source_target_pairs={{0,3},{1,0},{2,1},{3,2},{4,7},{5,4},{6,5},{7,6},{8,11},{9,8},{10,9... | collective-permute-start | bytes 442376 | tf_op jit(solution)/shard_map/ppermute | solution.py:798
  175.3 21.5 %collective-permute-start.18 = (bf16[2,96,1920]{2,1,0:T(8,128)(2,1)}, bf16[2,96,1920]{2,1,0:T(8,128)(2,1)}, u32[]{:S(2)}, u32[]{:S(2)}) collective-permute-start(bf16[2,96,1920]{2,1,0:T(8,128)(2,1)} %fusion.3), channel_id=1, source_target_pairs={{0,8},{4,12},{8,0},{12,4},{16,24},{20,28},{24,16},{28,20},{1,9},{5... | collective-permute-start | bytes 2211848 | tf_op jit(solution)/shard_map/ppermute | solution.py:719
  176.8 20.0 %collective-permute-start.19 = (bf16[2,96,1920]{2,1,0:T(8,128)(2,1)}, bf16[2,96,1920]{2,1,0:T(8,128)(2,1)}, u32[]{:S(2)}, u32[]{:S(2)}) collective-permute-start(bf16[2,96,1920]{2,1,0:T(8,128)(2,1)} %fusion.4), channel_id=1, source_target_pairs={{0,16},{4,20},{8,24},{12,28},{16,0},{20,4},{24,8},{28,12},{1,17},{... | collective-permute-start | bytes 2211848 | tf_op jit(solution)/shard_map/ppermute | solution.py:719
  199.1 18.5 %collective-permute-start.21 = (bf16[96,768]{1,0:T(8,128)(2,1)}, bf16[96,768]{1,0:T(8,128)(2,1)}, u32[]{:S(2)}, u32[]{:S(2)}) collective-permute-start(bf16[96,768]{1,0:T(8,128)(2,1)} %fusion.36.refs_0_), channel_id=1, source_target_pairs={{0,2},{1,3},{2,0},{3,1},{4,6},{5,7},{6,4},{7,5},{8,10},{9,11},{10,... | collective-permute-start | bytes 442376 | tf_op jit(solution)/shard_map/ppermute | solution.py:801
  203.9 17.8 %collective-permute-start.23 = (bf16[96,1920]{1,0:T(8,128)(2,1)}, bf16[96,1920]{1,0:T(8,128)(2,1)}, u32[]{:S(2)}, u32[]{:S(2)}) collective-permute-start(bf16[96,1920]{1,0:T(8,128)(2,1)} %get-tuple-element.318), channel_id=1, source_target_pairs={{0,16},{4,20},{8,24},{12,28},{16,0},{20,4},{24,8},{28,12},{1,17},{... | collective-permute-start | bytes 1105928 | tf_op jit(solution)/shard_map/ppermute | solution.py:719
  204.4 17.3 %collective-permute-start.24 = (bf16[96,1920]{1,0:T(8,128)(2,1)S(1)}, bf16[96,1920]{1,0:T(8,128)(2,1)}, u32[]{:S(2)}, u32[]{:S(2)}) collective-permute-start(bf16[96,1920]{1,0:T(8,128)(2,1)S(1)} %get-tuple-element.317), channel_id=1, source_target_pairs={{0,8},{4,12},{8,0},{12,4},{16,24},{20,28},{24,16},{28,20},{1,9},{5... | collective-permute-start | bytes 1105928 | tf_op jit(solution)/shard_map/ppermute | solution.py:719
  205.0 16.8 %collective-permute-start.25 = (bf16[384,2304]{1,0:T(8,128)(2,1)}, bf16[384,2304]{1,0:T(8,128)(2,1)}, u32[]{:S(2)}, u32[]{:S(2)}) collective-permute-start(bf16[384,2304]{1,0:T(8,128)(2,1)} %get-tuple-element.250), channel_id=1, source_target_pairs={{0,4},{4,0},{8,12},{12,8},{16,20},{20,16},{24,28},{28,24},{1,5},{5... | collective-permute-start | bytes 5308424 | tf_op jit(solution)/shard_map/ppermute | solution.py:719
  224.3 22.0 %collective-permute-start.30 = (bf16[2,96,1152]{2,1,0:T(8,128)(2,1)S(1)}, bf16[2,96,1152]{2,1,0:T(8,128)(2,1)S(1)}, u32[]{:S(2)}, u32[]{:S(2)}) collective-permute-start(bf16[2,96,1152]{2,1,0:T(8,128)(2,1)S(1)} %fusion.19), channel_id=1, source_target_pairs={{0,8},{4,12},{8,0},{12,4},{16,24},{20,28},{24,16},{28,20},{1,9},{5... | collective-permute-start | bytes 1327112 | tf_op jit(solution)/shard_map/ppermute | solution.py:719
  225.9 20.5 %collective-permute-start.31 = (bf16[2,96,1152]{2,1,0:T(8,128)(2,1)S(1)}, bf16[2,96,1152]{2,1,0:T(8,128)(2,1)S(1)}, u32[]{:S(2)}, u32[]{:S(2)}) collective-permute-start(bf16[2,96,1152]{2,1,0:T(8,128)(2,1)S(1)} %fusion.20), channel_id=1, source_target_pairs={{0,16},{4,20},{8,24},{12,28},{16,0},{20,4},{24,8},{28,12},{1,17},{... | collective-permute-start | bytes 1327112 | tf_op jit(solution)/shard_map/ppermute | solution.py:719
  246.4 23.6 %collective-permute-start.32 = (bf16[144,768]{1,0:T(8,128)(2,1)S(1)}, bf16[144,768]{1,0:T(8,128)(2,1)S(1)}, u32[]{:S(2)}, u32[]{:S(2)}) collective-permute-start(bf16[144,768]{1,0:T(8,128)(2,1)S(1)} %copy-done.40), channel_id=1, source_target_pairs={{0,1},{1,2},{2,3},{3,0},{4,5},{5,6},{6,7},{7,4},{8,9},{9,10},{10,1... | collective-permute-start | bytes 663560 | tf_op jit(solution)/shard_map/ppermute | solution.py:889
  252.9 17.1 %collective-permute-start.37 = (bf16[96,1152]{1,0:T(8,128)(2,1)S(1)}, bf16[96,1152]{1,0:T(8,128)(2,1)S(1)}, u32[]{:S(2)}, u32[]{:S(2)}) collective-permute-start(bf16[96,1152]{1,0:T(8,128)(2,1)S(1)} %get-tuple-element.326), channel_id=1, source_target_pairs={{0,16},{4,20},{8,24},{12,28},{16,0},{20,4},{24,8},{28,12},{1,17},{... | collective-permute-start | bytes 663560 | tf_op jit(solution)/shard_map/ppermute | solution.py:719
  270.0 17.1 %collective-permute-start.39 = (bf16[144,768]{1,0:T(8,128)(2,1)S(1)}, bf16[144,768]{1,0:T(8,128)(2,1)S(1)}, u32[]{:S(2)}, u32[]{:S(2)}) collective-permute-start(bf16[144,768]{1,0:T(8,128)(2,1)S(1)} %copy-done.39), channel_id=1, source_target_pairs={{0,3},{1,0},{2,1},{3,2},{4,7},{5,4},{6,5},{7,6},{8,11},{9,8},{10,9... | collective-permute-start | bytes 663560 | tf_op jit(solution)/shard_map/ppermute | solution.py:889
  287.2 19.8 %collective-permute-start.47 = (bf16[24,2304]{1,0:T(8,128)(2,1)S(1)}, bf16[24,2304]{1,0:T(8,128)(2,1)S(1)}, u32[]{:S(2)}, u32[]{:S(2)}) collective-permute-start(bf16[24,2304]{1,0:T(8,128)(2,1)S(1)} %fusion.39.refs_0_), channel_id=1, source_target_pairs={{0,1},{1,2},{2,3},{3,0},{4,5},{5,6},{6,7},{7,4},{8,9},{9,10},{10,1... | collective-permute-start | bytes 331784 | tf_op jit(solution)/shard_map/ppermute | solution.py:801
  289.7 17.3 %collective-permute-start.48 = (bf16[24,2304]{1,0:T(8,128)(2,1)S(1)}, bf16[24,2304]{1,0:T(8,128)(2,1)S(1)}, u32[]{:S(2)}, u32[]{:S(2)}) collective-permute-start(bf16[24,2304]{1,0:T(8,128)(2,1)S(1)} %fusion.39.refs_0_), channel_id=1, source_target_pairs={{0,2},{1,3},{2,0},{3,1},{4,6},{5,7},{6,4},{7,5},{8,10},{9,11},{10,... | collective-permute-start | bytes 331784 | tf_op jit(solution)/shard_map/ppermute | solution.py:801
  297.4 22.5 %collective-permute-start.44 = (bf16[144,768]{1,0:T(8,128)(2,1)S(1)}, bf16[144,768]{1,0:T(8,128)(2,1)S(1)}, u32[]{:S(2)}, u32[]{:S(2)}) collective-permute-start(bf16[144,768]{1,0:T(8,128)(2,1)S(1)} %copy-done.38), channel_id=1, source_target_pairs={{0,2},{1,3},{2,0},{3,1},{4,6},{5,7},{6,4},{7,5},{8,10},{9,11},{10,... | collective-permute-start | bytes 663560 | tf_op jit(solution)/shard_map/ppermute | solution.py:889
  (63 other events, 588.4 us)

commit v3 on v2

--- a/solution.py
+++ b/solution.py
@@ -16,6 +16,7 @@
 NEG = -1e30
 BOX = 64
 RT = 64
+LR = 32
 EDGE = 16
 CELLS = 56
 OFFSETS = (-128, -64, 0, 64)
@@ -49,8 +50,19 @@
     return [slice(128 * c, 128 * (c + 1)) for c in range(n // 128)]
 
 
+def line(ref, part=slice(None)):
+    return ref[part].reshape(1, -1)
+
+
 def row_sum(x):
     return jnp.sum(x, axis=0, keepdims=True)
+
+
+def fold(x):
+    out = x[:8]
+    for r in range(8, x.shape[0], 8):
+        out = out + x[r : r + 8]
+    return out
 
 
 def shift_rows(window, offset, rows):
@@ -66,17 +78,49 @@
         dest[pl.ds(pl.multiple_of(row0 + source * stretch, 16), stretch), :] = block[...].astype(dest.dtype)
 
 
-def front_kernel(info_ref, edge_ref, *refs, n_seq):
+def turned_transpose(x_ref, turn_ref, core, block, dest, raw):
+    rows = dest.shape[0]
+    if block % 16:
+        dest[...] = dot_t(turn_ref[...], x_ref[...]).astype(BF)
+        return
+    raw[...] = jnp.transpose(x_ref[...])
+    half = rows // 2
+    for k in range(half // block):
+        for side in range(2):
+            parity = core if side == 0 else 1 - core
+            source = pl.multiple_of((2 * k + parity) * block, 16)
+            dest[side * half + k * block : side * half + (k + 1) * block, :] = raw[pl.ds(source, block), :]
+
+
+def moves(pairs, sems):
+    return [pltpu.make_async_copy(source, dest, sems.at[n]) for n, (source, dest) in enumerate(pairs)]
+
+
+def start(copies):
+    for c in copies:
+        c.start()
+
+
+def wait(copies):
+    for c in copies:
+        c.wait()
+
+
+def front_kernel(info_ref, edge_ref, *refs, n_seq, block):
     blocks = refs[:n_seq]
-    (ct_ref, cp_ref, pm_ref, turn_ref, wq_ref, bq_ref, wk_ref, wv_ref, bv_ref, oh_ref, wt_ref, ord_ref,
-     set_ref, et_ref, q_ref, k_ref, v_ref, p_ref, o_ref,
-     entry_ref, xs_ref, ms_ref, ka_ref, qa_ref, s_ref) = refs[n_seq:]
+    (ct_ref, cp_ref, pm_ref, turn_ref, wq_any, bq_ref, wk_any, wv_any, bv_ref, oh_ref, wt_ref, ord_ref,
+     set_any, et_any, q_any, k_any, v_any, p_ref, o_ref,
+     entry_ref, xs_ref, ms_ref, ka_ref, qa_ref, s_ref, raw_ref,
+     set_ref, et_ref, q_ref, k_ref, v_ref, wq_ref, wk_ref, wv_ref, in_sems, out_sems) = refs[n_seq:]
     g = pl.program_id(0)
+    arriving = moves([(wq_any, wq_ref), (wk_any, wk_ref), (wv_any, wv_ref)], in_sems)
+    leaving = moves([(set_ref, set_any), (et_ref, et_any), (q_ref, q_any), (k_ref, k_any), (v_ref, v_any)], out_sems)
     length, width = entry_ref.shape
     place, count = info_ref[0], info_ref[1]
 
     @pl.when(g == 0)
     def _():
+        start(arriving)
         zero = jnp.zeros((EDGE, width), F32)
         xs_ref[0:EDGE, :] = zero
         xs_ref[EDGE + length :, :] = zero
@@ -114,14 +158,20 @@
                 term = term + shift_rows(window, off, CELLS) * (cp_ref[n : n + 1, c] * pm_ref[:, n : n + 1])
             set_ref[TEXT : TEXT + CELLS, c] = set_ref[TEXT : TEXT + CELLS, c] + term
         entry_ref[...] = set_ref[...].astype(BF)
-        et_ref[...] = dot_t(turn_ref[...], entry_ref[...]).astype(BF)
+        turned_transpose(entry_ref, turn_ref, info_ref[2], block, et_ref, raw_ref)
+        wait(arriving)
         for c in range(width // 256):
             s = slice(256 * c, 256 * (c + 1))
-            q_ref[:, s] = (dot(entry_ref[...], wq_ref[:, s]) + bq_ref[:, s]).astype(BF) * jnp.asarray(SCALE, BF)
+            q_ref[:, s] = (dot(entry_ref[...], wq_ref[:, s]) + line(bq_ref, s)).astype(BF) * jnp.asarray(SCALE, BF)
             k_ref[:, s] = dot(entry_ref[...], wk_ref[:, s]).astype(BF)
-            v_ref[:, s] = (dot(entry_ref[...], wv_ref[:, s]) + bv_ref[:, s]).astype(BF)
+            v_ref[:, s] = (dot(entry_ref[...], wv_ref[:, s]) + line(bv_ref, s)).astype(BF)
         ka_ref[:, 128:256] = oh_ref[...]
         ka_ref[:, 256:384] = oh_ref[...]
+        start(leaving)
+
+    @pl.when(g == pl.num_programs(0) - 1)
+    def _():
+        wait(leaving)
 
     pair = pl.ds(pl.multiple_of(g * 128, 128), 128)
     ka_ref[:, 0:128] = k_ref[:, pair]
@@ -160,7 +210,7 @@
     o_ref[...] = jnp.where(lane < 64, outs[0], outs[1]).astype(BF)
 
 
-def front(info, edge, blocks, ct, cp, pm, turn, wq, bq, wk, wv, bv, oh, wt, od):
+def front(info, edge, blocks, ct, cp, pm, turn, wq, bq, wk, wv, bv, oh, wt, od, block):
     n_seq = len(blocks)
     stretch, width = blocks[0].shape
     length = n_seq * stretch
@@ -168,20 +218,23 @@
     sds = jax.ShapeDtypeStruct
     flops = 2 * length * width * width * 3 + heads * 2 * length * length * (384 + 128)
     return pl.pallas_call(
-        functools.partial(front_kernel, n_seq=n_seq),
+        functools.partial(front_kernel, n_seq=n_seq, block=block),
         out_shape=(sds((length, width), F32), sds((width, length), BF)) + (sds((length, width), BF),) * 3
         + (sds((heads, length, length), BF), sds((length, width), BF)),
         grid_spec=pltpu.PrefetchScalarGridSpec(
             num_scalar_prefetch=2, grid=(heads // 2,),
             in_specs=[whole((stretch, width))] * n_seq
-            + [whole(ct.shape), whole(cp.shape), whole(pm.shape), whole(turn.shape), whole(wq.shape), whole(bq.shape), whole(wk.shape),
-               whole(wv.shape), whole(bv.shape), whole(oh.shape),
+            + [whole(ct.shape), whole(cp.shape), whole(pm.shape), whole(turn.shape), pl.BlockSpec(memory_space=pl.ANY), whole(bq.shape), pl.BlockSpec(memory_space=pl.ANY),
+               pl.BlockSpec(memory_space=pl.ANY), whole(bv.shape), whole(oh.shape),
                pl.BlockSpec((2, 128, 256), lambda g, *_: (g, 0, 0)),
                pl.BlockSpec((2, len(OFFSETS), RT, 128), lambda g, *_: (g, 0, 0, 0))],
-            out_specs=[whole_out((length, width)), whole_out((width, length))] + [whole_out((length, width))] * 3
+            out_specs=[pl.BlockSpec(memory_space=pl.ANY)] * 5
             + [pl.BlockSpec((2, length, length), lambda g, *_: (g, 0, 0)), pl.BlockSpec((length, 128), lambda g, *_: (0, g))],
             scratch_shapes=[pltpu.VMEM((length, width), BF), pltpu.VMEM((length + 2 * EDGE, width), F32), pltpu.VMEM((length + 2 * EDGE, width), F32),
-                            pltpu.VMEM((length, 384), BF), pltpu.VMEM((2, length, 384), BF), pltpu.VMEM((2, length, length), F32)],
+                            pltpu.VMEM((length, 384), BF), pltpu.VMEM((2, length, 384), BF), pltpu.VMEM((2, length, length), F32), pltpu.VMEM((width, length), BF),
+                            pltpu.VMEM((length, width), F32), pltpu.VMEM((width, length), BF)]
+            + [pltpu.VMEM((length, width), BF)] * 3 + [pltpu.VMEM((width, width), BF)] * 3
+            + [pltpu.SemaphoreType.DMA((3,)), pltpu.SemaphoreType.DMA((5,))],
         ),
         cost_estimate=pl.CostEstimate(flops=25_000_000_000, bytes_accessed=8 << 20, transcendentals=0),
         name="front",
@@ -201,13 +254,13 @@
 
 def gelu_pair(x):
     t = 1.0 / (1.0 + jnp.abs(x) * (ERF_P * 0.7071067811865476))
-    bell = jnp.exp(x * x * -0.5)
+    bell = jnp.exp2(x * x * -0.7213475204444817)
     q = jnp.full_like(t, 0.5 * ERF_Q[7])
     for k in range(6, -1, -1):
         q = q * t + 0.5 * ERF_Q[k]
     tail = q * t * bell
     cdf = jnp.where(x < 0, tail, 1.0 - tail)
-    return x * cdf, cdf + x * (bell * 0.3989422804014327)
+    return x * cdf, cdf + x * bell * 0.3989422804014327
 
 
 def middle_kernel(info_ref, *refs, n_seq, tiles, tile, block):
@@ -215,30 +268,40 @@
     (att_ref, set_ref, wo_ref, bo_ref, ng_ref, ns_ref, w1_ref, b1_ref, w2_ref, b2_ref, fg_ref, fs_ref, turn_ref) = refs[n_seq : n_seq + 13]
     outs = refs[n_seq + 13 :]
     mixed = outs[:n_seq]
-    (xh_ref, rs_ref, fl_ref, gp_ref, ds_ref, dr_ref, gk_ref, gs_ref, sm_ref, act_ref, fn_ref, acc_ref, cot_ref, mix_ref, e_ref, g_ref) = outs[n_seq:]
+    (xh_any, rs_any, fl_any, gp_ref, ds_any, dr_any, gk_ref, gs_ref, sm_ref, act_ref, fn_ref, acc_ref, cot_ref, mix_ref, e_ref, g_ref, b1_rows,
+     xh_ref, rs_ref, fl_ref, ds_ref, dr_ref, cot_sems, norm_sems, out_sems) = outs[n_seq:]
     i = pl.program_id(0)
     length, width = fl_ref.shape
     place = info_ref[0]
+    stretch = length // n_seq
+    block_of = lambda ref, d: ref.at[pl.ds(pl.multiple_of(lax.rem(place + d, n_seq) * stretch, 16), stretch), :]
+    arriving = moves([(cots[d], block_of(cot_ref, n_seq - d)) for d in range(n_seq)], cot_sems)
+    normed = moves([(xh_ref, xh_any), (rs_ref, rs_any), (fl_ref, fl_any)], norm_sems)
+    leaving = moves([(ds_ref, ds_any), (dr_ref, dr_any)] + [(block_of(mix_ref, d), mixed[d]) for d in range(n_seq)], out_sems)
 
     @pl.when(i == 0)
     def _():
+        start(arriving)
         for c in range(width // 256):
             s = slice(256 * c, 256 * (c + 1))
             acc_ref[:, s] = dot(att_ref[...], wo_ref[:, s])
 
         def chunk(j, carry):
-            r = pl.ds(pl.multiple_of(j * RT, RT), RT)
-            u = set_ref[r, :] + (acc_ref[r, :] + bo_ref[...])
+            r = pl.ds(pl.multiple_of(j * LR, LR), LR)
+            u = set_ref[r, :] + (acc_ref[r, :] + line(bo_ref))
             xhat, rs = norm_stats(u)
             xh_ref[r, :] = xhat
-            rs_ref[r, :] = jnp.broadcast_to(rs, (RT, 128))
-            fn = xhat * ng_ref[...] + ns_ref[...]
+            rs_ref[r, :] = jnp.broadcast_to(rs, (LR, 128))
+            fn = xhat * line(ng_ref) + line(ns_ref)
             fn_ref[r, :] = fn
             fl_ref[r, :] = fn.astype(BF)
+            acc_ref[r, :] = jnp.broadcast_to(line(b2_ref), (LR, width))
             return carry
 
-        lax.fori_loop(0, length // RT, chunk, 0)
-        gather_page(cot_ref, 0, place, n_seq, cots[0], cots[1:])
+        lax.fori_loop(0, length // LR, chunk, 0, unroll=2)
+        start(normed)
+        for t in range(tiles):
+            b1_rows[t] = line(b1_ref, slice(t * tile, (t + 1) * tile))
 
     @pl.when(i < tiles)
     def _():
@@ -247,41 +310,39 @@
             e_ref[n] = dot(fl_ref[...], w1_ref[:, n * half : (n + 1) * half])
         for n in range(3):
             s = slice(n * half, (n + 1) * half)
-            act, gp = gelu_pair(e_ref[n] + b1_ref[:, s])
+            act, gp = gelu_pair(e_ref[n] + b1_rows[i, :, s])
             act_ref[i, :, s] = act.astype(BF)
             gp_ref[:, s] = gp.astype(gp_ref.dtype)
-        part = dot(act_ref[i], w2_ref[...])
-
-        @pl.when(i == 0)
-        def _():
-            acc_ref[...] = part
-
-        @pl.when(i > 0)
-        def _():
-            acc_ref[...] += part
+        for c in range(width // 256):
+            s = slice(256 * c, 256 * (c + 1))
+            acc_ref[:, s] += dot(act_ref[i], w2_ref[:, s])
 
     @pl.when(i == tiles - 1)
     def _():
+        wait(arriving)
+
         def chunk(j, sums):
-            r0 = pl.multiple_of(j * RT, RT)
-            r = pl.ds(r0, RT)
-            second = fn_ref[r, :] + (acc_ref[r, :] + b2_ref[...])
+            r0 = pl.multiple_of(j * LR, LR)
+            r = pl.ds(r0, LR)
+            second = fn_ref[r, :] + acc_ref[r, :]
             xhat, rs = norm_stats(second)
-            mix_ref[r, :] = (xhat * fg_ref[...] + fs_ref[...]).astype(BF)
+            mix_ref[r, :] = (xhat * line(fg_ref) + line(fs_ref)).astype(BF)
             cot = cot_ref[r, :].astype(F32)
-            back = norm_back(cot * fg_ref[...], xhat, rs)
+            back = norm_back(cot * line(fg_ref), xhat, rs)
             ds_ref[r, :] = back
             low = back.astype(BF)
             dr_ref[r, :] = low
-            return (sums[0] + row_sum(cot * xhat), sums[1] + row_sum(cot), sums[2] + row_sum(low.astype(F32)))
-
-        sums = lax.fori_loop(0, length // RT, chunk, (jnp.zeros((1, width), F32),) * 3)
+            return (sums[0] + fold(cot * xhat), sums[1] + fold(cot), sums[2] + fold(low.astype(F32)))
+
+        sums = lax.fori_loop(0, length // LR, chunk, (jnp.zeros((8, width), F32),) * 3, unroll=2)
         for n in range(3):
-            sm_ref[n : n + 1, :] = sums[n]
-        stretch = length // n_seq
-        for d in range(n_seq):
-            dest = lax.rem(place + d, n_seq)
-            mixed[d][...] = mix_ref[pl.ds(pl.multiple_of(dest * stretch, 16), stretch), :]
+            sm_ref[n : n + 1, :] = row_sum(sums[n])
+        start(leaving)
+
+    @pl.when(i == pl.num_programs(0) - 1)
+    def _():
+        wait(normed)
+        wait(leaving)
 
     @pl.when(i >= tiles)
     def _():
@@ -314,38 +375,44 @@
            sds((length, width), F32), sds((length, width), BF), sds((ff // 2, width), BF), sds((ff // 2, width), BF), sds((8, width), F32)),
         grid_spec=pltpu.PrefetchScalarGridSpec(
             num_scalar_prefetch=1, grid=(2 * tiles,),
-            in_specs=[whole((stretch, width))] * n_seq
+            in_specs=[pl.BlockSpec(memory_space=pl.ANY)] * n_seq
             + [whole(att.shape), whole(settled.shape), whole(wo.shape), whole(bo.shape), whole(ng.shape), whole(ns.shape),
-               pl.BlockSpec((width, tile), lambda i, *_: (0, early(i))), pl.BlockSpec((1, tile), lambda i, *_: (0, early(i))),
+               pl.BlockSpec((width, tile), lambda i, *_: (0, early(i))), whole(b1.shape),
                pl.BlockSpec((tile, width), lambda i, *_: (early(i), 0)), whole(b2.shape), whole(fg.shape), whole(fs.shape), whole(turn.shape)],
-            out_specs=[whole_out((stretch, width))] * n_seq
-            + [whole_out((length, width)), whole_out((length, 128)), whole_out((length, width)),
-               pl.BlockSpec((length, tile), lambda i, *_: (0, early(i))),
-               whole_out((length, width)), whole_out((length, width)),
+            out_specs=[pl.BlockSpec(memory_space=pl.ANY)] * (n_seq + 3)
+            + [pl.BlockSpec((length, tile), lambda i, *_: (0, early(i))), pl.BlockSpec(memory_space=pl.ANY), pl.BlockSpec(memory_space=pl.ANY),
                pl.BlockSpec((tile // 2, width), lambda i, *_: (late(i), 0)), pl.BlockSpec((tile // 2, width), lambda i, *_: (late(i), 0)),
                whole_out((8, width))],
             scratch_shapes=[pltpu.VMEM((tiles, length, tile), BF), pltpu.VMEM((length, width), F32), pltpu.VMEM((length, width), F32),
                             pltpu.VMEM((length, width), BF), pltpu.VMEM((length, width), BF), pltpu.VMEM((3, length, tile // 3), F32),
-                            pltpu.VMEM((tile, width), BF)],
+                            pltpu.VMEM((tile, width), BF), pltpu.VMEM((tiles, 1, tile), F32),
+                            pltpu.VMEM((length, width), F32), pltpu.VMEM((length, 128), F32), pltpu.VMEM((length, width), BF),
+                            pltpu.VMEM((length, width), F32), pltpu.VMEM((length, width), BF),
+                            pltpu.SemaphoreType.DMA((n_seq,)), pltpu.SemaphoreType.DMA((3,)), pltpu.SemaphoreType.DMA((2 + n_seq,))],
         ),
         cost_estimate=pl.CostEstimate(flops=35_000_000_000, bytes_accessed=8 << 20, transcendentals=0),
         name="middle",
     )(info, *cots, att, settled, wo, bo, ng, ns, w1, b1, w2, b2, fg, fs, turn)
 
 
-def back_kernel(*refs, tiles, last):
+def back_kernel(info_ref, *refs, tiles, last, block):
+    core = info_ref[2]
     if last:
-        (dr_ref, in_ref, w2_ref, gp_ref, w1_ref, fl_ref, turn_ref, xh_ref, rs_ref, ng_ref, att_ref, wo_ref) = refs[:12]
-        (gk_ref, gs_ref, be_ref, df_ref, da_ref, sm_ref, flt_ref, acc_ref, db_ref) = refs[-9:]
+        (dr_ref, in_ref, w2_ref, gp_ref, w1_ref, fl_ref, turn_ref, xh_any, rs_any, ng_ref, att_any, wo_any) = refs[:12]
+        (gk_ref, gs_ref, be_ref, df_ref, da_ref, sm_ref, flt_ref, raw_ref, acc_ref, db_ref,
+         xh_ref, rs_ref, att_ref, wo_ref, sems) = refs[-15:]
+        arriving = moves([(xh_any, xh_ref), (rs_any, rs_ref), (att_any, att_ref), (wo_any, wo_ref)], sems)
     else:
         (dr_ref, in_ref, w2_ref, gp_ref, w1_ref, fl_ref, turn_ref) = refs[:7]
-        (gk_ref, gs_ref, be_ref, acc_ref, flt_ref) = refs[-5:]
+        (gk_ref, gs_ref, be_ref, acc_ref, flt_ref, raw_ref) = refs[-6:]
     i = pl.program_id(0)
     length, width = dr_ref.shape
 
     @pl.when(i == 0)
     def _():
-        flt_ref[...] = dot_t(turn_ref[...], fl_ref[...]).astype(BF)
+        if last:
+            start(arriving)
+        turned_transpose(fl_ref, turn_ref, core, block, flt_ref, raw_ref)
         acc_ref[...] = in_ref[...]
 
     @pl.when(i < tiles)
@@ -363,53 +430,61 @@
 
     @pl.when(i == tiles)
     def _():
+        wait(arriving)
+
         def chunk(j, sums):
-            r = pl.ds(pl.multiple_of(j * RT, RT), RT)
+            r = pl.ds(pl.multiple_of(j * LR, LR), LR)
             first = acc_ref[r, :]
             xhat = xh_ref[r, :]
-            back = norm_back(first * ng_ref[...], xhat, rs_ref[r, 0:1])
+            back = norm_back(first * line(ng_ref), xhat, rs_ref[r, 0:1])
             df_ref[r, :] = back
             low = back.astype(BF)
             db_ref[r, :] = low
-            return (sums[0] + row_sum(first * xhat), sums[1] + row_sum(first), sums[2] + row_sum(low.astype(F32)))
-
-        sums = lax.fori_loop(0, length // RT, chunk, (jnp.zeros((1, width), F32),) * 3)
+            return (sums[0] + fold(first * xhat), sums[1] + fold(first), sums[2] + fold(low.astype(F32)))
+
+        sums = lax.fori_loop(0, length // LR, chunk, (jnp.zeros((8, width), F32),) * 3, unroll=2)
         for n in range(3):
-            sm_ref[n : n + 1, :] = sums[n]
+            sm_ref[n : n + 1, :] = row_sum(sums[n])
         da_ref[...] = dot_t(db_ref[...], wo_ref[...]).astype(BF)
-        grad = dot(dot_t(turn_ref[...], att_ref[...]).astype(BF), db_ref[...]).astype(BF)
+        turned_transpose(att_ref, turn_ref, core, block, flt_ref, raw_ref)
+        grad = dot(flt_ref[...], db_ref[...]).astype(BF)
         gk_ref[...] = grad[: width // 2]
         gs_ref[...] = grad[width // 2 :]
 
 
-def back(first, tiles, dr, acc, w2, gp, w1, fl, turn, filled=(), norm=None):
+def back(info, block, first, tiles, dr, acc, w2, gp, w1, fl, turn, filled=(), norm=None):
     length, width = dr.shape
     ff = w1.shape[1]
     last = norm is not None
     sds = jax.ShapeDtypeStruct
     at = lambda i: jnp.minimum(i, tiles - 1) + first
-    grad = pl.BlockSpec((width // 2, width), lambda i: (0, i + first))
+    grad = pl.BlockSpec((width // 2, width), lambda i, *_: (0, i + first))
     args = [dr, acc, w2, gp, w1, fl, turn] + list(norm or ())
     out_shape = [sds((width // 2, ff + width), BF), sds((width // 2, ff + width), BF), sds((1, ff), F32), sds((length, width), F32)]
-    out_specs = [grad, grad, pl.BlockSpec((1, width), lambda i: (0, at(i))), whole_out((length, width))]
-    scratch = [pltpu.VMEM((width, length), BF)]
+    out_specs = [grad, grad, pl.BlockSpec((1, width), lambda i, *_: (0, at(i))), whole_out((length, width))]
+    scratch = [pltpu.VMEM((width, length), BF), pltpu.VMEM((width, length), BF)]
     if last:
         out_shape += [sds((length, width), BF), sds((8, width), F32)]
         out_specs += [whole_out((length, width)), whole_out((8, width))]
-        scratch += [pltpu.VMEM((length, width), F32), pltpu.VMEM((length, width), BF)]
+        scratch += [pltpu.VMEM((length, width), F32), pltpu.VMEM((length, width), BF), pltpu.VMEM((length, width), F32),
+                    pltpu.VMEM((length, 128), F32), pltpu.VMEM((length, width), BF), pltpu.VMEM((width, width), BF),
+                    pltpu.SemaphoreType.DMA((4,))]
     return pl.pallas_call(
-        functools.partial(back_kernel, tiles=tiles, last=last),
+        functools.partial(back_kernel, tiles=tiles, last=last, block=block),
         out_shape=tuple(out_shape),
-        grid=(tiles + last,),
-        in_specs=[whole(dr.shape), whole(acc.shape), pl.BlockSpec((width, width), lambda i: (at(i), 0)),
-                  pl.BlockSpec((length, width), lambda i: (0, at(i))), pl.BlockSpec((width, width), lambda i: (0, at(i)))]
-        + [whole(x.shape) for x in args[5:]] + [pl.BlockSpec(memory_space=pl.ANY)] * len(filled),
-        out_specs=out_specs,
-        scratch_shapes=scratch,
-        input_output_aliases={len(args) + n: n for n in range(len(filled))},
+        grid_spec=pltpu.PrefetchScalarGridSpec(
+            num_scalar_prefetch=1, grid=(tiles + last,),
+            in_specs=[whole(dr.shape), whole(acc.shape), pl.BlockSpec((width, width), lambda i, *_: (at(i), 0)),
+                      pl.BlockSpec((length, width), lambda i, *_: (0, at(i))), pl.BlockSpec((width, width), lambda i, *_: (0, at(i)))]
+            + [pl.BlockSpec(memory_space=pl.ANY) if n in (7, 8, 10, 11) else whole(x.shape) for n, x in enumerate(args) if n >= 5]
+            + [pl.BlockSpec(memory_space=pl.ANY)] * len(filled),
+            out_specs=out_specs,
+            scratch_shapes=scratch,
+        ),
+        input_output_aliases={1 + len(args) + n: n for n in range(len(filled))},
         cost_estimate=pl.CostEstimate(flops=12_000_000_000, bytes_accessed=8 << 20, transcendentals=0),
         name="back",
-    )(*args, *filled)
+    )(info, *args, *filled)
 
 
 def diagonals(x):
@@ -423,8 +498,9 @@
 
 
 def heads_kernel(*refs):
-    (p_ref, q_ref, k_ref, v_ref, do_ref, o_ref, oh_ref, oht_ref, et_ref, wq_ref, wk_ref, wv_ref, in_ref) = refs[:13]
-    (gk_ref, gs_ref, qb_ref, diag_ref, acc_ref, va_ref, rhs_ref, dsc_ref, dp_ref, w_ref, d_ref) = refs[-11:]
+    (p_ref, q_ref, k_ref, v_ref, do_ref, o_ref, oh_ref, oht_ref, et_any, wq_ref, wk_ref, wv_ref, in_any) = refs[:13]
+    (gk_ref, gs_ref, qb_ref, diag_ref, acc_ref, va_ref, rhs_ref, dsc_ref, dp_ref, w_ref, d_ref, et_ref, sems) = refs[-13:]
+    arriving = moves([(et_any, et_ref), (in_any, acc_ref)], sems)
     g = pl.program_id(0)
     length = q_ref.shape[0]
     lane = lax.broadcasted_iota(jnp.int32, (length, 128), 1)
@@ -433,7 +509,7 @@
     def _():
         va_ref[:, 128:256] = jnp.where(lane < 2, 1.0, 0.0).astype(BF)
         rhs_ref[:, 128:256] = oh_ref[...]
-        acc_ref[...] = in_ref[...]
+        start(arriving)
 
     va_ref[:, 0:128] = v_ref[...]
     rhs_ref[:, 0:128] = k_ref[...]
@@ -483,6 +559,11 @@
     dq = (jnp.where(first, res[0][0], res[1][0]) * SCALE).astype(BF)
     dk = jnp.where(first, res[0][1], res[1][1]).astype(BF)
     dv = jnp.where(first, res[0][2], res[1][2]).astype(BF)
+
+    @pl.when(g == 0)
+    def _():
+        wait(arriving)
+
     d_ref[:, 0:128] = dq
     d_ref[:, 128:256] = dk
     d_ref[:, 256:384] = dv
@@ -511,12 +592,13 @@
         out_shape=(sds((width // 2, 3 * width), BF), sds((width // 2, 3 * width), BF), sds((8, width), F32), sds((heads, 8, 256), F32), sds((length, width), F32)),
         grid=(steps,),
         in_specs=[pl.BlockSpec((2, length, length), lambda g: (g + base, 0, 0)), col, col, col, col, col, whole(oh.shape), whole(oht.shape),
-                  whole(et.shape), wcol, wcol, wcol, whole(acc.shape)] + [pl.BlockSpec(memory_space=pl.ANY)] * len(filled),
+                  pl.BlockSpec(memory_space=pl.ANY), wcol, wcol, wcol] + [pl.BlockSpec(memory_space=pl.ANY)] * (1 + len(filled)),
         out_specs=[pl.BlockSpec((width // 2, 384), lambda g: (0, g + base)), pl.BlockSpec((width // 2, 384), lambda g: (0, g + base)),
                    pl.BlockSpec((8, 128), lambda g: (0, g + base)), pl.BlockSpec((2, 8, 256), lambda g: (g + base, 0, 0)), whole_out((length, width))],
         input_output_aliases={13 + n: n for n in range(len(filled))},
         scratch_shapes=[pltpu.VMEM((length, 256), BF), pltpu.VMEM((length, 256), BF), pltpu.VMEM((2, length, length), BF),
-                        pltpu.VMEM((2, length, length), F32), pltpu.VMEM((width, 384), BF), pltpu.VMEM((length, 384), BF)],
+                        pltpu.VMEM((2, length, length), F32), pltpu.VMEM((width, 384), BF), pltpu.VMEM((length, 384), BF),
+                        pltpu.VMEM((width, length), BF), pltpu.SemaphoreType.DMA((2,))],
         cost_estimate=pl.CostEstimate(flops=20_000_000_000, bytes_accessed=8 << 20, transcendentals=0),
         name="heads_back",
     )(probs, q, k, v, do, o, oh, oht, et, wq, wk, wv, acc, *filled)
@@ -627,23 +709,63 @@
     return (source[:, None] == r[None]).astype(BF)
 
 
-def restack_kernel(info_ref, *refs):
-    out_ref = refs[-1]
-    n = len(refs) - 1
-    for d, part in enumerate(refs[:-1]):
-        out_ref[lax.rem(info_ref[0] - d + n, n)] = part[...].astype(out_ref.dtype)
-
-
-def restack(info, parts, dtype):
+def restack_kernel(info_ref, *refs, n, layout):
+    parts, outs = refs[:n], refs[n:]
+    for d, part in enumerate(parts):
+        source = lax.rem(info_ref[0] - d + n, n)
+        for out, pieces in zip(outs, layout):
+            at = 0
+            for start, width in pieces:
+                out[source, :, at : at + width] = part[:, start : start + width].astype(out.dtype)
+                at += width
+
+
+def restack(info, parts, dtype, layout=None):
     n = len(parts)
     rows, cols = parts[0].shape
-    return pl.pallas_call(
-        restack_kernel, out_shape=jax.ShapeDtypeStruct((n, rows, cols), dtype),
+    layout = layout or [[(0, cols)]]
+    outs = pl.pallas_call(
+        functools.partial(restack_kernel, n=n, layout=layout),
+        out_shape=[jax.ShapeDtypeStruct((n, rows, sum(w for _, w in pieces)), dtype) for pieces in layout],
         in_specs=[pl.BlockSpec(memory_space=pltpu.SMEM)] + [pl.BlockSpec(memory_space=pltpu.VMEM)] * n,
-        out_specs=pl.BlockSpec(memory_space=pltpu.VMEM),
+        out_specs=[pl.BlockSpec(memory_space=pltpu.VMEM)] * len(layout),
         cost_estimate=pl.CostEstimate(flops=1000, bytes_accessed=1000, transcendentals=0),
         name="restack",
     )(info, *parts)
+    return outs
+
+
+def unpack_kernel(small_ref, *outs, heads, tiles):
+    gct, gcp, qb, vb, ob, order, horiz, vert, ng, ns, be, rb, fg, fs = outs
+    for row, out in ((0, fg), (1, fs), (2, rb), (3, ng), (4, ns), (5, ob), (6, qb), (7, vb)):
+        out[...] = small_ref[row, :]
+    width = small_ref.shape[1]
+    for t in range(tiles):
+        be[t * width : (t + 1) * width] = small_ref[8 + t, :]
+    taps, cells, bias = 8 + tiles, 15 + tiles, 24 + tiles
+    for s in range(3):
+        for t in range(3):
+            gct[s, t, :] = small_ref[taps + 3 + (t - 1) * (s + 1), :]
+            gcp[s, t, :] = small_ref[cells + 3 * s + t, :]
+    nb = order.shape[1]
+    per = width // 128
+    for h in range(heads):
+        row, at = bias + h // per, 128 * (h % per)
+        for n, out in enumerate((order, horiz, vert)):
+            out[h, :] = small_ref[row, at + n * nb : at + (n + 1) * nb]
+
+
+def unpack(small, heads, nb, ff):
+    width = small.shape[1]
+    sds = lambda *shape: jax.ShapeDtypeStruct(shape, F32)
+    vec = sds(width)
+    return pl.pallas_call(
+        functools.partial(unpack_kernel, heads=heads, tiles=ff // width),
+        out_shape=(sds(3, 3, width), sds(3, 3, width), vec, vec, vec, sds(heads, nb), sds(heads, nb), sds(heads, nb),
+                   vec, vec, sds(ff), vec, vec, vec),
+        cost_estimate=pl.CostEstimate(flops=1000, bytes_accessed=1000, transcendentals=0),
+        name="unpack",
+    )(small)
 
 
 def one_hot_rows(ids, size):
@@ -707,10 +829,6 @@
     return jnp.stack(rows)
 
 
-def text_tap_grads(rows):
-    return jnp.stack([jnp.stack([rows[3 - s], rows[3], rows[3 + s]]) for s in (1, 2, 3)])
-
-
 def xor_pairs(n, bit):
     return [(i, i ^ bit) for i in range(n)]
 
@@ -741,80 +859,87 @@
 
 
 class Reduction:
-    def __init__(self, keep, send):
+    def __init__(self, keep, send, line=False):
+        self.line = line and lax.axis_size("seq") == 4
         n = lax.axis_size("pages")
-        self.bits = [1 << b for b in range(n.bit_length() - 1)][:0:-1]
-        self.shape = [2] * len(self.bits) + [keep.shape[0] * 2 // n]
-        cols = keep.shape[1]
-        self.cols = cols // 2
-        self.orders = (self.bits[::-1], list(self.bits))
-        self.at = 0
-        self.send = send
-        self.terms = [(tuple(self.bits), keep.reshape(self.shape + [cols]))]
-        self.own = ([], [])
-        self.fresh = []
-
-    def pick(self, term, side, closed, sent=None):
-        bits, value = term
-        starts = [0] * value.ndim
-        sizes = list(value.shape)
-        for axis, bit in enumerate(bits):
-            if bit in closed:
-                mine = jnp.minimum(lax.axis_index("pages") & bit, 1)
-                starts[axis] = 1 - mine if bit == sent else mine
-                sizes[axis] = 1
-        if value.shape[-1] > self.cols:
-            starts[-1] = side * self.cols
-            sizes[-1] = self.cols
-        out = lax.dynamic_slice(value, starts, sizes)
-        return out.reshape([n for axis, n in enumerate(sizes) if axis >= len(bits) or bits[axis] not in closed])
-
-    def parts(self, side, closed, sent=None):
-        return total([self.pick(t, side, closed, sent) for t in self.terms + self.own[side]])
+        self.n = n
+        self.page = lax.axis_index("pages")
+        self.first = (self.page & 1) == 0
+        self.bits = [1 << b for b in range(1, n.bit_length() - 1)]
+        self.shape = (n // 2, keep.shape[0] * 2 // n, keep.shape[1])
+        self.terms = [keep.reshape(self.shape)]
+        self.send, self.at, self.name = send, 0, None
+
+    def blocks(self, depth, other):
+        up, down = self.bits[:depth], self.bits[::-1][:depth]
+        out = []
+        for k in range((self.n // 2) >> depth):
+            pair = []
+            for closed in (up, down):
+                free = [b for b in self.bits if b not in closed]
+                index = sum((((k >> i) & 1) * b) for i, b in enumerate(free))
+                mine = sum(closed)
+                flip = closed[-1] if other and closed else 0
+                pair.append((index + ((self.page ^ flip) & mine)) // 2)
+            out.append(jnp.where(self.first, *pair))
+        return out
+
+    def pick(self, depth, other):
+        rows = []
+        for k, block in enumerate(self.blocks(depth, other)):
+            parts = []
+            for t, term in enumerate(self.terms):
+                have = max(t - 1, 0)
+                if have == 0:
+                    place = block
+                else:
+                    known = self.blocks(have, False)
+                    place = sum(jnp.where(known[i] == block, i, 0) for i in range(len(known)))
+                parts.append(lax.dynamic_index_in_dim(term, place, 0, keepdims=False))
+            rows.append(total(parts))
+        return jnp.stack(rows) if len(rows) > 1 else rows[0][None]
 
     def step(self):
+        assert not self.over()
         at, last = self.at, len(self.bits)
         self.at += 1
         n = lax.axis_size("seq")
         ring = lambda d: [(i, (i + d) % n) for i in range(n)]
         place = lax.axis_index("seq")
         if at == 0:
-            got = swap(self.send, "pages", 1)
-            self.fresh = [got]
+            self.fresh = [swap(self.send, "pages", 1)]
         elif at <= last:
-            self.settle()
-            self.fresh = []
-            for side in range(2):
-                closed = self.orders[side][:at]
-                send = self.parts(side, closed, closed[-1])
-                self.fresh.append(swap(send, "pages", closed[-1]))
+            self.terms.append(self.fresh[0].reshape((-1,) + self.shape[1:]))
+            pairs = [(i, i ^ (self.bits[-at] if i & 1 else self.bits[at - 1])) for i in range(self.n)]
+            self.fresh = [lax.ppermute(self.pick(at, True), "pages", pairs)]
         elif at == last + 1:
-            self.settle()
-            value = jnp.concatenate([self.parts(side, self.bits) for side in range(2)], 1)
+            self.terms.append(self.fresh[0].reshape((-1,) + self.shape[1:]))
+            value = self.pick(last, False)[0]
             rows, cols = value.shape
+            if self.line:
+                self.own = value
+                self.fresh = [lax.ppermute(value, "seq", [(0, 1), (3, 2)])]
+                return
             quarters = value.reshape(n, rows // n, cols)
             piece = lambda d: lax.dynamic_index_in_dim(quarters, lax.rem(place + d, n), 0, keepdims=False)
-            self.own = [(), piece(0)]
+            self.own = piece(0)
             self.fresh = [lax.ppermute(piece(d), "seq", ring(d)) for d in range(1, n)]
         else:
-            self.own = total([self.own[1]] + self.fresh)
+            self.own = total([self.own] + self.fresh)
+            if self.line:
+                self.fresh = [lax.ppermute(self.own, "seq", [(1, 2), (2, 1)] if at == last + 2 else [(1, 0), (2, 3)])]
+                return
             self.fresh = [lax.ppermute(self.own, "seq", ring(d)) for d in range(1, n)]
 
-    def settle(self):
-        at, last = self.at - 1, len(self.bits)
-        if at == 1:
-            self.terms.append((tuple(self.bits), self.fresh[0].reshape(self.terms[0][1].shape)))
-        elif at > 1:
-            for side in range(2):
-                closed = self.orders[side][: at - 1]
-                self.own[side].append((tuple(b for b in self.bits if b not in closed), self.fresh[side]))
-
     def over(self):
-        return self.at == len(self.bits) + 3
-
-    def result(self, info):
-        out = restack(info, [self.own] + self.fresh, F32)
-        return out.reshape(-1, out.shape[-1])
+        return self.at == len(self.bits) + (4 if self.line else 3)
+
+    def result(self, info, layout=None):
+        if self.line:
+            place = lax.axis_index("seq")
+            return [jnp.where((place == 0) | (place == 3), self.fresh[0], self.own).astype(F32)]
+        outs = restack(info, [self.own] + self.fresh, F32, layout)
+        return [out.reshape(-1, out.shape[-1]) for out in outs]
 
 
 def tie(value, *reductions):
@@ -842,87 +967,93 @@
     blocks = spread(rotated(tokens))
     core = lax.axis_index("pages") & 1
     info = jnp.stack([place, count, core]).astype(jnp.int32)
-    turn = turn_matrix(width, n_pages, core)
+    turn = turn_matrix(width, n_pages, core) if width // n_pages % 16 else jnp.zeros((8, 128), BF)
     cells = jnp.arange(BOX, dtype=jnp.int32)
     oh = jnp.concatenate([left[:, None] == cells[None], top[:, None] == cells[None]], 1).astype(BF)
     oht = jnp.concatenate([left[None] == cells[::-1, None], top[None] == cells[::-1, None]], 0).astype(BF)
     wt, od, edge = tables(rel_order, rel_horiz, rel_vert)
     pm, ct = patch_masks(), text_taps(conv_text)
     cp = jnp.pad(conv_patch.reshape(9, width), ((0, 7), (0, 0)))
-    row = lambda x: x[None]
 
     cot_out, blocks = lax.optimization_barrier((rotated(cotangent), blocks))
     cots = spread(cot_out)
     settled, et, q, k, v, probs, att = front(
-        info, edge, blocks, ct, cp, pm, turn, proj_query, row(bias_query), proj_key, proj_value, row(bias_value), oh, wt, od)
+        info, edge, blocks, ct, cp, pm, turn, proj_query, bias_query, proj_key, proj_value, bias_value, oh, wt, od, width // n_pages)
     *mixed, xh, rs, fl, gp, ds, dr, grk, grs, sm = middle(
-        info, cots, att, settled, proj_output, row(bias_output), row(norm_gain), row(norm_shift), expand_weight,
-        row(expand_bias), reduce_weight, row(reduce_bias), row(final_gain), row(final_shift), turn, ff // n_pages)
+        info, cots, att, settled, proj_output, bias_output, norm_gain, norm_shift, expand_weight,
+        expand_bias, reduce_weight, reduce_bias, final_gain, final_shift, turn, ff // n_pages)
     c_reduce = Reduction(grk, grs)
     c_reduce.step()
     mixed = spread(mixed)
-    done = back(0, 2, dr, ds, reduce_weight, gp, expand_weight, fl, turn)
+    done = back(info, width // n_pages, 0, 2, dr, ds, reduce_weight, gp, expand_weight, fl, turn)
     done = tie(done, c_reduce)
     c_reduce.step()
-    done = back(2, ff // width - 2, dr, done[3], reduce_weight, gp, expand_weight, fl, turn, done[:3],
-                (xh, rs, row(norm_gain), att, proj_output))
+    done = back(info, width // n_pages, 2, ff // width - 2, dr, done[3], reduce_weight, gp, expand_weight, fl, turn, done[:3],
+                (xh, rs, norm_gain, att, proj_output))
     done, mixed = tie((done, mixed), c_reduce)
     gek, ges, be, df, da, sm2 = done
     c_expand = Reduction(gek, ges)
     heads_of = lambda first, count, da, acc, filled=(): heads_back(
         first, count, probs, q, k, v, da, att, oh, oht, et, proj_query, proj_key, proj_value, acc, filled)
-    half = heads // 2
+    cuts = (0, heads // 2, heads)
     c_reduce.step()
     c_expand.step()
-    done = heads_of(0, half, da, df)
+    done = heads_of(0, cuts[1], da, df)
     done, da = tie((done, da), c_reduce, c_expand)
-    c_reduce.step()
-    c_expand.step()
-    done = heads_of(half, half, da, done[4], done[:4])
-    gqk, gqs, qb, diag, acc = tie(done, c_reduce, c_expand)
+    for first, last in zip(cuts[1:-1], cuts[2:]):
+        c_reduce.step()
+        c_expand.step()
+        done = heads_of(first, last - first, da, done[4], done[:4])
+        done, da = tie((done, da), c_reduce, c_expand)
+    gqk, gqs, qb, diag, acc = done
     c_qkv = Reduction(gqk, gqs)
-    c_reduce.step()
-    c_expand.step()
-    c_qkv.step()
+    for r in (c_reduce, c_expand, c_qkv):
+        if not r.over():
+            r.step()
     *gts, small = encode_back(info, blocks, acc, ct, cp, pm, sm, sm2, be, qb)
     rounds = [("pages", 1 << b) for b in range(n_pages.bit_length() - 1)] + [("seq", 1 << b) for b in range(n_seq.bit_length() - 1)]
     hop = lambda d: lax.ppermute(gts[d], "seq", [(i, (i + d) % n_seq) for i in range(n_seq)])
     work = [c_reduce, c_expand, c_qkv]
+    for r, name in zip(work, ("reduce", "expand", "qkv")):
+        r.name = name
     bias = jnp.concatenate(bias_grads(diag, nb), 1)
     bias = jnp.pad(bias, ((0, 0), (0, 128 - 3 * nb))).reshape(-1, width)
+    hops = {0: (1,), 1: (3,), 2: (2,)}
+    turns = [rounds[1:2], rounds[2:3], rounds[:1] + rounds[3:4], rounds[4:]] if len(rounds) == 5 else [rounds]
+    layouts = {
+        "reduce": None,
+        "expand": [[(0, ff)], [(ff, width)]],
+        "qkv": [[(384 * p + 128 * n, 128) for p in range(heads // 2)] for n in range(3)],
+    }
+    ready = {}
     phase = 0
-    while rounds or not c_qkv.over():
-        gts, small, bias = tie((gts, small, bias), *work)
+    while turns or not c_qkv.over():
+        gts, small, bias, ready = tie((gts, small, bias, ready), *work)
         if phase == 0:
             small = lax.dynamic_update_slice(small, bias, (24 + ff // width, 0))
+            ready["mixed"] = restack(info, mixed, BF)
         for r in work:
             if not r.over():
                 r.step()
-        for d in {1: (1,), 2: (3,), 3: (2,)}.get(phase, ()):
+            elif r.own is not None and r is not c_qkv:
+                ready[r.name] = r.result(info, layouts[r.name])
+                r.own, r.fresh = None, []
+        for d in hops.get(phase, ()):
             gts = [hop(d) if e == d else part for e, part in enumerate(gts)]
-        for axis, bit in rounds[: 1 if phase < 3 else 2]:
+        for axis, bit in turns.pop(0) if turns else ():
             small = small + swap(small, axis, bit)
-        rounds = rounds[1 if phase < 3 else 2 :]
         phase += 1
-    o_reduce, o_expand, o_qkv = (r.result(info) for r in work)
-    mixed_out = restack(info, mixed, BF)
-    grad_tokens = restack(info, gts, F32)
-    g3 = o_qkv.reshape(width // n_pages, heads // 2, 3, 128)
-    o_query, o_key, o_value = (g3[:, :, n].reshape(width // n_pages, width) for n in range(3))
-    bias = small[24 + ff // width : 24 + ff // width + heads * 128 // width].reshape(heads, 128)
-
-    at = 0
-
-    def take(n):
-        nonlocal at
-        at += n
-        return small[at - n : at]
-
-    sm, sm2, qb, be, gct, gcp = take(3), take(3), take(2), take(ff // width), take(7), take(9)
+    (mixed_out,) = ready["mixed"]
+    (o_reduce,), (o_expand, o_output) = (
+        ready[r.name] if r.name in ready else r.result(info, layouts[r.name]) for r in (c_reduce, c_expand))
+    o_query, o_key, o_value = c_qkv.result(info, layouts["qkv"])
+    (grad_tokens,) = restack(info, gts, F32)
+
+    (g_conv_text, g_conv_patch, g_qb, g_vb, g_ob, g_order, g_horiz, g_vert, g_ng, g_ns, g_be, g_rb, g_fg, g_fs) = unpack(
+        small, heads, nb, ff)
     return (
-        mixed_out, grad_tokens, text_tap_grads(gct), gcp.reshape(3, 3, width), o_query, qb[0], o_key, o_value, qb[1],
-        o_expand[:, ff:], sm2[2], bias[:, :nb], bias[:, nb : 2 * nb], bias[:, 2 * nb : 3 * nb], sm2[0], sm2[1],
-        o_expand[:, :ff], be.reshape(ff), o_reduce, sm[2], sm[0], sm[1],
+        mixed_out, grad_tokens, g_conv_text, g_conv_patch, o_query, g_qb, o_key, o_value, g_vb,
+        o_output, g_ob, g_order, g_horiz, g_vert, g_ng, g_ns, o_expand, g_be, o_reduce, g_rb, g_fg, g_fs,
     )
 
 

time: 329 us -> 297 us (0.903)
  local copies, waits for them, and re-layouts: 32.7 us -> 17.3 us
  Pallas kernels: 144 us -> 135 us
  other arithmetic: 35.1 us -> 27.1 us
  waiting for transfers between devices: 37.2 us -> 40.5 us
    ppermute x20 -> x8, waiting for transfers between devices: 4.98 us -> 20.1 us  [swap(): return lax.ppermute(value, axis, xor_pairs(lax.axis_size(axis), bit))]
    ppermute x20 -> x8, starting transfers between devices: 19.5 us -> 4.43 us  [swap(): return lax.ppermute(value, axis, xor_pairs(lax.axis_size(axis), bit))]
    convert_element_type x15 -> x9, other arithmetic: 23.2 us -> 12.8 us  [total(): return out.astype(BF)]
    ppermute x0 -> x6, starting transfers between devices: none -> 8.04 us  [step(): self.fresh = [lax.ppermute(self.pick(at, True), 'pages', pairs)]]
    ppermute x9, waiting for transfers between devices: 14.6 us -> 7.25 us  [step(): self.fresh = [lax.ppermute(piece(d), 'seq', ring(d)) for d in range(1, n)]]
    another operation x3 -> x7, other arithmetic: 0.85 us -> 8.04 us  [the longest x2 0.64 us: text_tap_grads(): jnp.stack([jnp.stack([rows[3 - s], rows[3], rows[3 + s]]) for s in (1, 2,...]
    ppermute x9, waiting for transfers between devices: 17.7 us -> 10.8 us  [step(): self.fresh = [lax.ppermute(self.own, 'seq', ring(d)) for d in range(1, n)]]
    slice x8 -> x0, local copies, waits for them, and re-layouts: 5.53 us -> none  [the longest x1 2.32 us: per_device(): g3[:, :, n].reshape(width // n_pages, width)]
  transfers between devices with their start and end apart: 50 -> 44, of which waited for: 9 -> 9; matrix products, arithmetic and copies ran while one was open for 17% -> 11% of each run, Pallas kernels for 34% -> 35%
where the time goes in v3:
time: 297 us; the launch traced here: 292 us
  Pallas kernels  135 us (45%)
  starting transfers between devices  67.5 us (23%)
  waiting for transfers between devices  40.5 us (14%)
  other arithmetic  27.1 us (9%)
  local copies, waits for them, and re-layouts  17.3 us (6%)
  matrix products  3.13 us (1%)
    pallas_call x2, Pallas kernels, heads_back(): pl.pallas_call(heads_kernel, out_shape=(sds((width // 2, 3 * width), BF),...  35.3 us
    pallas_call x1, Pallas kernels, middle(): pl.pallas_call(functools.partial(middle_kernel, n_seq=n_seq, tiles=tiles,...  29.2 us
    pallas_call x2, Pallas kernels, back(): pl.pallas_call(functools.partial(back_kernel, tiles=tiles, last=last, blo...  26.4 us
    pallas_call x1, Pallas kernels, front(): pl.pallas_call(functools.partial(front_kernel, n_seq=n_seq, block=block),...  22.7 us
    ppermute x8, waiting for transfers between devices, swap(): return lax.ppermute(value, axis, xor_pairs(lax.axis_size(axis), bit))  20.1 us
    ppermute x9, starting transfers between devices, spread(): lax.ppermute(blocks[d], 'seq', [(i, (i + d) % n) for i in range(n)])  17.5 us
    ppermute x9, starting transfers between devices, step(): self.fresh = [lax.ppermute(piece(d), 'seq', ring(d)) for d in range(1, n)]  16 us
    ppermute x9, starting transfers between devices, step(): self.fresh = [lax.ppermute(self.own, 'seq', ring(d)) for d in range(1, n)]  13.6 us
  transfers between devices with their start and end apart: 44, of which 9 were waited for; matrix products, arithmetic and copies ran while one was open for 11% of the time, Pallas kernels for 35%

profile of v3, /device:TPU:0, one launch (start us, length us, event | category | flops | bytes accessed | tf_op | source)
XLA Modules:
  0.0 292.1 jit_solution(17455614198723153850)
XLA Ops:
  0.8 2.1 dynamic-slice_bitcast_fusion
  2.8 3.0 %collective-permute-start = (bf16[144,768]{1,0:T(8,128)(2,1)S(1)}, bf16[144,768]{1,0:T(8,128)(2,1)S(1)}, u32[]{:S(2)}, u32[]{:S(2)}) collective-permute-start(bf16[144,768]{1,0:T(8,128)(2,1)S(1)} %get-tuple-element.329), channel_id=1, source_target_pairs={{0,1},{1,2},{2,3},{3,0},{4,5},{5,6},{6,7},{7,4},{8,9},{9,10},{10,1... | collective-permute-start | bytes 663560 | tf_op jit(solution)/shard_map/ppermute | solution.py:844
  5.9 2.6 collective-permute-start.1
  24.1 4.1 %collective-permute-start.3 = (bf16[144,768]{1,0:T(8,128)(2,1)S(1)}, bf16[144,768]{1,0:T(8,128)(2,1)S(1)}, u32[]{:S(2)}, u32[]{:S(2)}) collective-permute-start(bf16[144,768]{1,0:T(8,128)(2,1)S(1)} %get-tuple-element.181), channel_id=1, source_target_pairs={{0,1},{1,2},{2,3},{3,0},{4,5},{5,6},{6,7},{7,4},{8,9},{9,10},{10,1... | collective-permute-start | bytes 663560 | tf_op jit(solution)/shard_map/ppermute | solution.py:844
  31.4 22.7 %front.1 = (f32[576,768]{1,0:T(8,128)}, bf16[768,576]{1,0:T(8,128)(2,1)}, bf16[576,768]{1,0:T(8,128)(2,1)}, bf16[576,768]{1,0:T(8,128)(2,1)}, bf16[576,768]{1,0:...) custom-call(s32[3]{0:T(128)} %pad_add_fusion.1.info_ref, f32[12,2]{1,0:T(8,128)} %copy.57.edge_ref, ...), custom_call_target="tpu_custom_call" | custom-call | flops 24999999488 | bytes 8388608 | tf_op jit(solution)/shard_map/front/pallas_call | solution.py:220
  54.9 29.2 %middle.1 = (bf16[144,768]{1,0:T(8,128)(2,1)}, bf16[144,768]{1,0:T(8,128)(2,1)}, bf16[144,768]{1,0:T(8,128)(2,1)}, bf16[144,768]{1,0:T(8,128)(2,1)}, f32[576,768...) custom-call(s32[3]{0:T(128)} %pad_add_fusion.1.info_ref, ...), custom_call_target="tpu_custom_call" | custom-call | flops 35000000512 | bytes 8388608 | tf_op jit(solution)/shard_map/middle/pallas_call | solution.py:371
  84.2 11.4 %back.2 = (bf16[384,3840]{1,0:T(8,128)(2,1)}, bf16[384,3840]{1,0:T(8,128)(2,1)}, f32[1,3072]{1,0:T(1,128)}, f32[576,768]{1,0:T(8,128)}) custom-call(s32[3]{0:T(128)} %pad_add_fusion.1.info_ref, bf16[576,768]{1,0:T(8,128)(2,1)} %get-tuple-element.186.refs_0_, f32[576,768]{1,0:T(8,128)} %get-tuple-element.187.refs_1_, bf16[3072,768]{1,0:T(8,128)(2,1)} %refs_2_.3, ...), custom_call_target="tpu_custom_call" | custom-call | flops 12000000000 | bytes 8388608 | tf_op jit(solution)/shard_map/back/pallas_call | solution.py:472
  102.8 14.9 %back.3 = (bf16[384,3840]{1,0:T(8,128)(2,1)}, bf16[384,3840]{1,0:T(8,128)(2,1)}, f32[1,3072]{1,0:T(1,128)}, f32[576,768]{1,0:T(8,128)}, bf16[576,768]{1,0:T(8,128)(2,1)}, /*index=5*/f32[8,768]{1,0:T(8,128)}) custom-call(s32[3]{0:T(128)} %pad_add_fusion.1.info_ref, ...), custom_call_target="tpu_custom_call", output_to_operand_aliasing={{0}: (13, {}), {1}: (14, {}), {2}: (15, {})} | custom-call | flops 12000000000 | bytes 8388608 | tf_op jit(solution)/shard_map/back/pallas_call | solution.py:472
  120.3 2.5 add_convert_fusion.5
  124.1 17.5 %heads_back.2 = (bf16[384,2304]{1,0:T(8,128)(2,1)}, bf16[384,2304]{1,0:T(8,128)(2,1)}, f32[8,768]{1,0:T(8,128)}, f32[12,8,256]{2,1,0:T(8,128)}, f32[576,768]{1,0:T(8,128)}) custom-call(bf16[12,576,576]{2,1,0:T(8,128)(2,1)} %get-tuple-element.176.refs_0_, bf16[576,768]{1,0:T(8,128)(2,1)} %get-tuple-element.177.refs_1_, ...), custom_call_target="tpu_custom_call" | custom-call | flops 20000000000 | bytes 8388608 | tf_op jit(solution)/shard_map/heads_back/pallas_call | solution.py:590
  142.4 2.0 add_convert_fusion.4
  145.2 4.1 %collective-permute-start.13 = (bf16[96,768]{1,0:T(8,128)(2,1)}, bf16[96,768]{1,0:T(8,128)(2,1)}, u32[]{:S(2)}, u32[]{:S(2)}) collective-permute-start(bf16[96,768]{1,0:T(8,128)(2,1)} %get-tuple-element.341), channel_id=1, source_target_pairs={{0,1},{1,2},{2,3},{3,0},{4,5},{5,6},{6,7},{7,4},{8,9},{9,10},{10,1... | collective-permute-start | bytes 442376 | tf_op jit(solution)/shard_map/ppermute | solution.py:926
  149.6 2.1 collective-permute-start.15
  154.9 17.8 %heads_back.3 = (bf16[384,2304]{1,0:T(8,128)(2,1)}, bf16[384,2304]{1,0:T(8,128)(2,1)}, f32[8,768]{1,0:T(8,128)}, f32[12,8,256]{2,1,0:T(8,128)}, f32[576,768]{1,0:T(8,128)}) custom-call(bf16[12,576,576]{2,1,0:T(8,128)(2,1)} %get-tuple-element.176.refs_0_, ...), custom_call_target="tpu_custom_call", output_to_operand_aliasing={{0}: (13, {}), {1}: (14, {}), {2}: (15, {}), {3}: (16, {})} | custom-call | flops 20000000000 | bytes 8388608 | tf_op jit(solution)/shard_map/heads_back/pallas_call | solution.py:590
  174.9 2.6 collective-permute-start.18
  178.7 2.5 add_convert_fusion.1
  182.9 7.9 %encode_back.1 = (bf16[144,768]{1,0:T(8,128)(2,1)}, bf16[144,768]{1,0:T(8,128)(2,1)}, bf16[144,768]{1,0:T(8,128)(2,1)}, bf16[144,768]{1,0:T(8,128)(2,1)}, f32[32,768]{1,0:T(8,128)}) custom-call(s32[3]{0:T(128)} %pad_add_fusion.1.info_ref, bf16[144,768]{1,0:T(8,128)(2,1)} %get-tuple-element.172.refs_0_, bf16[144,768]{1,0:T(8,128)(2,1)} %copy-done.34, ...), custom_call_target="tpu_custom_call" | custom-call | flops 10000000000 | bytes 8388608 | tf_op jit(solution)/shard_map/encode_back/pallas_call | solution.py:688
  207.1 2.2 restack.5
  209.3 2.2 restack.6
  211.6 6.7 %collective-permute-done.25 = bf16[24,3840]{1,0:T(8,128)(2,1)S(1)} collective-permute-done((bf16[24,3840]{1,0:T(8,128)(2,1)S(1)}, bf16[24,3840]{1,0:T(8,128)(2,1)S(1)}, u32[]{:S(2)}, u32[]{:S(2)}) %collective-permute-start.25) | collective-permute-done | bytes 184352 | tf_op jit(solution)/shard_map/ppermute | solution.py:926
  218.3 4.5 %collective-permute-start.28 = (bf16[144,768]{1,0:T(8,128)(2,1)}, bf16[144,768]{1,0:T(8,128)(2,1)S(1)}, u32[]{:S(2)}, u32[]{:S(2)}) collective-permute-start(bf16[144,768]{1,0:T(8,128)(2,1)} %get-tuple-element.272), channel_id=1, source_target_pairs={{0,3},{1,0},{2,1},{3,2},{4,7},{5,4},{6,5},{7,6},{8,11},{9,8},{10,9... | collective-permute-start | bytes 663560 | tf_op jit(solution)/shard_map/ppermute | solution.py:1015
  228.9 2.8 collective-permute-start.32
  231.7 5.0 %collective-permute-done.30.refs_1_ = bf16[24,3840]{1,0:T(8,128)(2,1)S(1)} collective-permute-done((bf16[24,3840]{1,0:T(8,128)(2,1)S(1)}, bf16[24,3840]{1,0:T(8,128)(2,1)S(1)}, u32[]{:S(2)}, u32[]{:S(2)}) %collective-permute-start.30) | collective-permute-done | bytes 184352 | tf_op jit(solution)/shard_map/ppermute | solution.py:932
  236.8 5.7 %collective-permute-done.31.refs_2_ = bf16[24,3840]{1,0:T(8,128)(2,1)S(1)} collective-permute-done((bf16[24,3840]{1,0:T(8,128)(2,1)S(1)}, bf16[24,3840]{1,0:T(8,128)(2,1)S(1)}, u32[]{:S(2)}, u32[]{:S(2)}) %collective-permute-start.31) | collective-permute-done | bytes 184352 | tf_op jit(solution)/shard_map/ppermute | solution.py:932
  243.2 2.6 collective-permute-start.34
  247.3 2.8 collective-permute-start.37
  253.4 2.4 restack.7
  255.8 7.6 %collective-permute-done.36 = f32[32,768]{1,0:T(8,128)S(1)} collective-permute-done((f32[32,768]{1,0:T(8,128)S(1)}, f32[32,768]{1,0:T(8,128)S(1)}, u32[]{:S(2)}, u32[]{:S(2)}) %collective-permute-start.36) | collective-permute-done | bytes 98336 | tf_op jit(solution)/shard_map/ppermute | solution.py:837
  266.1 3.4 %collective-permute-start.42 = (bf16[24,2304]{1,0:T(8,128)(2,1)S(1)}, bf16[24,2304]{1,0:T(8,128)(2,1)S(1)}, u32[]{:S(2)}, u32[]{:S(2)}) collective-permute-start(bf16[24,2304]{1,0:T(8,128)(2,1)S(1)} %fusion.14.refs_0_), channel_id=1, source_target_pairs={{0,2},{1,3},{2,0},{3,1},{4,6},{5,7},{6,4},{7,5},{8,10},{9,11},{10,... | collective-permute-start | bytes 331784 | tf_op jit(solution)/shard_map/ppermute | solution.py:932
  271.0 12.5 %collective-permute-done.40 = f32[32,768]{1,0:T(8,128)S(1)} collective-permute-done((f32[32,768]{1,0:T(8,128)S(1)}, f32[32,768]{1,0:T(8,128)S(1)}, u32[]{:S(2)}, u32[]{:S(2)}) %collective-permute-start.40) | collective-permute-done | bytes 98336 | tf_op jit(solution)/shard_map/ppermute | solution.py:837
  284.1 2.6 restack.8
  289.7 2.0 restack.9
  (242 shorter events, 75.7 us)
Async XLA Ops:
  2.8 21.3 %collective-permute-start = (bf16[144,768]{1,0:T(8,128)(2,1)S(1)}, bf16[144,768]{1,0:T(8,128)(2,1)S(1)}, u32[]{:S(2)}, u32[]{:S(2)}) collective-permute-start(bf16[144,768]{1,0:T(8,128)(2,1)S(1)} %get-tuple-element.329), channel_id=1, source_target_pairs={{0,1},{1,2},{2,3},{3,0},{4,5},{5,6},{6,7},{7,4},{8,9},{9,10},{10,1... | collective-permute-start | bytes 663560 | tf_op jit(solution)/shard_map/ppermute | solution.py:844
  5.9 18.3 %collective-permute-start.1 = (bf16[144,768]{1,0:T(8,128)(2,1)S(1)}, bf16[144,768]{1,0:T(8,128)(2,1)S(1)}, u32[]{:S(2)}, u32[]{:S(2)}) collective-permute-start(bf16[144,768]{1,0:T(8,128)(2,1)S(1)} %get-tuple-element.331), channel_id=1, source_target_pairs={{0,2},{1,3},{2,0},{3,1},{4,6},{5,7},{6,4},{7,5},{8,10},{9,11},{10,... | collective-permute-start | bytes 663560 | tf_op jit(solution)/shard_map/ppermute | solution.py:844
  8.5 15.7 %collective-permute-start.2 = (bf16[144,768]{1,0:T(8,128)(2,1)S(1)}, bf16[144,768]{1,0:T(8,128)(2,1)}, u32[]{:S(2)}, u32[]{:S(2)}) collective-permute-start(bf16[144,768]{1,0:T(8,128)(2,1)S(1)} %get-tuple-element.328), channel_id=1, source_target_pairs={{0,3},{1,0},{2,1},{3,2},{4,7},{5,4},{6,5},{7,6},{8,11},{9,8},{10,9... | collective-permute-start | bytes 663560 | tf_op jit(solution)/shard_map/ppermute | solution.py:844
  24.1 29.9 %collective-permute-start.3 = (bf16[144,768]{1,0:T(8,128)(2,1)S(1)}, bf16[144,768]{1,0:T(8,128)(2,1)S(1)}, u32[]{:S(2)}, u32[]{:S(2)}) collective-permute-start(bf16[144,768]{1,0:T(8,128)(2,1)S(1)} %get-tuple-element.181), channel_id=1, source_target_pairs={{0,1},{1,2},{2,3},{3,0},{4,5},{5,6},{6,7},{7,4},{8,9},{9,10},{10,1... | collective-permute-start | bytes 663560 | tf_op jit(solution)/shard_map/ppermute | solution.py:844
  28.2 25.8 %collective-permute-start.4 = (bf16[144,768]{1,0:T(8,128)(2,1)S(1)}, bf16[144,768]{1,0:T(8,128)(2,1)S(1)}, u32[]{:S(2)}, u32[]{:S(2)}) collective-permute-start(bf16[144,768]{1,0:T(8,128)(2,1)S(1)} %get-tuple-element.182), channel_id=1, source_target_pairs={{0,2},{1,3},{2,0},{3,1},{4,6},{5,7},{6,4},{7,5},{8,10},{9,11},{10,... | collective-permute-start | bytes 663560 | tf_op jit(solution)/shard_map/ppermute | solution.py:844
  29.7 24.3 %collective-permute-start.5 = (bf16[144,768]{1,0:T(8,128)(2,1)S(1)}, bf16[144,768]{1,0:T(8,128)(2,1)S(1)}, u32[]{:S(2)}, u32[]{:S(2)}) collective-permute-start(bf16[144,768]{1,0:T(8,128)(2,1)S(1)} %get-tuple-element.183), channel_id=1, source_target_pairs={{0,3},{1,0},{2,1},{3,2},{4,7},{5,4},{6,5},{7,6},{8,11},{9,8},{10,9... | collective-permute-start | bytes 663560 | tf_op jit(solution)/shard_map/ppermute | solution.py:844
  97.4 20.7 %collective-permute-start.10 = (bf16[2,384,768]{2,1,0:T(8,128)(2,1)S(1)}, bf16[2,384,768]{2,1,0:T(8,128)(2,1)S(1)}, u32[]{:S(2)}, u32[]{:S(2)}) collective-permute-start(bf16[2,384,768]{2,1,0:T(8,128)(2,1)S(1)} %pad_maximum_fusion.1), channel_id=1, source_target_pairs={{0,8},{4,20},{8,0},{12,28},{16,24},{20,4},{24,16},{28,12},{1,9},{5... | collective-permute-start | bytes 3538952 | tf_op jit(solution)/shard_map/ppermute | solution.py:914
  98.9 18.8 %collective-permute-start.7 = (bf16[144,768]{1,0:T(8,128)(2,1)}, bf16[144,768]{1,0:T(8,128)(2,1)S(1)}, u32[]{:S(2)}, u32[]{:S(2)}) collective-permute-start(bf16[144,768]{1,0:T(8,128)(2,1)} %get-tuple-element.208), channel_id=1, source_target_pairs={{0,1},{1,2},{2,3},{3,0},{4,5},{5,6},{6,7},{7,4},{8,9},{9,10},{10,1... | collective-permute-start | bytes 663560 | tf_op jit(solution)/shard_map/ppermute | solution.py:844
  100.1 18.0 %collective-permute-start.8 = (bf16[144,768]{1,0:T(8,128)(2,1)S(1)}, bf16[144,768]{1,0:T(8,128)(2,1)S(1)}, u32[]{:S(2)}, u32[]{:S(2)}) collective-permute-start(bf16[144,768]{1,0:T(8,128)(2,1)S(1)} %copy-done.37), channel_id=1, source_target_pairs={{0,2},{1,3},{2,0},{3,1},{4,6},{5,7},{6,4},{7,5},{8,10},{9,11},{10,... | collective-permute-start | bytes 663560 | tf_op jit(solution)/shard_map/ppermute | solution.py:844
  101.5 16.6 %collective-permute-start.9 = (bf16[144,768]{1,0:T(8,128)(2,1)S(1)}, bf16[144,768]{1,0:T(8,128)(2,1)S(1)}, u32[]{:S(2)}, u32[]{:S(2)}) collective-permute-start(bf16[144,768]{1,0:T(8,128)(2,1)S(1)} %copy-done.36), channel_id=1, source_target_pairs={{0,3},{1,0},{2,1},{3,2},{4,7},{5,4},{6,5},{7,6},{8,11},{9,8},{10,9... | collective-permute-start | bytes 663560 | tf_op jit(solution)/shard_map/ppermute | solution.py:844
  119.2 22.4 %collective-permute-start.12 = (bf16[384,3840]{1,0:T(8,128)(2,1)}, bf16[384,3840]{1,0:T(8,128)(2,1)S(1)}, u32[]{:S(2)}, u32[]{:S(2)}) collective-permute-start(bf16[384,3840]{1,0:T(8,128)(2,1)} %get-tuple-element.222), channel_id=1, source_target_pairs={{0,4},{4,0},{8,12},{12,8},{16,20},{20,16},{24,28},{28,24},{1,5},{5... | collective-permute-start | bytes 8847368 | tf_op jit(solution)/shard_map/ppermute | solution.py:837
  122.8 18.8 %collective-permute-start.11 = (bf16[1,384,768]{2,1,0:T(8,128)(2,1)}, bf16[1,384,768]{2,1,0:T(8,128)(2,1)S(1)}, u32[]{:S(2)}, u32[]{:S(2)}) collective-permute-start(bf16[1,384,768]{2,1,0:T(8,128)(2,1)} %add_convert_fusion.5), channel_id=1, source_target_pairs={{0,16},{4,12},{8,24},{12,4},{16,0},{20,28},{24,8},{28,20},{1,17},{... | collective-permute-start | bytes 1769480 | tf_op jit(solution)/shard_map/ppermute | solution.py:914
  145.2 27.5 %collective-permute-start.13 = (bf16[96,768]{1,0:T(8,128)(2,1)}, bf16[96,768]{1,0:T(8,128)(2,1)}, u32[]{:S(2)}, u32[]{:S(2)}) collective-permute-start(bf16[96,768]{1,0:T(8,128)(2,1)} %get-tuple-element.341), channel_id=1, source_target_pairs={{0,1},{1,2},{2,3},{3,0},{4,5},{5,6},{6,7},{7,4},{8,9},{9,10},{10,1... | collective-permute-start | bytes 442376 | tf_op jit(solution)/shard_map/ppermute | solution.py:926
  149.3 23.4 %collective-permute-start.14 = (bf16[96,768]{1,0:T(8,128)(2,1)}, bf16[96,768]{1,0:T(8,128)(2,1)}, u32[]{:S(2)}, u32[]{:S(2)}) collective-permute-start(bf16[96,768]{1,0:T(8,128)(2,1)} %get-tuple-element.340), channel_id=1, source_target_pairs={{0,2},{1,3},{2,0},{3,1},{4,6},{5,7},{6,4},{7,5},{8,10},{9,11},{10,... | collective-permute-start | bytes 442376 | tf_op jit(solution)/shard_map/ppermute | solution.py:926
  149.6 23.2 %collective-permute-start.15 = (bf16[96,768]{1,0:T(8,128)(2,1)}, bf16[96,768]{1,0:T(8,128)(2,1)}, u32[]{:S(2)}, u32[]{:S(2)}) collective-permute-start(bf16[96,768]{1,0:T(8,128)(2,1)} %get-tuple-element.339), channel_id=1, source_target_pairs={{0,3},{1,0},{2,1},{3,2},{4,7},{5,4},{6,5},{7,6},{8,11},{9,8},{10,9... | collective-permute-start | bytes 442376 | tf_op jit(solution)/shard_map/ppermute | solution.py:926
  153.4 19.7 %collective-permute-start.16 = (bf16[2,96,3840]{2,1,0:T(8,128)(2,1)}, bf16[2,96,3840]{2,1,0:T(8,128)(2,1)}, u32[]{:S(2)}, u32[]{:S(2)}) collective-permute-start(bf16[2,96,3840]{2,1,0:T(8,128)(2,1)} %pad_maximum_fusion), channel_id=1, source_target_pairs={{0,8},{4,20},{8,0},{12,28},{16,24},{20,4},{24,16},{28,12},{1,9},{5... | collective-permute-start | bytes 4423688 | tf_op jit(solution)/shard_map/ppermute | solution.py:914
  174.9 16.5 %collective-permute-start.17 = (bf16[96,768]{1,0:T(8,128)(2,1)}, bf16[96,768]{1,0:T(8,128)(2,1)S(1)}, u32[]{:S(2)}, u32[]{:S(2)}) collective-permute-start(bf16[96,768]{1,0:T(8,128)(2,1)} %fusion.11.refs_0_), channel_id=1, source_target_pairs={{0,1},{1,2},{2,3},{3,0},{4,5},{5,6},{6,7},{7,4},{8,9},{9,10},{10,1... | collective-permute-start | bytes 442376 | tf_op jit(solution)/shard_map/ppermute | solution.py:932
  174.9 16.5 %collective-permute-start.18 = (bf16[96,768]{1,0:T(8,128)(2,1)}, bf16[96,768]{1,0:T(8,128)(2,1)S(1)}, u32[]{:S(2)}, u32[]{:S(2)}) collective-permute-start(bf16[96,768]{1,0:T(8,128)(2,1)} %fusion.11.refs_0_), channel_id=1, source_target_pairs={{0,2},{1,3},{2,0},{3,1},{4,6},{5,7},{6,4},{7,5},{8,10},{9,11},{10,... | collective-permute-start | bytes 442376 | tf_op jit(solution)/shard_map/ppermute | solution.py:932
  177.4 14.0 %collective-permute-start.19 = (bf16[96,768]{1,0:T(8,128)(2,1)}, bf16[96,768]{1,0:T(8,128)(2,1)S(1)}, u32[]{:S(2)}, u32[]{:S(2)}) collective-permute-start(bf16[96,768]{1,0:T(8,128)(2,1)} %fusion.11.refs_0_), channel_id=1, source_target_pairs={{0,3},{1,0},{2,1},{3,2},{4,7},{5,4},{6,5},{7,6},{8,11},{9,8},{10,9... | collective-permute-start | bytes 442376 | tf_op jit(solution)/shard_map/ppermute | solution.py:932
  193.2 25.2 %collective-permute-start.22 = (bf16[144,768]{1,0:T(8,128)(2,1)}, bf16[144,768]{1,0:T(8,128)(2,1)S(1)}, u32[]{:S(2)}, u32[]{:S(2)}) collective-permute-start(bf16[144,768]{1,0:T(8,128)(2,1)} %get-tuple-element.254), channel_id=1, source_target_pairs={{0,1},{1,2},{2,3},{3,0},{4,5},{5,6},{6,7},{7,4},{8,9},{9,10},{10,1... | collective-permute-start | bytes 663560 | tf_op jit(solution)/shard_map/ppermute | solution.py:1015
  198.6 19.7 %collective-permute-start.27 = (bf16[2,96,2304]{2,1,0:T(8,128)(2,1)}, bf16[2,96,2304]{2,1,0:T(8,128)(2,1)}, u32[]{:S(2)}, u32[]{:S(2)}) collective-permute-start(bf16[2,96,2304]{2,1,0:T(8,128)(2,1)} %pad_maximum_fusion.2), channel_id=1, source_target_pairs={{0,8},{4,20},{8,0},{12,28},{16,24},{20,4},{24,16},{28,12},{1,9},{5... | collective-permute-start | bytes 2654216 | tf_op jit(solution)/shard_map/ppermute | solution.py:914
  204.0 14.3 %collective-permute-start.25 = (bf16[24,3840]{1,0:T(8,128)(2,1)S(1)}, bf16[24,3840]{1,0:T(8,128)(2,1)S(1)}, u32[]{:S(2)}, u32[]{:S(2)}) collective-permute-start(bf16[24,3840]{1,0:T(8,128)(2,1)S(1)} %get-tuple-element.337), channel_id=1, source_target_pairs={{0,2},{1,3},{2,0},{3,1},{4,6},{5,7},{6,4},{7,5},{8,10},{9,11},{10,... | collective-permute-start | bytes 552968 | tf_op jit(solution)/shard_map/ppermute | solution.py:926
  218.3 24.2 %collective-permute-start.28 = (bf16[144,768]{1,0:T(8,128)(2,1)}, bf16[144,768]{1,0:T(8,128)(2,1)S(1)}, u32[]{:S(2)}, u32[]{:S(2)}) collective-permute-start(bf16[144,768]{1,0:T(8,128)(2,1)} %get-tuple-element.272), channel_id=1, source_target_pairs={{0,3},{1,0},{2,1},{3,2},{4,7},{5,4},{6,5},{7,6},{8,11},{9,8},{10,9... | collective-permute-start | bytes 663560 | tf_op jit(solution)/shard_map/ppermute | solution.py:1015
  224.7 18.5 %collective-permute-start.33 = (bf16[1,96,2304]{2,1,0:T(8,128)(2,1)S(1)}, bf16[1,96,2304]{2,1,0:T(8,128)(2,1)S(1)}, u32[]{:S(2)}, u32[]{:S(2)}) collective-permute-start(bf16[1,96,2304]{2,1,0:T(8,128)(2,1)S(1)} %add_convert_fusion.9), channel_id=1, source_target_pairs={{0,16},{4,12},{8,24},{12,4},{16,0},{20,28},{24,8},{28,20},{1,17},{... | collective-permute-start | bytes 1327112 | tf_op jit(solution)/shard_map/ppermute | solution.py:914
  227.4 15.1 %collective-permute-start.31 = (bf16[24,3840]{1,0:T(8,128)(2,1)S(1)}, bf16[24,3840]{1,0:T(8,128)(2,1)S(1)}, u32[]{:S(2)}, u32[]{:S(2)}) collective-permute-start(bf16[24,3840]{1,0:T(8,128)(2,1)S(1)} %fusion.6.refs_0_), channel_id=1, source_target_pairs={{0,2},{1,3},{2,0},{3,1},{4,6},{5,7},{6,4},{7,5},{8,10},{9,11},{10,... | collective-permute-start | bytes 552968 | tf_op jit(solution)/shard_map/ppermute | solution.py:932
  243.2 20.8 %collective-permute-start.34 = (bf16[144,768]{1,0:T(8,128)(2,1)}, bf16[144,768]{1,0:T(8,128)(2,1)S(1)}, u32[]{:S(2)}, u32[]{:S(2)}) collective-permute-start(bf16[144,768]{1,0:T(8,128)(2,1)} %get-tuple-element.282), channel_id=1, source_target_pairs={{0,2},{1,3},{2,0},{3,1},{4,6},{5,7},{6,4},{7,5},{8,10},{9,11},{10,... | collective-permute-start | bytes 663560 | tf_op jit(solution)/shard_map/ppermute | solution.py:1015
  247.3 16.2 %collective-permute-start.37 = (bf16[24,2304]{1,0:T(8,128)(2,1)S(1)}, bf16[24,2304]{1,0:T(8,128)(2,1)S(1)}, u32[]{:S(2)}, u32[]{:S(2)}) collective-permute-start(bf16[24,2304]{1,0:T(8,128)(2,1)S(1)} %get-tuple-element.344), channel_id=1, source_target_pairs={{0,1},{1,2},{2,3},{3,0},{4,5},{5,6},{6,7},{7,4},{8,9},{9,10},{10,1... | collective-permute-start | bytes 331784 | tf_op jit(solution)/shard_map/ppermute | solution.py:926
  250.1 13.8 %collective-permute-start.38 = (bf16[24,2304]{1,0:T(8,128)(2,1)S(1)}, bf16[24,2304]{1,0:T(8,128)(2,1)S(1)}, u32[]{:S(2)}, u32[]{:S(2)}) collective-permute-start(bf16[24,2304]{1,0:T(8,128)(2,1)S(1)} %get-tuple-element.343), channel_id=1, source_target_pairs={{0,2},{1,3},{2,0},{3,1},{4,6},{5,7},{6,4},{7,5},{8,10},{9,11},{10,... | collective-permute-start | bytes 331784 | tf_op jit(solution)/shard_map/ppermute | solution.py:926
  264.1 24.3 %collective-permute-start.41 = (bf16[24,2304]{1,0:T(8,128)(2,1)S(1)}, bf16[24,2304]{1,0:T(8,128)(2,1)S(1)}, u32[]{:S(2)}, u32[]{:S(2)}) collective-permute-start(bf16[24,2304]{1,0:T(8,128)(2,1)S(1)} %fusion.14.refs_0_), channel_id=1, source_target_pairs={{0,1},{1,2},{2,3},{3,0},{4,5},{5,6},{6,7},{7,4},{8,9},{9,10},{10,1... | collective-permute-start | bytes 331784 | tf_op jit(solution)/shard_map/ppermute | solution.py:932
  266.1 22.3 %collective-permute-start.42 = (bf16[24,2304]{1,0:T(8,128)(2,1)S(1)}, bf16[24,2304]{1,0:T(8,128)(2,1)S(1)}, u32[]{:S(2)}, u32[]{:S(2)}) collective-permute-start(bf16[24,2304]{1,0:T(8,128)(2,1)S(1)} %fusion.14.refs_0_), channel_id=1, source_target_pairs={{0,2},{1,3},{2,0},{3,1},{4,6},{5,7},{6,4},{7,5},{8,10},{9,11},{10,... | collective-permute-start | bytes 331784 | tf_op jit(solution)/shard_map/ppermute | solution.py:932
  269.4 18.9 %collective-permute-start.43 = (bf16[24,2304]{1,0:T(8,128)(2,1)S(1)}, bf16[24,2304]{1,0:T(8,128)(2,1)S(1)}, u32[]{:S(2)}, u32[]{:S(2)}) collective-permute-start(bf16[24,2304]{1,0:T(8,128)(2,1)S(1)} %fusion.14.refs_0_), channel_id=1, source_target_pairs={{0,3},{1,0},{2,1},{3,2},{4,7},{5,4},{6,5},{7,6},{8,11},{9,8},{10,9... | collective-permute-start | bytes 331784 | tf_op jit(solution)/shard_map/ppermute | solution.py:932
  269.5 14.0 %collective-permute-start.40 = (f32[32,768]{1,0:T(8,128)S(1)}, f32[32,768]{1,0:T(8,128)S(1)}, u32[]{:S(2)}, u32[]{:S(2)}) collective-permute-start(f32[32,768]{1,0:T(8,128)S(1)} %add.791), channel_id=1, source_target_pairs={{0,2},{1,3},{2,0},{3,1},{4,6},{5,7},{6,4},{7,5},{8,10},{9,11},{10,... | collective-permute-start | bytes 294920 | tf_op jit(solution)/shard_map/ppermute | solution.py:837
  (54 other events, 438.4 us)

commit v4 on v3

--- a/solution.py
+++ b/solution.py
@@ -298,7 +298,7 @@
             acc_ref[r, :] = jnp.broadcast_to(line(b2_ref), (LR, width))
             return carry
 
-        lax.fori_loop(0, length // LR, chunk, 0, unroll=2)
+        lax.fori_loop(0, length // LR, chunk, 0, unroll=6)
         start(normed)
         for t in range(tiles):
             b1_rows[t] = line(b1_ref, slice(t * tile, (t + 1) * tile))
@@ -334,7 +334,7 @@
             dr_ref[r, :] = low
             return (sums[0] + fold(cot * xhat), sums[1] + fold(cot), sums[2] + fold(low.astype(F32)))
 
-        sums = lax.fori_loop(0, length // LR, chunk, (jnp.zeros((8, width), F32),) * 3, unroll=2)
+        sums = lax.fori_loop(0, length // LR, chunk, (jnp.zeros((8, width), F32),) * 3, unroll=6)
         for n in range(3):
             sm_ref[n : n + 1, :] = row_sum(sums[n])
         start(leaving)
@@ -442,7 +442,7 @@
             db_ref[r, :] = low
             return (sums[0] + fold(first * xhat), sums[1] + fold(first), sums[2] + fold(low.astype(F32)))
 
-        sums = lax.fori_loop(0, length // LR, chunk, (jnp.zeros((8, width), F32),) * 3, unroll=2)
+        sums = lax.fori_loop(0, length // LR, chunk, (jnp.zeros((8, width), F32),) * 3, unroll=6)
         for n in range(3):
             sm_ref[n : n + 1, :] = row_sum(sums[n])
         da_ref[...] = dot_t(db_ref[...], wo_ref[...]).astype(BF)
@@ -1019,7 +1019,7 @@
     bias = jnp.concatenate(bias_grads(diag, nb), 1)
     bias = jnp.pad(bias, ((0, 0), (0, 128 - 3 * nb))).reshape(-1, width)
     hops = {0: (1,), 1: (3,), 2: (2,)}
-    turns = [rounds[1:2], rounds[2:3], rounds[:1] + rounds[3:4], rounds[4:]] if len(rounds) == 5 else [rounds]
+    turns = [rounds[1:3], rounds[:1] + rounds[3:4], rounds[4:]] if len(rounds) == 5 else [rounds]
     layouts = {
         "reduce": None,
         "expand": [[(0, ff)], [(ff, width)]],
@@ -1046,11 +1046,13 @@
     (mixed_out,) = ready["mixed"]
     (o_reduce,), (o_expand, o_output) = (
         ready[r.name] if r.name in ready else r.result(info, layouts[r.name]) for r in (c_reduce, c_expand))
+    (grad_tokens,) = restack(info, gts, F32)
+    smalls = unpack(small, heads, nb, ff)
+    (grad_tokens, smalls, o_reduce, o_expand, o_output), c_qkv.fresh = lax.optimization_barrier(
+        ((grad_tokens, smalls, o_reduce, o_expand, o_output), c_qkv.fresh))
     o_query, o_key, o_value = c_qkv.result(info, layouts["qkv"])
-    (grad_tokens,) = restack(info, gts, F32)
-
-    (g_conv_text, g_conv_patch, g_qb, g_vb, g_ob, g_order, g_horiz, g_vert, g_ng, g_ns, g_be, g_rb, g_fg, g_fs) = unpack(
-        small, heads, nb, ff)
+
+    (g_conv_text, g_conv_patch, g_qb, g_vb, g_ob, g_order, g_horiz, g_vert, g_ng, g_ns, g_be, g_rb, g_fg, g_fs) = smalls
     return (
         mixed_out, grad_tokens, g_conv_text, g_conv_patch, o_query, g_qb, o_key, o_value, g_vb,
         o_output, g_ob, g_order, g_horiz, g_vert, g_ng, g_ns, o_expand, g_be, o_reduce, g_rb, g_fg, g_fs,

time: 297 us -> 290 us (0.976)
  waiting for transfers between devices: 40.5 us -> 35.6 us
  Pallas kernels: 135 us -> 132 us
    ppermute x8, waiting for transfers between devices: 20.1 us -> 15.9 us  [swap(): return lax.ppermute(value, axis, xor_pairs(lax.axis_size(axis), bit))]
    ppermute x9, waiting for transfers between devices: 7.25 us -> 3.86 us  [step(): self.fresh = [lax.ppermute(piece(d), 'seq', ring(d)) for d in range(1, n)]]
    unnamed x90 -> x86, local copies, waits for them, and re-layouts: 8.3 us -> 6.09 us
  transfers between devices with their start and end apart: 44 -> 44, of which waited for: 9 -> 11; matrix products, arithmetic and copies ran while one was open for 11% -> 11% of each run, Pallas kernels for 35% -> 36%
where the time goes in v4:
time: 290 us; the launch traced here: 284 us
  Pallas kernels  132 us (46%)
  starting transfers between devices  69.5 us (24%)
  waiting for transfers between devices  35.6 us (12%)
  other arithmetic  27 us (9%)
  local copies, waits for them, and re-layouts  15.1 us (5%)
  matrix products  3.13 us (1%)
    pallas_call x2, Pallas kernels, heads_back(): pl.pallas_call(heads_kernel, out_shape=(sds((width // 2, 3 * width), BF),...  35.4 us
    pallas_call x1, Pallas kernels, middle(): pl.pallas_call(functools.partial(middle_kernel, n_seq=n_seq, tiles=tiles,...  26.9 us
    pallas_call x2, Pallas kernels, back(): pl.pallas_call(functools.partial(back_kernel, tiles=tiles, last=last, blo...  26.1 us
    pallas_call x1, Pallas kernels, front(): pl.pallas_call(functools.partial(front_kernel, n_seq=n_seq, block=block),...  22.7 us
    ppermute x9, starting transfers between devices, step(): self.fresh = [lax.ppermute(piece(d), 'seq', ring(d)) for d in range(1, n)]  17.6 us
    ppermute x9, starting transfers between devices, spread(): lax.ppermute(blocks[d], 'seq', [(i, (i + d) % n) for i in range(n)])  17.5 us
    ppermute x8, waiting for transfers between devices, swap(): return lax.ppermute(value, axis, xor_pairs(lax.axis_size(axis), bit))  15.9 us
    ppermute x9, starting transfers between devices, step(): self.fresh = [lax.ppermute(self.own, 'seq', ring(d)) for d in range(1, n)]  13.5 us
  transfers between devices with their start and end apart: 44, of which 11 were waited for; matrix products, arithmetic and copies ran while one was open for 11% of the time, Pallas kernels for 36%

profile of v4, /device:TPU:0, one launch (start us, length us, event | category | flops | bytes accessed | tf_op | source)
XLA Modules:
  0.0 284.3 jit_solution(13683561452196446884)
XLA Ops:
  0.8 2.1 dynamic-slice_bitcast_fusion
  2.8 3.0 %collective-permute-start = (bf16[144,768]{1,0:T(8,128)(2,1)S(1)}, bf16[144,768]{1,0:T(8,128)(2,1)S(1)}, u32[]{:S(2)}, u32[]{:S(2)}) collective-permute-start(bf16[144,768]{1,0:T(8,128)(2,1)S(1)} %get-tuple-element.371), channel_id=1, source_target_pairs={{0,1},{1,2},{2,3},{3,0},{4,5},{5,6},{6,7},{7,4},{8,9},{9,10},{10,1... | collective-permute-start | bytes 663560 | tf_op jit(solution)/shard_map/ppermute | solution.py:844
  5.9 2.6 collective-permute-start.1
  24.1 4.2 %collective-permute-start.3 = (bf16[144,768]{1,0:T(8,128)(2,1)S(1)}, bf16[144,768]{1,0:T(8,128)(2,1)S(1)}, u32[]{:S(2)}, u32[]{:S(2)}) collective-permute-start(bf16[144,768]{1,0:T(8,128)(2,1)S(1)} %get-tuple-element.202), channel_id=1, source_target_pairs={{0,1},{1,2},{2,3},{3,0},{4,5},{5,6},{6,7},{7,4},{8,9},{9,10},{10,1... | collective-permute-start | bytes 663560 | tf_op jit(solution)/shard_map/ppermute | solution.py:844
  31.3 22.7 %front.1 = (f32[576,768]{1,0:T(8,128)}, bf16[768,576]{1,0:T(8,128)(2,1)}, bf16[576,768]{1,0:T(8,128)(2,1)}, bf16[576,768]{1,0:T(8,128)(2,1)}, bf16[576,768]{1,0:...) custom-call(s32[3]{0:T(128)} %pad_add_fusion.1.info_ref, f32[12,2]{1,0:T(8,128)} %copy.57.edge_ref, ...), custom_call_target="tpu_custom_call" | custom-call | flops 24999999488 | bytes 8388608 | tf_op jit(solution)/shard_map/front/pallas_call | solution.py:220
  54.9 26.9 %middle.1 = (bf16[144,768]{1,0:T(8,128)(2,1)}, bf16[144,768]{1,0:T(8,128)(2,1)}, bf16[144,768]{1,0:T(8,128)(2,1)}, bf16[144,768]{1,0:T(8,128)(2,1)}, f32[576,768...) custom-call(s32[3]{0:T(128)} %pad_add_fusion.1.info_ref, ...), custom_call_target="tpu_custom_call" | custom-call | flops 35000000512 | bytes 8388608 | tf_op jit(solution)/shard_map/middle/pallas_call | solution.py:371
  81.9 11.4 %back.2 = (bf16[384,3840]{1,0:T(8,128)(2,1)}, bf16[384,3840]{1,0:T(8,128)(2,1)}, f32[1,3072]{1,0:T(1,128)}, f32[576,768]{1,0:T(8,128)}) custom-call(s32[3]{0:T(128)} %pad_add_fusion.1.info_ref, bf16[576,768]{1,0:T(8,128)(2,1)} %get-tuple-element.207.refs_0_, f32[576,768]{1,0:T(8,128)} %get-tuple-element.208.refs_1_, bf16[3072,768]{1,0:T(8,128)(2,1)} %refs_2_.3, ...), custom_call_target="tpu_custom_call" | custom-call | flops 12000000000 | bytes 8388608 | tf_op jit(solution)/shard_map/back/pallas_call | solution.py:472
  100.5 14.7 %back.3 = (bf16[384,3840]{1,0:T(8,128)(2,1)}, bf16[384,3840]{1,0:T(8,128)(2,1)}, f32[1,3072]{1,0:T(1,128)}, f32[576,768]{1,0:T(8,128)}, bf16[576,768]{1,0:T(8,128)(2,1)}, /*index=5*/f32[8,768]{1,0:T(8,128)}) custom-call(s32[3]{0:T(128)} %pad_add_fusion.1.info_ref, ...), custom_call_target="tpu_custom_call", output_to_operand_aliasing={{0}: (13, {}), {1}: (14, {}), {2}: (15, {})} | custom-call | flops 12000000000 | bytes 8388608 | tf_op jit(solution)/shard_map/back/pallas_call | solution.py:472
  118.0 2.5 add_convert_fusion.5
  121.5 17.5 %heads_back.2 = (bf16[384,2304]{1,0:T(8,128)(2,1)}, bf16[384,2304]{1,0:T(8,128)(2,1)}, f32[8,768]{1,0:T(8,128)}, f32[12,8,256]{2,1,0:T(8,128)}, f32[576,768]{1,0:T(8,128)}) custom-call(bf16[12,576,576]{2,1,0:T(8,128)(2,1)} %get-tuple-element.197.refs_0_, bf16[576,768]{1,0:T(8,128)(2,1)} %get-tuple-element.198.refs_1_, ...), custom_call_target="tpu_custom_call" | custom-call | flops 20000000000 | bytes 8388608 | tf_op jit(solution)/shard_map/heads_back/pallas_call | solution.py:590
  139.8 2.0 add_convert_fusion.4
  142.6 4.4 %collective-permute-start.13 = (bf16[96,768]{1,0:T(8,128)(2,1)}, bf16[96,768]{1,0:T(8,128)(2,1)}, u32[]{:S(2)}, u32[]{:S(2)}) collective-permute-start(bf16[96,768]{1,0:T(8,128)(2,1)} %get-tuple-element.383), channel_id=1, source_target_pairs={{0,1},{1,2},{2,3},{3,0},{4,5},{5,6},{6,7},{7,4},{8,9},{9,10},{10,1... | collective-permute-start | bytes 442376 | tf_op jit(solution)/shard_map/ppermute | solution.py:926
  147.3 2.1 collective-permute-start.15
  152.6 17.9 %heads_back.3 = (bf16[384,2304]{1,0:T(8,128)(2,1)}, bf16[384,2304]{1,0:T(8,128)(2,1)}, f32[8,768]{1,0:T(8,128)}, f32[12,8,256]{2,1,0:T(8,128)}, f32[576,768]{1,0:T(8,128)}) custom-call(bf16[12,576,576]{2,1,0:T(8,128)(2,1)} %get-tuple-element.197.refs_0_, ...), custom_call_target="tpu_custom_call", output_to_operand_aliasing={{0}: (13, {}), {1}: (14, {}), {2}: (15, {}), {3}: (16, {})} | custom-call | flops 20000000000 | bytes 8388608 | tf_op jit(solution)/shard_map/heads_back/pallas_call | solution.py:590
  172.6 2.6 collective-permute-start.18
  176.4 2.5 add_convert_fusion.1
  180.6 7.9 %encode_back.1 = (bf16[144,768]{1,0:T(8,128)(2,1)}, bf16[144,768]{1,0:T(8,128)(2,1)}, bf16[144,768]{1,0:T(8,128)(2,1)}, bf16[144,768]{1,0:T(8,128)(2,1)}, f32[32,768]{1,0:T(8,128)}) custom-call(s32[3]{0:T(128)} %pad_add_fusion.1.info_ref, bf16[144,768]{1,0:T(8,128)(2,1)} %get-tuple-element.193.refs_0_, bf16[144,768]{1,0:T(8,128)(2,1)} %copy-done.32, ...), custom_call_target="tpu_custom_call" | custom-call | flops 10000000000 | bytes 8388608 | tf_op jit(solution)/shard_map/encode_back/pallas_call | solution.py:688
  204.7 3.0 %collective-permute-start.27 = (bf16[24,3840]{1,0:T(8,128)(2,1)S(1)}, bf16[24,3840]{1,0:T(8,128)(2,1)S(1)}, u32[]{:S(2)}, u32[]{:S(2)}) collective-permute-start(bf16[24,3840]{1,0:T(8,128)(2,1)S(1)} %get-tuple-element.378), channel_id=1, source_target_pairs={{0,3},{1,0},{2,1},{3,2},{4,7},{5,4},{6,5},{7,6},{8,11},{9,8},{10,9... | collective-permute-start | bytes 552968 | tf_op jit(solution)/shard_map/ppermute | solution.py:926
  207.7 2.2 restack.5
  210.0 2.2 restack.6
  212.2 3.8 %collective-permute-done.26 = bf16[24,3840]{1,0:T(8,128)(2,1)S(1)} collective-permute-done((bf16[24,3840]{1,0:T(8,128)(2,1)S(1)}, bf16[24,3840]{1,0:T(8,128)(2,1)S(1)}, u32[]{:S(2)}, u32[]{:S(2)}) %collective-permute-start.26) | collective-permute-done | bytes 184352 | tf_op jit(solution)/shard_map/ppermute | solution.py:926
  216.1 4.5 %collective-permute-start.29 = (bf16[144,768]{1,0:T(8,128)(2,1)}, bf16[144,768]{1,0:T(8,128)(2,1)S(1)}, u32[]{:S(2)}, u32[]{:S(2)}) collective-permute-start(bf16[144,768]{1,0:T(8,128)(2,1)} %get-tuple-element.293), channel_id=1, source_target_pairs={{0,3},{1,0},{2,1},{3,2},{4,7},{5,4},{6,5},{7,6},{8,11},{9,8},{10,9... | collective-permute-start | bytes 663560 | tf_op jit(solution)/shard_map/ppermute | solution.py:1015
  228.5 2.2 collective-permute-start.34
  230.8 2.8 collective-permute-done.32.refs_1_
  233.6 7.0 %collective-permute-done.33.refs_2_ = bf16[24,3840]{1,0:T(8,128)(2,1)S(1)} collective-permute-done((bf16[24,3840]{1,0:T(8,128)(2,1)S(1)}, bf16[24,3840]{1,0:T(8,128)(2,1)S(1)}, u32[]{:S(2)}, u32[]{:S(2)}) %collective-permute-start.33) | collective-permute-done | bytes 184352 | tf_op jit(solution)/shard_map/ppermute | solution.py:932
  241.3 3.4 %collective-permute-start.36 = (bf16[144,768]{1,0:T(8,128)(2,1)}, bf16[144,768]{1,0:T(8,128)(2,1)S(1)}, u32[]{:S(2)}, u32[]{:S(2)}) collective-permute-start(bf16[144,768]{1,0:T(8,128)(2,1)} %get-tuple-element.303), channel_id=1, source_target_pairs={{0,2},{1,3},{2,0},{3,1},{4,6},{5,7},{6,4},{7,5},{8,10},{9,11},{10,... | collective-permute-start | bytes 663560 | tf_op jit(solution)/shard_map/ppermute | solution.py:1015
  247.8 2.3 collective-permute-start.39
  252.0 2.4 restack.7
  254.4 14.5 %collective-permute-done.37 = f32[32,768]{1,0:T(8,128)S(1)} collective-permute-done((f32[32,768]{1,0:T(8,128)S(1)}, f32[32,768]{1,0:T(8,128)S(1)}, u32[]{:S(2)}, u32[]{:S(2)}) %collective-permute-start.37) | collective-permute-done | bytes 98336 | tf_op jit(solution)/shard_map/ppermute | solution.py:837
  270.3 3.4 %collective-permute-start.42 = (bf16[24,2304]{1,0:T(8,128)(2,1)S(1)}, bf16[24,2304]{1,0:T(8,128)(2,1)S(1)}, u32[]{:S(2)}, u32[]{:S(2)}) collective-permute-start(bf16[24,2304]{1,0:T(8,128)(2,1)S(1)} %fusion.14.refs_0_), channel_id=1, source_target_pairs={{0,2},{1,3},{2,0},{3,1},{4,6},{5,7},{6,4},{7,5},{8,10},{9,11},{10,... | collective-permute-start | bytes 331784 | tf_op jit(solution)/shard_map/ppermute | solution.py:932
  275.3 2.6 restack.8
  277.9 3.1 %collective-permute-done.42.refs_2_ = bf16[24,2304]{1,0:T(8,128)(2,1)S(1)} collective-permute-done((bf16[24,2304]{1,0:T(8,128)(2,1)S(1)}, bf16[24,2304]{1,0:T(8,128)(2,1)S(1)}, u32[]{:S(2)}, u32[]{:S(2)}) %collective-permute-start.42) | collective-permute-done | bytes 110624 | tf_op jit(solution)/shard_map/ppermute | solution.py:932
  (238 shorter events, 75.9 us)
Async XLA Ops:
  2.8 21.2 %collective-permute-start = (bf16[144,768]{1,0:T(8,128)(2,1)S(1)}, bf16[144,768]{1,0:T(8,128)(2,1)S(1)}, u32[]{:S(2)}, u32[]{:S(2)}) collective-permute-start(bf16[144,768]{1,0:T(8,128)(2,1)S(1)} %get-tuple-element.371), channel_id=1, source_target_pairs={{0,1},{1,2},{2,3},{3,0},{4,5},{5,6},{6,7},{7,4},{8,9},{9,10},{10,1... | collective-permute-start | bytes 663560 | tf_op jit(solution)/shard_map/ppermute | solution.py:844
  5.9 18.2 %collective-permute-start.1 = (bf16[144,768]{1,0:T(8,128)(2,1)S(1)}, bf16[144,768]{1,0:T(8,128)(2,1)S(1)}, u32[]{:S(2)}, u32[]{:S(2)}) collective-permute-start(bf16[144,768]{1,0:T(8,128)(2,1)S(1)} %get-tuple-element.373), channel_id=1, source_target_pairs={{0,2},{1,3},{2,0},{3,1},{4,6},{5,7},{6,4},{7,5},{8,10},{9,11},{10,... | collective-permute-start | bytes 663560 | tf_op jit(solution)/shard_map/ppermute | solution.py:844
  8.4 15.6 %collective-permute-start.2 = (bf16[144,768]{1,0:T(8,128)(2,1)S(1)}, bf16[144,768]{1,0:T(8,128)(2,1)}, u32[]{:S(2)}, u32[]{:S(2)}) collective-permute-start(bf16[144,768]{1,0:T(8,128)(2,1)S(1)} %get-tuple-element.370), channel_id=1, source_target_pairs={{0,3},{1,0},{2,1},{3,2},{4,7},{5,4},{6,5},{7,6},{8,11},{9,8},{10,9... | collective-permute-start | bytes 663560 | tf_op jit(solution)/shard_map/ppermute | solution.py:844
  24.1 30.0 %collective-permute-start.3 = (bf16[144,768]{1,0:T(8,128)(2,1)S(1)}, bf16[144,768]{1,0:T(8,128)(2,1)S(1)}, u32[]{:S(2)}, u32[]{:S(2)}) collective-permute-start(bf16[144,768]{1,0:T(8,128)(2,1)S(1)} %get-tuple-element.202), channel_id=1, source_target_pairs={{0,1},{1,2},{2,3},{3,0},{4,5},{5,6},{6,7},{7,4},{8,9},{9,10},{10,1... | collective-permute-start | bytes 663560 | tf_op jit(solution)/shard_map/ppermute | solution.py:844
  28.2 25.8 %collective-permute-start.4 = (bf16[144,768]{1,0:T(8,128)(2,1)S(1)}, bf16[144,768]{1,0:T(8,128)(2,1)S(1)}, u32[]{:S(2)}, u32[]{:S(2)}) collective-permute-start(bf16[144,768]{1,0:T(8,128)(2,1)S(1)} %get-tuple-element.203), channel_id=1, source_target_pairs={{0,2},{1,3},{2,0},{3,1},{4,6},{5,7},{6,4},{7,5},{8,10},{9,11},{10,... | collective-permute-start | bytes 663560 | tf_op jit(solution)/shard_map/ppermute | solution.py:844
  29.7 24.4 %collective-permute-start.5 = (bf16[144,768]{1,0:T(8,128)(2,1)S(1)}, bf16[144,768]{1,0:T(8,128)(2,1)S(1)}, u32[]{:S(2)}, u32[]{:S(2)}) collective-permute-start(bf16[144,768]{1,0:T(8,128)(2,1)S(1)} %get-tuple-element.204), channel_id=1, source_target_pairs={{0,3},{1,0},{2,1},{3,2},{4,7},{5,4},{6,5},{7,6},{8,11},{9,8},{10,9... | collective-permute-start | bytes 663560 | tf_op jit(solution)/shard_map/ppermute | solution.py:844
  95.1 20.7 %collective-permute-start.10 = (bf16[2,384,768]{2,1,0:T(8,128)(2,1)S(1)}, bf16[2,384,768]{2,1,0:T(8,128)(2,1)S(1)}, u32[]{:S(2)}, u32[]{:S(2)}) collective-permute-start(bf16[2,384,768]{2,1,0:T(8,128)(2,1)S(1)} %pad_maximum_fusion.1), channel_id=1, source_target_pairs={{0,8},{4,20},{8,0},{12,28},{16,24},{20,4},{24,16},{28,12},{1,9},{5... | collective-permute-start | bytes 3538952 | tf_op jit(solution)/shard_map/ppermute | solution.py:914
  96.6 18.6 %collective-permute-start.7 = (bf16[144,768]{1,0:T(8,128)(2,1)}, bf16[144,768]{1,0:T(8,128)(2,1)S(1)}, u32[]{:S(2)}, u32[]{:S(2)}) collective-permute-start(bf16[144,768]{1,0:T(8,128)(2,1)} %get-tuple-element.229), channel_id=1, source_target_pairs={{0,1},{1,2},{2,3},{3,0},{4,5},{5,6},{6,7},{7,4},{8,9},{9,10},{10,1... | collective-permute-start | bytes 663560 | tf_op jit(solution)/shard_map/ppermute | solution.py:844
  97.8 18.0 %collective-permute-start.8 = (bf16[144,768]{1,0:T(8,128)(2,1)S(1)}, bf16[144,768]{1,0:T(8,128)(2,1)S(1)}, u32[]{:S(2)}, u32[]{:S(2)}) collective-permute-start(bf16[144,768]{1,0:T(8,128)(2,1)S(1)} %copy-done.35), channel_id=1, source_target_pairs={{0,2},{1,3},{2,0},{3,1},{4,6},{5,7},{6,4},{7,5},{8,10},{9,11},{10,... | collective-permute-start | bytes 663560 | tf_op jit(solution)/shard_map/ppermute | solution.py:844
  99.2 16.6 %collective-permute-start.9 = (bf16[144,768]{1,0:T(8,128)(2,1)S(1)}, bf16[144,768]{1,0:T(8,128)(2,1)S(1)}, u32[]{:S(2)}, u32[]{:S(2)}) collective-permute-start(bf16[144,768]{1,0:T(8,128)(2,1)S(1)} %copy-done.34), channel_id=1, source_target_pairs={{0,3},{1,0},{2,1},{3,2},{4,7},{5,4},{6,5},{7,6},{8,11},{9,8},{10,9... | collective-permute-start | bytes 663560 | tf_op jit(solution)/shard_map/ppermute | solution.py:844
  116.9 22.1 %collective-permute-start.12 = (bf16[384,3840]{1,0:T(8,128)(2,1)}, bf16[384,3840]{1,0:T(8,128)(2,1)S(1)}, u32[]{:S(2)}, u32[]{:S(2)}) collective-permute-start(bf16[384,3840]{1,0:T(8,128)(2,1)} %get-tuple-element.243), channel_id=1, source_target_pairs={{0,4},{4,0},{8,12},{12,8},{16,20},{20,16},{24,28},{28,24},{1,5},{5... | collective-permute-start | bytes 8847368 | tf_op jit(solution)/shard_map/ppermute | solution.py:837
  120.5 18.5 %collective-permute-start.11 = (bf16[1,384,768]{2,1,0:T(8,128)(2,1)}, bf16[1,384,768]{2,1,0:T(8,128)(2,1)S(1)}, u32[]{:S(2)}, u32[]{:S(2)}) collective-permute-start(bf16[1,384,768]{2,1,0:T(8,128)(2,1)} %add_convert_fusion.5), channel_id=1, source_target_pairs={{0,16},{4,12},{8,24},{12,4},{16,0},{20,28},{24,8},{28,20},{1,17},{... | collective-permute-start | bytes 1769480 | tf_op jit(solution)/shard_map/ppermute | solution.py:914
  142.6 27.8 %collective-permute-start.13 = (bf16[96,768]{1,0:T(8,128)(2,1)}, bf16[96,768]{1,0:T(8,128)(2,1)}, u32[]{:S(2)}, u32[]{:S(2)}) collective-permute-start(bf16[96,768]{1,0:T(8,128)(2,1)} %get-tuple-element.383), channel_id=1, source_target_pairs={{0,1},{1,2},{2,3},{3,0},{4,5},{5,6},{6,7},{7,4},{8,9},{9,10},{10,1... | collective-permute-start | bytes 442376 | tf_op jit(solution)/shard_map/ppermute | solution.py:926
  147.0 23.4 %collective-permute-start.14 = (bf16[96,768]{1,0:T(8,128)(2,1)}, bf16[96,768]{1,0:T(8,128)(2,1)}, u32[]{:S(2)}, u32[]{:S(2)}) collective-permute-start(bf16[96,768]{1,0:T(8,128)(2,1)} %get-tuple-element.382), channel_id=1, source_target_pairs={{0,2},{1,3},{2,0},{3,1},{4,6},{5,7},{6,4},{7,5},{8,10},{9,11},{10,... | collective-permute-start | bytes 442376 | tf_op jit(solution)/shard_map/ppermute | solution.py:926
  147.3 23.2 %collective-permute-start.15 = (bf16[96,768]{1,0:T(8,128)(2,1)}, bf16[96,768]{1,0:T(8,128)(2,1)}, u32[]{:S(2)}, u32[]{:S(2)}) collective-permute-start(bf16[96,768]{1,0:T(8,128)(2,1)} %get-tuple-element.381), channel_id=1, source_target_pairs={{0,3},{1,0},{2,1},{3,2},{4,7},{5,4},{6,5},{7,6},{8,11},{9,8},{10,9... | collective-permute-start | bytes 442376 | tf_op jit(solution)/shard_map/ppermute | solution.py:926
  151.1 19.7 %collective-permute-start.16 = (bf16[2,96,3840]{2,1,0:T(8,128)(2,1)}, bf16[2,96,3840]{2,1,0:T(8,128)(2,1)}, u32[]{:S(2)}, u32[]{:S(2)}) collective-permute-start(bf16[2,96,3840]{2,1,0:T(8,128)(2,1)} %pad_maximum_fusion), channel_id=1, source_target_pairs={{0,8},{4,20},{8,0},{12,28},{16,24},{20,4},{24,16},{28,12},{1,9},{5... | collective-permute-start | bytes 4423688 | tf_op jit(solution)/shard_map/ppermute | solution.py:914
  172.6 16.5 %collective-permute-start.17 = (bf16[96,768]{1,0:T(8,128)(2,1)}, bf16[96,768]{1,0:T(8,128)(2,1)S(1)}, u32[]{:S(2)}, u32[]{:S(2)}) collective-permute-start(bf16[96,768]{1,0:T(8,128)(2,1)} %fusion.11.refs_0_), channel_id=1, source_target_pairs={{0,1},{1,2},{2,3},{3,0},{4,5},{5,6},{6,7},{7,4},{8,9},{9,10},{10,1... | collective-permute-start | bytes 442376 | tf_op jit(solution)/shard_map/ppermute | solution.py:932
  172.6 16.5 %collective-permute-start.18 = (bf16[96,768]{1,0:T(8,128)(2,1)}, bf16[96,768]{1,0:T(8,128)(2,1)S(1)}, u32[]{:S(2)}, u32[]{:S(2)}) collective-permute-start(bf16[96,768]{1,0:T(8,128)(2,1)} %fusion.11.refs_0_), channel_id=1, source_target_pairs={{0,2},{1,3},{2,0},{3,1},{4,6},{5,7},{6,4},{7,5},{8,10},{9,11},{10,... | collective-permute-start | bytes 442376 | tf_op jit(solution)/shard_map/ppermute | solution.py:932
  175.2 14.0 %collective-permute-start.19 = (bf16[96,768]{1,0:T(8,128)(2,1)}, bf16[96,768]{1,0:T(8,128)(2,1)S(1)}, u32[]{:S(2)}, u32[]{:S(2)}) collective-permute-start(bf16[96,768]{1,0:T(8,128)(2,1)} %fusion.11.refs_0_), channel_id=1, source_target_pairs={{0,3},{1,0},{2,1},{3,2},{4,7},{5,4},{6,5},{7,6},{8,11},{9,8},{10,9... | collective-permute-start | bytes 442376 | tf_op jit(solution)/shard_map/ppermute | solution.py:932
  178.9 11.9 %collective-permute-start.21 = (bf16[384,2304]{1,0:T(8,128)(2,1)}, bf16[384,2304]{1,0:T(8,128)(2,1)}, u32[]{:S(2)}, u32[]{:S(2)}) collective-permute-start(bf16[384,2304]{1,0:T(8,128)(2,1)} %get-tuple-element.273), channel_id=1, source_target_pairs={{0,4},{4,0},{8,12},{12,8},{16,20},{20,16},{24,28},{28,24},{1,5},{5... | collective-permute-start | bytes 5308424 | tf_op jit(solution)/shard_map/ppermute | solution.py:837
  190.9 25.2 %collective-permute-start.22 = (bf16[144,768]{1,0:T(8,128)(2,1)}, bf16[144,768]{1,0:T(8,128)(2,1)S(1)}, u32[]{:S(2)}, u32[]{:S(2)}) collective-permute-start(bf16[144,768]{1,0:T(8,128)(2,1)} %get-tuple-element.275), channel_id=1, source_target_pairs={{0,1},{1,2},{2,3},{3,0},{4,5},{5,6},{6,7},{7,4},{8,9},{9,10},{10,1... | collective-permute-start | bytes 663560 | tf_op jit(solution)/shard_map/ppermute | solution.py:1015
  196.3 19.7 %collective-permute-start.28 = (bf16[2,96,2304]{2,1,0:T(8,128)(2,1)}, bf16[2,96,2304]{2,1,0:T(8,128)(2,1)}, u32[]{:S(2)}, u32[]{:S(2)}) collective-permute-start(bf16[2,96,2304]{2,1,0:T(8,128)(2,1)} %pad_maximum_fusion.2), channel_id=1, source_target_pairs={{0,8},{4,20},{8,0},{12,28},{16,24},{20,4},{24,16},{28,12},{1,9},{5... | collective-permute-start | bytes 2654216 | tf_op jit(solution)/shard_map/ppermute | solution.py:914
  202.4 13.7 %collective-permute-start.26 = (bf16[24,3840]{1,0:T(8,128)(2,1)S(1)}, bf16[24,3840]{1,0:T(8,128)(2,1)S(1)}, u32[]{:S(2)}, u32[]{:S(2)}) collective-permute-start(bf16[24,3840]{1,0:T(8,128)(2,1)S(1)} %get-tuple-element.379), channel_id=1, source_target_pairs={{0,2},{1,3},{2,0},{3,1},{4,6},{5,7},{6,4},{7,5},{8,10},{9,11},{10,... | collective-permute-start | bytes 552968 | tf_op jit(solution)/shard_map/ppermute | solution.py:926
  216.1 24.5 %collective-permute-start.29 = (bf16[144,768]{1,0:T(8,128)(2,1)}, bf16[144,768]{1,0:T(8,128)(2,1)S(1)}, u32[]{:S(2)}, u32[]{:S(2)}) collective-permute-start(bf16[144,768]{1,0:T(8,128)(2,1)} %get-tuple-element.293), channel_id=1, source_target_pairs={{0,3},{1,0},{2,1},{3,2},{4,7},{5,4},{6,5},{7,6},{8,11},{9,8},{10,9... | collective-permute-start | bytes 663560 | tf_op jit(solution)/shard_map/ppermute | solution.py:1015
  221.9 19.3 %collective-permute-start.35 = (bf16[1,96,2304]{2,1,0:T(8,128)(2,1)S(1)}, bf16[1,96,2304]{2,1,0:T(8,128)(2,1)S(1)}, u32[]{:S(2)}, u32[]{:S(2)}) collective-permute-start(bf16[1,96,2304]{2,1,0:T(8,128)(2,1)S(1)} %add_convert_fusion.9), channel_id=1, source_target_pairs={{0,16},{4,12},{8,24},{12,4},{16,0},{20,28},{24,8},{28,20},{1,17},{... | collective-permute-start | bytes 1327112 | tf_op jit(solution)/shard_map/ppermute | solution.py:914
  226.1 14.5 %collective-permute-start.33 = (bf16[24,3840]{1,0:T(8,128)(2,1)S(1)}, bf16[24,3840]{1,0:T(8,128)(2,1)S(1)}, u32[]{:S(2)}, u32[]{:S(2)}) collective-permute-start(bf16[24,3840]{1,0:T(8,128)(2,1)S(1)} %fusion.6.refs_0_), channel_id=1, source_target_pairs={{0,2},{1,3},{2,0},{3,1},{4,6},{5,7},{6,4},{7,5},{8,10},{9,11},{10,... | collective-permute-start | bytes 552968 | tf_op jit(solution)/shard_map/ppermute | solution.py:932
  228.5 12.1 %collective-permute-start.34 = (bf16[24,3840]{1,0:T(8,128)(2,1)S(1)}, bf16[24,3840]{1,0:T(8,128)(2,1)S(1)}, u32[]{:S(2)}, u32[]{:S(2)}) collective-permute-start(bf16[24,3840]{1,0:T(8,128)(2,1)S(1)} %fusion.6.refs_0_), channel_id=1, source_target_pairs={{0,3},{1,0},{2,1},{3,2},{4,7},{5,4},{6,5},{7,6},{8,11},{9,8},{10,9... | collective-permute-start | bytes 552968 | tf_op jit(solution)/shard_map/ppermute | solution.py:932
  241.3 28.3 %collective-permute-start.36 = (bf16[144,768]{1,0:T(8,128)(2,1)}, bf16[144,768]{1,0:T(8,128)(2,1)S(1)}, u32[]{:S(2)}, u32[]{:S(2)}) collective-permute-start(bf16[144,768]{1,0:T(8,128)(2,1)} %get-tuple-element.303), channel_id=1, source_target_pairs={{0,2},{1,3},{2,0},{3,1},{4,6},{5,7},{6,4},{7,5},{8,10},{9,11},{10,... | collective-permute-start | bytes 663560 | tf_op jit(solution)/shard_map/ppermute | solution.py:1015
  246.1 23.5 %collective-permute-start.38 = (bf16[24,2304]{1,0:T(8,128)(2,1)S(1)}, bf16[24,2304]{1,0:T(8,128)(2,1)S(1)}, u32[]{:S(2)}, u32[]{:S(2)}) collective-permute-start(bf16[24,2304]{1,0:T(8,128)(2,1)S(1)} %get-tuple-element.386), channel_id=1, source_target_pairs={{0,1},{1,2},{2,3},{3,0},{4,5},{5,6},{6,7},{7,4},{8,9},{9,10},{10,1... | collective-permute-start | bytes 331784 | tf_op jit(solution)/shard_map/ppermute | solution.py:926
  247.8 21.8 %collective-permute-start.39 = (bf16[24,2304]{1,0:T(8,128)(2,1)S(1)}, bf16[24,2304]{1,0:T(8,128)(2,1)S(1)}, u32[]{:S(2)}, u32[]{:S(2)}) collective-permute-start(bf16[24,2304]{1,0:T(8,128)(2,1)S(1)} %get-tuple-element.385), channel_id=1, source_target_pairs={{0,2},{1,3},{2,0},{3,1},{4,6},{5,7},{6,4},{7,5},{8,10},{9,11},{10,... | collective-permute-start | bytes 331784 | tf_op jit(solution)/shard_map/ppermute | solution.py:926
  250.1 19.5 %collective-permute-start.40 = (bf16[24,2304]{1,0:T(8,128)(2,1)S(1)}, bf16[24,2304]{1,0:T(8,128)(2,1)S(1)}, u32[]{:S(2)}, u32[]{:S(2)}) collective-permute-start(bf16[24,2304]{1,0:T(8,128)(2,1)S(1)} %get-tuple-element.384), channel_id=1, source_target_pairs={{0,3},{1,0},{2,1},{3,2},{4,7},{5,4},{6,5},{7,6},{8,11},{9,8},{10,9... | collective-permute-start | bytes 331784 | tf_op jit(solution)/shard_map/ppermute | solution.py:926
  250.2 18.7 %collective-permute-start.37 = (f32[32,768]{1,0:T(8,128)S(1)}, f32[32,768]{1,0:T(8,128)S(1)}, u32[]{:S(2)}, u32[]{:S(2)}) collective-permute-start(f32[32,768]{1,0:T(8,128)S(1)} %add.786), channel_id=1, source_target_pairs={{0,2},{1,3},{2,0},{3,1},{4,6},{5,7},{6,4},{7,5},{8,10},{9,11},{10,... | collective-permute-start | bytes 294920 | tf_op jit(solution)/shard_map/ppermute | solution.py:837
  (52 other events, 378.5 us)

commit v5 on v4

--- a/solution.py
+++ b/solution.py
@@ -1018,7 +1018,7 @@
         r.name = name
     bias = jnp.concatenate(bias_grads(diag, nb), 1)
     bias = jnp.pad(bias, ((0, 0), (0, 128 - 3 * nb))).reshape(-1, width)
-    hops = {0: (1,), 1: (3,), 2: (2,)}
+    hops = {0: (2,), 1: (1,), 2: (3,)}
     turns = [rounds[1:3], rounds[:1] + rounds[3:4], rounds[4:]] if len(rounds) == 5 else [rounds]
     layouts = {
         "reduce": None,

time: 290 us -> 287 us (0.990)
  starting transfers between devices: 69.5 us -> 61 us
  waiting for transfers between devices: 35.6 us -> 41 us
    ppermute x8, waiting for transfers between devices: 15.9 us -> 20.3 us  [swap(): return lax.ppermute(value, axis, xor_pairs(lax.axis_size(axis), bit))]
    ppermute x9, starting transfers between devices: 13.5 us -> 10.5 us  [step(): self.fresh = [lax.ppermute(self.own, 'seq', ring(d)) for d in range(1, n)]]
  transfers between devices with their start and end apart: 44 -> 44, of which waited for: 11 -> 11; matrix products, arithmetic and copies ran while one was open for 11% -> 12% of each run, Pallas kernels for 36% -> 37%
where the time goes in v5:
time: 287 us; the launch traced here: 281 us
  Pallas kernels  132 us (46%)
  starting transfers between devices  61 us (21%)
  waiting for transfers between devices  41 us (14%)
  other arithmetic  27 us (9%)
  local copies, waits for them, and re-layouts  15.1 us (5%)
  matrix products  3.13 us (1%)
    pallas_call x2, Pallas kernels, heads_back(): pl.pallas_call(heads_kernel, out_shape=(sds((width // 2, 3 * width), BF),...  35.4 us
    pallas_call x1, Pallas kernels, middle(): pl.pallas_call(functools.partial(middle_kernel, n_seq=n_seq, tiles=tiles,...  26.9 us
    pallas_call x2, Pallas kernels, back(): pl.pallas_call(functools.partial(back_kernel, tiles=tiles, last=last, blo...  26.1 us
    pallas_call x1, Pallas kernels, front(): pl.pallas_call(functools.partial(front_kernel, n_seq=n_seq, block=block),...  22.7 us
    ppermute x8, waiting for transfers between devices, swap(): return lax.ppermute(value, axis, xor_pairs(lax.axis_size(axis), bit))  20.3 us
    ppermute x9, starting transfers between devices, spread(): lax.ppermute(blocks[d], 'seq', [(i, (i + d) % n) for i in range(n)])  17.5 us
    ppermute x9, starting transfers between devices, step(): self.fresh = [lax.ppermute(piece(d), 'seq', ring(d)) for d in range(1, n)]  14.7 us
    convert_element_type x9, other arithmetic, total(): return out.astype(BF)  12.8 us
  transfers between devices with their start and end apart: 44, of which 11 were waited for; matrix products, arithmetic and copies ran while one was open for 12% of the time, Pallas kernels for 37%

profile of v5, /device:TPU:0, one launch (start us, length us, event | category | flops | bytes accessed | tf_op | source)
XLA Modules:
  0.0 281.3 jit_solution(13045265834101169645)
XLA Ops:
  0.8 2.1 dynamic-slice_bitcast_fusion
  2.8 3.0 %collective-permute-start = (bf16[144,768]{1,0:T(8,128)(2,1)S(1)}, bf16[144,768]{1,0:T(8,128)(2,1)S(1)}, u32[]{:S(2)}, u32[]{:S(2)}) collective-permute-start(bf16[144,768]{1,0:T(8,128)(2,1)S(1)} %get-tuple-element.371), channel_id=1, source_target_pairs={{0,1},{1,2},{2,3},{3,0},{4,5},{5,6},{6,7},{7,4},{8,9},{9,10},{10,1... | collective-permute-start | bytes 663560 | tf_op jit(solution)/shard_map/ppermute | solution.py:844
  5.9 2.6 collective-permute-start.1
  24.1 4.2 %collective-permute-start.3 = (bf16[144,768]{1,0:T(8,128)(2,1)S(1)}, bf16[144,768]{1,0:T(8,128)(2,1)S(1)}, u32[]{:S(2)}, u32[]{:S(2)}) collective-permute-start(bf16[144,768]{1,0:T(8,128)(2,1)S(1)} %get-tuple-element.202), channel_id=1, source_target_pairs={{0,1},{1,2},{2,3},{3,0},{4,5},{5,6},{6,7},{7,4},{8,9},{9,10},{10,1... | collective-permute-start | bytes 663560 | tf_op jit(solution)/shard_map/ppermute | solution.py:844
  31.3 22.7 %front.1 = (f32[576,768]{1,0:T(8,128)}, bf16[768,576]{1,0:T(8,128)(2,1)}, bf16[576,768]{1,0:T(8,128)(2,1)}, bf16[576,768]{1,0:T(8,128)(2,1)}, bf16[576,768]{1,0:...) custom-call(s32[3]{0:T(128)} %pad_add_fusion.1.info_ref, f32[12,2]{1,0:T(8,128)} %copy.57.edge_ref, ...), custom_call_target="tpu_custom_call" | custom-call | flops 24999999488 | bytes 8388608 | tf_op jit(solution)/shard_map/front/pallas_call | solution.py:220
  54.9 26.9 %middle.1 = (bf16[144,768]{1,0:T(8,128)(2,1)}, bf16[144,768]{1,0:T(8,128)(2,1)}, bf16[144,768]{1,0:T(8,128)(2,1)}, bf16[144,768]{1,0:T(8,128)(2,1)}, f32[576,768...) custom-call(s32[3]{0:T(128)} %pad_add_fusion.1.info_ref, ...), custom_call_target="tpu_custom_call" | custom-call | flops 35000000512 | bytes 8388608 | tf_op jit(solution)/shard_map/middle/pallas_call | solution.py:371
  81.9 11.4 %back.2 = (bf16[384,3840]{1,0:T(8,128)(2,1)}, bf16[384,3840]{1,0:T(8,128)(2,1)}, f32[1,3072]{1,0:T(1,128)}, f32[576,768]{1,0:T(8,128)}) custom-call(s32[3]{0:T(128)} %pad_add_fusion.1.info_ref, bf16[576,768]{1,0:T(8,128)(2,1)} %get-tuple-element.207.refs_0_, f32[576,768]{1,0:T(8,128)} %get-tuple-element.208.refs_1_, bf16[3072,768]{1,0:T(8,128)(2,1)} %refs_2_.3, ...), custom_call_target="tpu_custom_call" | custom-call | flops 12000000000 | bytes 8388608 | tf_op jit(solution)/shard_map/back/pallas_call | solution.py:472
  100.5 14.7 %back.3 = (bf16[384,3840]{1,0:T(8,128)(2,1)}, bf16[384,3840]{1,0:T(8,128)(2,1)}, f32[1,3072]{1,0:T(1,128)}, f32[576,768]{1,0:T(8,128)}, bf16[576,768]{1,0:T(8,128)(2,1)}, /*index=5*/f32[8,768]{1,0:T(8,128)}) custom-call(s32[3]{0:T(128)} %pad_add_fusion.1.info_ref, ...), custom_call_target="tpu_custom_call", output_to_operand_aliasing={{0}: (13, {}), {1}: (14, {}), {2}: (15, {})} | custom-call | flops 12000000000 | bytes 8388608 | tf_op jit(solution)/shard_map/back/pallas_call | solution.py:472
  118.0 2.5 add_convert_fusion.5
  121.5 17.5 %heads_back.2 = (bf16[384,2304]{1,0:T(8,128)(2,1)}, bf16[384,2304]{1,0:T(8,128)(2,1)}, f32[8,768]{1,0:T(8,128)}, f32[12,8,256]{2,1,0:T(8,128)}, f32[576,768]{1,0:T(8,128)}) custom-call(bf16[12,576,576]{2,1,0:T(8,128)(2,1)} %get-tuple-element.197.refs_0_, bf16[576,768]{1,0:T(8,128)(2,1)} %get-tuple-element.198.refs_1_, ...), custom_call_target="tpu_custom_call" | custom-call | flops 20000000000 | bytes 8388608 | tf_op jit(solution)/shard_map/heads_back/pallas_call | solution.py:590
  139.8 2.0 add_convert_fusion.4
  142.6 4.4 %collective-permute-start.13 = (bf16[96,768]{1,0:T(8,128)(2,1)}, bf16[96,768]{1,0:T(8,128)(2,1)}, u32[]{:S(2)}, u32[]{:S(2)}) collective-permute-start(bf16[96,768]{1,0:T(8,128)(2,1)} %get-tuple-element.383), channel_id=1, source_target_pairs={{0,1},{1,2},{2,3},{3,0},{4,5},{5,6},{6,7},{7,4},{8,9},{9,10},{10,1... | collective-permute-start | bytes 442376 | tf_op jit(solution)/shard_map/ppermute | solution.py:926
  147.3 2.1 collective-permute-start.15
  152.6 17.9 %heads_back.3 = (bf16[384,2304]{1,0:T(8,128)(2,1)}, bf16[384,2304]{1,0:T(8,128)(2,1)}, f32[8,768]{1,0:T(8,128)}, f32[12,8,256]{2,1,0:T(8,128)}, f32[576,768]{1,0:T(8,128)}) custom-call(bf16[12,576,576]{2,1,0:T(8,128)(2,1)} %get-tuple-element.197.refs_0_, ...), custom_call_target="tpu_custom_call", output_to_operand_aliasing={{0}: (13, {}), {1}: (14, {}), {2}: (15, {}), {3}: (16, {})} | custom-call | flops 20000000000 | bytes 8388608 | tf_op jit(solution)/shard_map/heads_back/pallas_call | solution.py:590
  172.6 2.6 collective-permute-start.18
  176.4 2.5 add_convert_fusion.1
  180.6 7.9 %encode_back.1 = (bf16[144,768]{1,0:T(8,128)(2,1)}, bf16[144,768]{1,0:T(8,128)(2,1)}, bf16[144,768]{1,0:T(8,128)(2,1)}, bf16[144,768]{1,0:T(8,128)(2,1)}, f32[32,768]{1,0:T(8,128)}) custom-call(s32[3]{0:T(128)} %pad_add_fusion.1.info_ref, bf16[144,768]{1,0:T(8,128)(2,1)} %get-tuple-element.193.refs_0_, bf16[144,768]{1,0:T(8,128)(2,1)} %copy-done.32, ...), custom_call_target="tpu_custom_call" | custom-call | flops 10000000000 | bytes 8388608 | tf_op jit(solution)/shard_map/encode_back/pallas_call | solution.py:688
  203.5 2.4 collective-permute-done.24
  207.1 2.2 restack.5
  209.3 2.2 restack.6
  211.6 5.8 %collective-permute-done.26 = bf16[24,3840]{1,0:T(8,128)(2,1)S(1)} collective-permute-done((bf16[24,3840]{1,0:T(8,128)(2,1)S(1)}, bf16[24,3840]{1,0:T(8,128)(2,1)S(1)}, u32[]{:S(2)}, u32[]{:S(2)}) %collective-permute-start.26) | collective-permute-done | bytes 184352 | tf_op jit(solution)/shard_map/ppermute | solution.py:926
  217.4 3.6 %collective-permute-start.29 = (bf16[144,768]{1,0:T(8,128)(2,1)}, bf16[144,768]{1,0:T(8,128)(2,1)S(1)}, u32[]{:S(2)}, u32[]{:S(2)}) collective-permute-start(bf16[144,768]{1,0:T(8,128)(2,1)} %get-tuple-element.291), channel_id=1, source_target_pairs={{0,1},{1,2},{2,3},{3,0},{4,5},{5,6},{6,7},{7,4},{8,9},{9,10},{10,1... | collective-permute-start | bytes 663560 | tf_op jit(solution)/shard_map/ppermute | solution.py:1015
  227.3 6.5 %collective-permute-done.31 = f32[32,768]{1,0:T(8,128)S(1)} collective-permute-done((f32[32,768]{1,0:T(8,128)S(1)}, f32[32,768]{1,0:T(8,128)S(1)}, u32[]{:S(2)}, u32[]{:S(2)}) %collective-permute-start.31) | collective-permute-done | bytes 98336 | tf_op jit(solution)/shard_map/ppermute | solution.py:837
  234.1 7.6 %collective-permute-done.33.refs_2_ = bf16[24,3840]{1,0:T(8,128)(2,1)S(1)} collective-permute-done((bf16[24,3840]{1,0:T(8,128)(2,1)S(1)}, bf16[24,3840]{1,0:T(8,128)(2,1)S(1)}, u32[]{:S(2)}, u32[]{:S(2)}) %collective-permute-start.33) | collective-permute-done | bytes 184352 | tf_op jit(solution)/shard_map/ppermute | solution.py:932
  241.7 2.2 collective-permute-done.34.refs_3_
  249.6 2.8 %collective-permute-start.40 = (bf16[24,2304]{1,0:T(8,128)(2,1)S(1)}, bf16[24,2304]{1,0:T(8,128)(2,1)S(1)}, u32[]{:S(2)}, u32[]{:S(2)}) collective-permute-start(bf16[24,2304]{1,0:T(8,128)(2,1)S(1)} %get-tuple-element.384), channel_id=1, source_target_pairs={{0,3},{1,0},{2,1},{3,2},{4,7},{5,4},{6,5},{7,6},{8,11},{9,8},{10,9... | collective-permute-start | bytes 331784 | tf_op jit(solution)/shard_map/ppermute | solution.py:926
  253.3 2.4 restack.7
  255.7 11.3 %collective-permute-done.37 = f32[32,768]{1,0:T(8,128)S(1)} collective-permute-done((f32[32,768]{1,0:T(8,128)S(1)}, f32[32,768]{1,0:T(8,128)S(1)}, u32[]{:S(2)}, u32[]{:S(2)}) %collective-permute-start.37) | collective-permute-done | bytes 98336 | tf_op jit(solution)/shard_map/ppermute | solution.py:837
  269.5 2.1 collective-permute-start.43
  273.3 2.6 restack.8
  275.9 2.2 collective-permute-done.42.refs_2_
  278.8 2.0 restack.9
  (238 shorter events, 74.2 us)
Async XLA Ops:
  2.8 21.2 %collective-permute-start = (bf16[144,768]{1,0:T(8,128)(2,1)S(1)}, bf16[144,768]{1,0:T(8,128)(2,1)S(1)}, u32[]{:S(2)}, u32[]{:S(2)}) collective-permute-start(bf16[144,768]{1,0:T(8,128)(2,1)S(1)} %get-tuple-element.371), channel_id=1, source_target_pairs={{0,1},{1,2},{2,3},{3,0},{4,5},{5,6},{6,7},{7,4},{8,9},{9,10},{10,1... | collective-permute-start | bytes 663560 | tf_op jit(solution)/shard_map/ppermute | solution.py:844
  5.9 18.2 %collective-permute-start.1 = (bf16[144,768]{1,0:T(8,128)(2,1)S(1)}, bf16[144,768]{1,0:T(8,128)(2,1)S(1)}, u32[]{:S(2)}, u32[]{:S(2)}) collective-permute-start(bf16[144,768]{1,0:T(8,128)(2,1)S(1)} %get-tuple-element.373), channel_id=1, source_target_pairs={{0,2},{1,3},{2,0},{3,1},{4,6},{5,7},{6,4},{7,5},{8,10},{9,11},{10,... | collective-permute-start | bytes 663560 | tf_op jit(solution)/shard_map/ppermute | solution.py:844
  8.4 15.6 %collective-permute-start.2 = (bf16[144,768]{1,0:T(8,128)(2,1)S(1)}, bf16[144,768]{1,0:T(8,128)(2,1)}, u32[]{:S(2)}, u32[]{:S(2)}) collective-permute-start(bf16[144,768]{1,0:T(8,128)(2,1)S(1)} %get-tuple-element.370), channel_id=1, source_target_pairs={{0,3},{1,0},{2,1},{3,2},{4,7},{5,4},{6,5},{7,6},{8,11},{9,8},{10,9... | collective-permute-start | bytes 663560 | tf_op jit(solution)/shard_map/ppermute | solution.py:844
  24.1 30.0 %collective-permute-start.3 = (bf16[144,768]{1,0:T(8,128)(2,1)S(1)}, bf16[144,768]{1,0:T(8,128)(2,1)S(1)}, u32[]{:S(2)}, u32[]{:S(2)}) collective-permute-start(bf16[144,768]{1,0:T(8,128)(2,1)S(1)} %get-tuple-element.202), channel_id=1, source_target_pairs={{0,1},{1,2},{2,3},{3,0},{4,5},{5,6},{6,7},{7,4},{8,9},{9,10},{10,1... | collective-permute-start | bytes 663560 | tf_op jit(solution)/shard_map/ppermute | solution.py:844
  28.2 25.8 %collective-permute-start.4 = (bf16[144,768]{1,0:T(8,128)(2,1)S(1)}, bf16[144,768]{1,0:T(8,128)(2,1)S(1)}, u32[]{:S(2)}, u32[]{:S(2)}) collective-permute-start(bf16[144,768]{1,0:T(8,128)(2,1)S(1)} %get-tuple-element.203), channel_id=1, source_target_pairs={{0,2},{1,3},{2,0},{3,1},{4,6},{5,7},{6,4},{7,5},{8,10},{9,11},{10,... | collective-permute-start | bytes 663560 | tf_op jit(solution)/shard_map/ppermute | solution.py:844
  29.7 24.4 %collective-permute-start.5 = (bf16[144,768]{1,0:T(8,128)(2,1)S(1)}, bf16[144,768]{1,0:T(8,128)(2,1)S(1)}, u32[]{:S(2)}, u32[]{:S(2)}) collective-permute-start(bf16[144,768]{1,0:T(8,128)(2,1)S(1)} %get-tuple-element.204), channel_id=1, source_target_pairs={{0,3},{1,0},{2,1},{3,2},{4,7},{5,4},{6,5},{7,6},{8,11},{9,8},{10,9... | collective-permute-start | bytes 663560 | tf_op jit(solution)/shard_map/ppermute | solution.py:844
  95.1 20.7 %collective-permute-start.10 = (bf16[2,384,768]{2,1,0:T(8,128)(2,1)S(1)}, bf16[2,384,768]{2,1,0:T(8,128)(2,1)S(1)}, u32[]{:S(2)}, u32[]{:S(2)}) collective-permute-start(bf16[2,384,768]{2,1,0:T(8,128)(2,1)S(1)} %pad_maximum_fusion.1), channel_id=1, source_target_pairs={{0,8},{4,20},{8,0},{12,28},{16,24},{20,4},{24,16},{28,12},{1,9},{5... | collective-permute-start | bytes 3538952 | tf_op jit(solution)/shard_map/ppermute | solution.py:914
  96.6 18.6 %collective-permute-start.7 = (bf16[144,768]{1,0:T(8,128)(2,1)}, bf16[144,768]{1,0:T(8,128)(2,1)S(1)}, u32[]{:S(2)}, u32[]{:S(2)}) collective-permute-start(bf16[144,768]{1,0:T(8,128)(2,1)} %get-tuple-element.229), channel_id=1, source_target_pairs={{0,1},{1,2},{2,3},{3,0},{4,5},{5,6},{6,7},{7,4},{8,9},{9,10},{10,1... | collective-permute-start | bytes 663560 | tf_op jit(solution)/shard_map/ppermute | solution.py:844
  97.8 18.0 %collective-permute-start.8 = (bf16[144,768]{1,0:T(8,128)(2,1)S(1)}, bf16[144,768]{1,0:T(8,128)(2,1)S(1)}, u32[]{:S(2)}, u32[]{:S(2)}) collective-permute-start(bf16[144,768]{1,0:T(8,128)(2,1)S(1)} %copy-done.35), channel_id=1, source_target_pairs={{0,2},{1,3},{2,0},{3,1},{4,6},{5,7},{6,4},{7,5},{8,10},{9,11},{10,... | collective-permute-start | bytes 663560 | tf_op jit(solution)/shard_map/ppermute | solution.py:844
  99.2 16.6 %collective-permute-start.9 = (bf16[144,768]{1,0:T(8,128)(2,1)S(1)}, bf16[144,768]{1,0:T(8,128)(2,1)S(1)}, u32[]{:S(2)}, u32[]{:S(2)}) collective-permute-start(bf16[144,768]{1,0:T(8,128)(2,1)S(1)} %copy-done.34), channel_id=1, source_target_pairs={{0,3},{1,0},{2,1},{3,2},{4,7},{5,4},{6,5},{7,6},{8,11},{9,8},{10,9... | collective-permute-start | bytes 663560 | tf_op jit(solution)/shard_map/ppermute | solution.py:844
  116.9 22.1 %collective-permute-start.12 = (bf16[384,3840]{1,0:T(8,128)(2,1)}, bf16[384,3840]{1,0:T(8,128)(2,1)S(1)}, u32[]{:S(2)}, u32[]{:S(2)}) collective-permute-start(bf16[384,3840]{1,0:T(8,128)(2,1)} %get-tuple-element.243), channel_id=1, source_target_pairs={{0,4},{4,0},{8,12},{12,8},{16,20},{20,16},{24,28},{28,24},{1,5},{5... | collective-permute-start | bytes 8847368 | tf_op jit(solution)/shard_map/ppermute | solution.py:837
  120.5 18.5 %collective-permute-start.11 = (bf16[1,384,768]{2,1,0:T(8,128)(2,1)}, bf16[1,384,768]{2,1,0:T(8,128)(2,1)S(1)}, u32[]{:S(2)}, u32[]{:S(2)}) collective-permute-start(bf16[1,384,768]{2,1,0:T(8,128)(2,1)} %add_convert_fusion.5), channel_id=1, source_target_pairs={{0,16},{4,12},{8,24},{12,4},{16,0},{20,28},{24,8},{28,20},{1,17},{... | collective-permute-start | bytes 1769480 | tf_op jit(solution)/shard_map/ppermute | solution.py:914
  142.6 27.8 %collective-permute-start.13 = (bf16[96,768]{1,0:T(8,128)(2,1)}, bf16[96,768]{1,0:T(8,128)(2,1)}, u32[]{:S(2)}, u32[]{:S(2)}) collective-permute-start(bf16[96,768]{1,0:T(8,128)(2,1)} %get-tuple-element.383), channel_id=1, source_target_pairs={{0,1},{1,2},{2,3},{3,0},{4,5},{5,6},{6,7},{7,4},{8,9},{9,10},{10,1... | collective-permute-start | bytes 442376 | tf_op jit(solution)/shard_map/ppermute | solution.py:926
  147.0 23.4 %collective-permute-start.14 = (bf16[96,768]{1,0:T(8,128)(2,1)}, bf16[96,768]{1,0:T(8,128)(2,1)}, u32[]{:S(2)}, u32[]{:S(2)}) collective-permute-start(bf16[96,768]{1,0:T(8,128)(2,1)} %get-tuple-element.382), channel_id=1, source_target_pairs={{0,2},{1,3},{2,0},{3,1},{4,6},{5,7},{6,4},{7,5},{8,10},{9,11},{10,... | collective-permute-start | bytes 442376 | tf_op jit(solution)/shard_map/ppermute | solution.py:926
  147.3 23.2 %collective-permute-start.15 = (bf16[96,768]{1,0:T(8,128)(2,1)}, bf16[96,768]{1,0:T(8,128)(2,1)}, u32[]{:S(2)}, u32[]{:S(2)}) collective-permute-start(bf16[96,768]{1,0:T(8,128)(2,1)} %get-tuple-element.381), channel_id=1, source_target_pairs={{0,3},{1,0},{2,1},{3,2},{4,7},{5,4},{6,5},{7,6},{8,11},{9,8},{10,9... | collective-permute-start | bytes 442376 | tf_op jit(solution)/shard_map/ppermute | solution.py:926
  151.1 19.7 %collective-permute-start.16 = (bf16[2,96,3840]{2,1,0:T(8,128)(2,1)}, bf16[2,96,3840]{2,1,0:T(8,128)(2,1)}, u32[]{:S(2)}, u32[]{:S(2)}) collective-permute-start(bf16[2,96,3840]{2,1,0:T(8,128)(2,1)} %pad_maximum_fusion), channel_id=1, source_target_pairs={{0,8},{4,20},{8,0},{12,28},{16,24},{20,4},{24,16},{28,12},{1,9},{5... | collective-permute-start | bytes 4423688 | tf_op jit(solution)/shard_map/ppermute | solution.py:914
  172.6 16.5 %collective-permute-start.17 = (bf16[96,768]{1,0:T(8,128)(2,1)}, bf16[96,768]{1,0:T(8,128)(2,1)S(1)}, u32[]{:S(2)}, u32[]{:S(2)}) collective-permute-start(bf16[96,768]{1,0:T(8,128)(2,1)} %fusion.11.refs_0_), channel_id=1, source_target_pairs={{0,1},{1,2},{2,3},{3,0},{4,5},{5,6},{6,7},{7,4},{8,9},{9,10},{10,1... | collective-permute-start | bytes 442376 | tf_op jit(solution)/shard_map/ppermute | solution.py:932
  172.6 16.5 %collective-permute-start.18 = (bf16[96,768]{1,0:T(8,128)(2,1)}, bf16[96,768]{1,0:T(8,128)(2,1)S(1)}, u32[]{:S(2)}, u32[]{:S(2)}) collective-permute-start(bf16[96,768]{1,0:T(8,128)(2,1)} %fusion.11.refs_0_), channel_id=1, source_target_pairs={{0,2},{1,3},{2,0},{3,1},{4,6},{5,7},{6,4},{7,5},{8,10},{9,11},{10,... | collective-permute-start | bytes 442376 | tf_op jit(solution)/shard_map/ppermute | solution.py:932
  175.2 14.0 %collective-permute-start.19 = (bf16[96,768]{1,0:T(8,128)(2,1)}, bf16[96,768]{1,0:T(8,128)(2,1)S(1)}, u32[]{:S(2)}, u32[]{:S(2)}) collective-permute-start(bf16[96,768]{1,0:T(8,128)(2,1)} %fusion.11.refs_0_), channel_id=1, source_target_pairs={{0,3},{1,0},{2,1},{3,2},{4,7},{5,4},{6,5},{7,6},{8,11},{9,8},{10,9... | collective-permute-start | bytes 442376 | tf_op jit(solution)/shard_map/ppermute | solution.py:932
  178.9 11.9 %collective-permute-start.21 = (bf16[384,2304]{1,0:T(8,128)(2,1)}, bf16[384,2304]{1,0:T(8,128)(2,1)}, u32[]{:S(2)}, u32[]{:S(2)}) collective-permute-start(bf16[384,2304]{1,0:T(8,128)(2,1)} %get-tuple-element.273), channel_id=1, source_target_pairs={{0,4},{4,0},{8,12},{12,8},{16,20},{20,16},{24,28},{28,24},{1,5},{5... | collective-permute-start | bytes 5308424 | tf_op jit(solution)/shard_map/ppermute | solution.py:837
  179.0 11.8 %collective-permute-start.20 = (bf16[1,96,3840]{2,1,0:T(8,128)(2,1)}, bf16[1,96,3840]{2,1,0:T(8,128)(2,1)}, u32[]{:S(2)}, u32[]{:S(2)}) collective-permute-start(bf16[1,96,3840]{2,1,0:T(8,128)(2,1)} %add_convert_fusion.1), channel_id=1, source_target_pairs={{0,16},{4,12},{8,24},{12,4},{16,0},{20,28},{24,8},{28,20},{1,17},{... | collective-permute-start | bytes 2211848 | tf_op jit(solution)/shard_map/ppermute | solution.py:914
  190.9 26.5 %collective-permute-start.22 = (bf16[144,768]{1,0:T(8,128)(2,1)}, bf16[144,768]{1,0:T(8,128)(2,1)S(1)}, u32[]{:S(2)}, u32[]{:S(2)}) collective-permute-start(bf16[144,768]{1,0:T(8,128)(2,1)} %get-tuple-element.276), channel_id=1, source_target_pairs={{0,2},{1,3},{2,0},{3,1},{4,6},{5,7},{6,4},{7,5},{8,10},{9,11},{10,... | collective-permute-start | bytes 663560 | tf_op jit(solution)/shard_map/ppermute | solution.py:1015
  197.6 19.8 %collective-permute-start.28 = (bf16[2,96,2304]{2,1,0:T(8,128)(2,1)}, bf16[2,96,2304]{2,1,0:T(8,128)(2,1)}, u32[]{:S(2)}, u32[]{:S(2)}) collective-permute-start(bf16[2,96,2304]{2,1,0:T(8,128)(2,1)} %pad_maximum_fusion.2), channel_id=1, source_target_pairs={{0,8},{4,20},{8,0},{12,28},{16,24},{20,4},{24,16},{28,12},{1,9},{5... | collective-permute-start | bytes 2654216 | tf_op jit(solution)/shard_map/ppermute | solution.py:914
  201.8 15.5 %collective-permute-start.26 = (bf16[24,3840]{1,0:T(8,128)(2,1)S(1)}, bf16[24,3840]{1,0:T(8,128)(2,1)S(1)}, u32[]{:S(2)}, u32[]{:S(2)}) collective-permute-start(bf16[24,3840]{1,0:T(8,128)(2,1)S(1)} %get-tuple-element.379), channel_id=1, source_target_pairs={{0,2},{1,3},{2,0},{3,1},{4,6},{5,7},{6,4},{7,5},{8,10},{9,11},{10,... | collective-permute-start | bytes 552968 | tf_op jit(solution)/shard_map/ppermute | solution.py:926
  217.4 26.6 %collective-permute-start.29 = (bf16[144,768]{1,0:T(8,128)(2,1)}, bf16[144,768]{1,0:T(8,128)(2,1)S(1)}, u32[]{:S(2)}, u32[]{:S(2)}) collective-permute-start(bf16[144,768]{1,0:T(8,128)(2,1)} %get-tuple-element.291), channel_id=1, source_target_pairs={{0,1},{1,2},{2,3},{3,0},{4,5},{5,6},{6,7},{7,4},{8,9},{9,10},{10,1... | collective-permute-start | bytes 663560 | tf_op jit(solution)/shard_map/ppermute | solution.py:1015
  222.3 22.3 %collective-permute-start.35 = (bf16[1,96,2304]{2,1,0:T(8,128)(2,1)S(1)}, bf16[1,96,2304]{2,1,0:T(8,128)(2,1)S(1)}, u32[]{:S(2)}, u32[]{:S(2)}) collective-permute-start(bf16[1,96,2304]{2,1,0:T(8,128)(2,1)S(1)} %add_convert_fusion.9), channel_id=1, source_target_pairs={{0,16},{4,12},{8,24},{12,4},{16,0},{20,28},{24,8},{28,20},{1,17},{... | collective-permute-start | bytes 1327112 | tf_op jit(solution)/shard_map/ppermute | solution.py:914
  226.5 15.2 %collective-permute-start.33 = (bf16[24,3840]{1,0:T(8,128)(2,1)S(1)}, bf16[24,3840]{1,0:T(8,128)(2,1)S(1)}, u32[]{:S(2)}, u32[]{:S(2)}) collective-permute-start(bf16[24,3840]{1,0:T(8,128)(2,1)S(1)} %fusion.6.refs_0_), channel_id=1, source_target_pairs={{0,2},{1,3},{2,0},{3,1},{4,6},{5,7},{6,4},{7,5},{8,10},{9,11},{10,... | collective-permute-start | bytes 552968 | tf_op jit(solution)/shard_map/ppermute | solution.py:932
  244.6 23.1 %collective-permute-start.36 = (bf16[144,768]{1,0:T(8,128)(2,1)}, bf16[144,768]{1,0:T(8,128)(2,1)S(1)}, u32[]{:S(2)}, u32[]{:S(2)}) collective-permute-start(bf16[144,768]{1,0:T(8,128)(2,1)} %get-tuple-element.304), channel_id=1, source_target_pairs={{0,3},{1,0},{2,1},{3,2},{4,7},{5,4},{6,5},{7,6},{8,11},{9,8},{10,9... | collective-permute-start | bytes 663560 | tf_op jit(solution)/shard_map/ppermute | solution.py:1015
  247.4 20.3 %collective-permute-start.38 = (bf16[24,2304]{1,0:T(8,128)(2,1)S(1)}, bf16[24,2304]{1,0:T(8,128)(2,1)S(1)}, u32[]{:S(2)}, u32[]{:S(2)}) collective-permute-start(bf16[24,2304]{1,0:T(8,128)(2,1)S(1)} %get-tuple-element.386), channel_id=1, source_target_pairs={{0,1},{1,2},{2,3},{3,0},{4,5},{5,6},{6,7},{7,4},{8,9},{9,10},{10,1... | collective-permute-start | bytes 331784 | tf_op jit(solution)/shard_map/ppermute | solution.py:926
  248.2 19.5 %collective-permute-start.39 = (bf16[24,2304]{1,0:T(8,128)(2,1)S(1)}, bf16[24,2304]{1,0:T(8,128)(2,1)S(1)}, u32[]{:S(2)}, u32[]{:S(2)}) collective-permute-start(bf16[24,2304]{1,0:T(8,128)(2,1)S(1)} %get-tuple-element.385), channel_id=1, source_target_pairs={{0,2},{1,3},{2,0},{3,1},{4,6},{5,7},{6,4},{7,5},{8,10},{9,11},{10,... | collective-permute-start | bytes 331784 | tf_op jit(solution)/shard_map/ppermute | solution.py:926
  249.6 18.1 %collective-permute-start.40 = (bf16[24,2304]{1,0:T(8,128)(2,1)S(1)}, bf16[24,2304]{1,0:T(8,128)(2,1)S(1)}, u32[]{:S(2)}, u32[]{:S(2)}) collective-permute-start(bf16[24,2304]{1,0:T(8,128)(2,1)S(1)} %get-tuple-element.384), channel_id=1, source_target_pairs={{0,3},{1,0},{2,1},{3,2},{4,7},{5,4},{6,5},{7,6},{8,11},{9,8},{10,9... | collective-permute-start | bytes 331784 | tf_op jit(solution)/shard_map/ppermute | solution.py:926
  252.5 14.6 %collective-permute-start.37 = (f32[32,768]{1,0:T(8,128)S(1)}, f32[32,768]{1,0:T(8,128)S(1)}, u32[]{:S(2)}, u32[]{:S(2)}) collective-permute-start(f32[32,768]{1,0:T(8,128)S(1)} %add.786), channel_id=1, source_target_pairs={{0,2},{1,3},{2,0},{3,1},{4,6},{5,7},{6,4},{7,5},{8,10},{9,11},{10,... | collective-permute-start | bytes 294920 | tf_op jit(solution)/shard_map/ppermute | solution.py:837
  (52 other events, 380.2 us)

commit v6 on v5

--- a/solution.py
+++ b/solution.py
@@ -1018,7 +1018,7 @@
         r.name = name
     bias = jnp.concatenate(bias_grads(diag, nb), 1)
     bias = jnp.pad(bias, ((0, 0), (0, 128 - 3 * nb))).reshape(-1, width)
-    hops = {0: (2,), 1: (1,), 2: (3,)}
+    hops = {0: (2,), 1: (3,), 2: (1,)}
     turns = [rounds[1:3], rounds[:1] + rounds[3:4], rounds[4:]] if len(rounds) == 5 else [rounds]
     layouts = {
         "reduce": None,

time: 287 us -> 286 us (level)
  waiting for transfers between devices: 41 us -> 33.9 us
  starting transfers between devices: 61 us -> 67.6 us
    ppermute x8, waiting for transfers between devices: 20.3 us -> 12.2 us  [swap(): return lax.ppermute(value, axis, xor_pairs(lax.axis_size(axis), bit))]
    ppermute x9, starting transfers between devices: 10.5 us -> 14 us  [step(): self.fresh = [lax.ppermute(self.own, 'seq', ring(d)) for d in range(1, n)]]
    ppermute x3, starting transfers between devices: 6.94 us -> 10.2 us  [per_device(): lax.ppermute(gts[d], 'seq', [(i, (i + d) % n_seq) for i in range(n_seq)])]
  transfers between devices with their start and end apart: 44 -> 44, of which waited for: 11 -> 10; matrix products, arithmetic and copies ran while one was open for 12% -> 12% of each run, Pallas kernels for 37% -> 37%
where the time goes in v6:
time: 286 us; the launch traced here: 281 us
  Pallas kernels  132 us (46%)
  starting transfers between devices  67.6 us (24%)
  waiting for transfers between devices  33.9 us (12%)
  other arithmetic  27 us (9%)
  local copies, waits for them, and re-layouts  15.2 us (5%)
  matrix products  3.13 us (1%)
    pallas_call x2, Pallas kernels, heads_back(): pl.pallas_call(heads_kernel, out_shape=(sds((width // 2, 3 * width), BF),...  35.4 us
    pallas_call x1, Pallas kernels, middle(): pl.pallas_call(functools.partial(middle_kernel, n_seq=n_seq, tiles=tiles,...  26.9 us
    pallas_call x2, Pallas kernels, back(): pl.pallas_call(functools.partial(back_kernel, tiles=tiles, last=last, blo...  26.1 us
    pallas_call x1, Pallas kernels, front(): pl.pallas_call(functools.partial(front_kernel, n_seq=n_seq, block=block),...  22.7 us
    ppermute x9, starting transfers between devices, spread(): lax.ppermute(blocks[d], 'seq', [(i, (i + d) % n) for i in range(n)])  17.5 us
    ppermute x9, starting transfers between devices, step(): self.fresh = [lax.ppermute(self.own, 'seq', ring(d)) for d in range(1, n)]  14 us
    ppermute x9, starting transfers between devices, step(): self.fresh = [lax.ppermute(piece(d), 'seq', ring(d)) for d in range(1, n)]  13.5 us
    ppermute x9, waiting for transfers between devices, step(): self.fresh = [lax.ppermute(self.own, 'seq', ring(d)) for d in range(1, n)]  13.2 us
  transfers between devices with their start and end apart: 44, of which 10 were waited for; matrix products, arithmetic and copies ran while one was open for 12% of the time, Pallas kernels for 37%

profile of v6, /device:TPU:0, one launch (start us, length us, event | category | flops | bytes accessed | tf_op | source)
XLA Modules:
  0.0 280.9 jit_solution(14534401152384200466)
XLA Ops:
  0.8 2.1 dynamic-slice_bitcast_fusion
  2.8 3.0 %collective-permute-start = (bf16[144,768]{1,0:T(8,128)(2,1)S(1)}, bf16[144,768]{1,0:T(8,128)(2,1)S(1)}, u32[]{:S(2)}, u32[]{:S(2)}) collective-permute-start(bf16[144,768]{1,0:T(8,128)(2,1)S(1)} %get-tuple-element.371), channel_id=1, source_target_pairs={{0,1},{1,2},{2,3},{3,0},{4,5},{5,6},{6,7},{7,4},{8,9},{9,10},{10,1... | collective-permute-start | bytes 663560 | tf_op jit(solution)/shard_map/ppermute | solution.py:844
  5.9 2.6 collective-permute-start.1
  24.1 4.2 %collective-permute-start.3 = (bf16[144,768]{1,0:T(8,128)(2,1)S(1)}, bf16[144,768]{1,0:T(8,128)(2,1)S(1)}, u32[]{:S(2)}, u32[]{:S(2)}) collective-permute-start(bf16[144,768]{1,0:T(8,128)(2,1)S(1)} %get-tuple-element.202), channel_id=1, source_target_pairs={{0,1},{1,2},{2,3},{3,0},{4,5},{5,6},{6,7},{7,4},{8,9},{9,10},{10,1... | collective-permute-start | bytes 663560 | tf_op jit(solution)/shard_map/ppermute | solution.py:844
  31.3 22.7 %front.1 = (f32[576,768]{1,0:T(8,128)}, bf16[768,576]{1,0:T(8,128)(2,1)}, bf16[576,768]{1,0:T(8,128)(2,1)}, bf16[576,768]{1,0:T(8,128)(2,1)}, bf16[576,768]{1,0:...) custom-call(s32[3]{0:T(128)} %pad_add_fusion.1.info_ref, f32[12,2]{1,0:T(8,128)} %copy.57.edge_ref, ...), custom_call_target="tpu_custom_call" | custom-call | flops 24999999488 | bytes 8388608 | tf_op jit(solution)/shard_map/front/pallas_call | solution.py:220
  54.9 26.9 %middle.1 = (bf16[144,768]{1,0:T(8,128)(2,1)}, bf16[144,768]{1,0:T(8,128)(2,1)}, bf16[144,768]{1,0:T(8,128)(2,1)}, bf16[144,768]{1,0:T(8,128)(2,1)}, f32[576,768...) custom-call(s32[3]{0:T(128)} %pad_add_fusion.1.info_ref, ...), custom_call_target="tpu_custom_call" | custom-call | flops 35000000512 | bytes 8388608 | tf_op jit(solution)/shard_map/middle/pallas_call | solution.py:371
  81.9 11.4 %back.2 = (bf16[384,3840]{1,0:T(8,128)(2,1)}, bf16[384,3840]{1,0:T(8,128)(2,1)}, f32[1,3072]{1,0:T(1,128)}, f32[576,768]{1,0:T(8,128)}) custom-call(s32[3]{0:T(128)} %pad_add_fusion.1.info_ref, bf16[576,768]{1,0:T(8,128)(2,1)} %get-tuple-element.207.refs_0_, f32[576,768]{1,0:T(8,128)} %get-tuple-element.208.refs_1_, bf16[3072,768]{1,0:T(8,128)(2,1)} %refs_2_.3, ...), custom_call_target="tpu_custom_call" | custom-call | flops 12000000000 | bytes 8388608 | tf_op jit(solution)/shard_map/back/pallas_call | solution.py:472
  100.5 14.7 %back.3 = (bf16[384,3840]{1,0:T(8,128)(2,1)}, bf16[384,3840]{1,0:T(8,128)(2,1)}, f32[1,3072]{1,0:T(1,128)}, f32[576,768]{1,0:T(8,128)}, bf16[576,768]{1,0:T(8,128)(2,1)}, /*index=5*/f32[8,768]{1,0:T(8,128)}) custom-call(s32[3]{0:T(128)} %pad_add_fusion.1.info_ref, ...), custom_call_target="tpu_custom_call", output_to_operand_aliasing={{0}: (13, {}), {1}: (14, {}), {2}: (15, {})} | custom-call | flops 12000000000 | bytes 8388608 | tf_op jit(solution)/shard_map/back/pallas_call | solution.py:472
  118.0 2.5 add_convert_fusion.5
  121.5 17.5 %heads_back.2 = (bf16[384,2304]{1,0:T(8,128)(2,1)}, bf16[384,2304]{1,0:T(8,128)(2,1)}, f32[8,768]{1,0:T(8,128)}, f32[12,8,256]{2,1,0:T(8,128)}, f32[576,768]{1,0:T(8,128)}) custom-call(bf16[12,576,576]{2,1,0:T(8,128)(2,1)} %get-tuple-element.197.refs_0_, bf16[576,768]{1,0:T(8,128)(2,1)} %get-tuple-element.198.refs_1_, ...), custom_call_target="tpu_custom_call" | custom-call | flops 20000000000 | bytes 8388608 | tf_op jit(solution)/shard_map/heads_back/pallas_call | solution.py:590
  142.6 4.4 %collective-permute-start.13 = (bf16[96,768]{1,0:T(8,128)(2,1)}, bf16[96,768]{1,0:T(8,128)(2,1)}, u32[]{:S(2)}, u32[]{:S(2)}) collective-permute-start(bf16[96,768]{1,0:T(8,128)(2,1)} %get-tuple-element.383), channel_id=1, source_target_pairs={{0,1},{1,2},{2,3},{3,0},{4,5},{5,6},{6,7},{7,4},{8,9},{9,10},{10,1... | collective-permute-start | bytes 442376 | tf_op jit(solution)/shard_map/ppermute | solution.py:926
  147.3 2.1 collective-permute-start.15
  152.6 17.9 %heads_back.3 = (bf16[384,2304]{1,0:T(8,128)(2,1)}, bf16[384,2304]{1,0:T(8,128)(2,1)}, f32[8,768]{1,0:T(8,128)}, f32[12,8,256]{2,1,0:T(8,128)}, f32[576,768]{1,0:T(8,128)}) custom-call(bf16[12,576,576]{2,1,0:T(8,128)(2,1)} %get-tuple-element.197.refs_0_, ...), custom_call_target="tpu_custom_call", output_to_operand_aliasing={{0}: (13, {}), {1}: (14, {}), {2}: (15, {}), {3}: (16, {})} | custom-call | flops 20000000000 | bytes 8388608 | tf_op jit(solution)/shard_map/heads_back/pallas_call | solution.py:590
  172.6 2.6 collective-permute-start.18
  176.4 2.5 add_convert_fusion.1
  180.6 7.9 %encode_back.1 = (bf16[144,768]{1,0:T(8,128)(2,1)}, bf16[144,768]{1,0:T(8,128)(2,1)}, bf16[144,768]{1,0:T(8,128)(2,1)}, bf16[144,768]{1,0:T(8,128)(2,1)}, f32[32,768]{1,0:T(8,128)}) custom-call(s32[3]{0:T(128)} %pad_add_fusion.1.info_ref, bf16[144,768]{1,0:T(8,128)(2,1)} %get-tuple-element.193.refs_0_, bf16[144,768]{1,0:T(8,128)(2,1)} %copy-done.32, ...), custom_call_target="tpu_custom_call" | custom-call | flops 10000000000 | bytes 8388608 | tf_op jit(solution)/shard_map/encode_back/pallas_call | solution.py:688
  203.5 2.4 collective-permute-done.24
  207.1 2.2 restack.5
  209.3 2.2 restack.6
  211.6 5.8 %collective-permute-done.26 = bf16[24,3840]{1,0:T(8,128)(2,1)S(1)} collective-permute-done((bf16[24,3840]{1,0:T(8,128)(2,1)S(1)}, bf16[24,3840]{1,0:T(8,128)(2,1)S(1)}, u32[]{:S(2)}, u32[]{:S(2)}) %collective-permute-start.26) | collective-permute-done | bytes 184352 | tf_op jit(solution)/shard_map/ppermute | solution.py:926
  217.4 3.8 %collective-permute-start.29 = (bf16[144,768]{1,0:T(8,128)(2,1)}, bf16[144,768]{1,0:T(8,128)(2,1)S(1)}, u32[]{:S(2)}, u32[]{:S(2)}) collective-permute-start(bf16[144,768]{1,0:T(8,128)(2,1)} %get-tuple-element.293), channel_id=1, source_target_pairs={{0,3},{1,0},{2,1},{3,2},{4,7},{5,4},{6,5},{7,6},{8,11},{9,8},{10,9... | collective-permute-start | bytes 663560 | tf_op jit(solution)/shard_map/ppermute | solution.py:1015
  224.7 2.1 collective-permute-start.32
  228.5 3.0 %collective-permute-start.34 = (bf16[24,3840]{1,0:T(8,128)(2,1)S(1)}, bf16[24,3840]{1,0:T(8,128)(2,1)S(1)}, u32[]{:S(2)}, u32[]{:S(2)}) collective-permute-start(bf16[24,3840]{1,0:T(8,128)(2,1)S(1)} %fusion.6.refs_0_), channel_id=1, source_target_pairs={{0,3},{1,0},{2,1},{3,2},{4,7},{5,4},{6,5},{7,6},{8,11},{9,8},{10,9... | collective-permute-start | bytes 552968 | tf_op jit(solution)/shard_map/ppermute | solution.py:932
  231.5 2.7 collective-permute-done.32.refs_1_
  234.2 7.1 %collective-permute-done.33.refs_2_ = bf16[24,3840]{1,0:T(8,128)(2,1)S(1)} collective-permute-done((bf16[24,3840]{1,0:T(8,128)(2,1)S(1)}, bf16[24,3840]{1,0:T(8,128)(2,1)S(1)}, u32[]{:S(2)}, u32[]{:S(2)}) %collective-permute-start.33) | collective-permute-done | bytes 184352 | tf_op jit(solution)/shard_map/ppermute | solution.py:932
  242.0 4.4 %collective-permute-start.36 = (bf16[144,768]{1,0:T(8,128)(2,1)}, bf16[144,768]{1,0:T(8,128)(2,1)S(1)}, u32[]{:S(2)}, u32[]{:S(2)}) collective-permute-start(bf16[144,768]{1,0:T(8,128)(2,1)} %get-tuple-element.302), channel_id=1, source_target_pairs={{0,1},{1,2},{2,3},{3,0},{4,5},{5,6},{6,7},{7,4},{8,9},{9,10},{10,1... | collective-permute-start | bytes 663560 | tf_op jit(solution)/shard_map/ppermute | solution.py:1015
  248.6 3.0 %collective-permute-start.40 = (bf16[24,2304]{1,0:T(8,128)(2,1)S(1)}, bf16[24,2304]{1,0:T(8,128)(2,1)S(1)}, u32[]{:S(2)}, u32[]{:S(2)}) collective-permute-start(bf16[24,2304]{1,0:T(8,128)(2,1)S(1)} %get-tuple-element.384), channel_id=1, source_target_pairs={{0,3},{1,0},{2,1},{3,2},{4,7},{5,4},{6,5},{7,6},{8,11},{9,8},{10,9... | collective-permute-start | bytes 331784 | tf_op jit(solution)/shard_map/ppermute | solution.py:926
  253.7 2.4 restack.7
  256.1 9.3 %collective-permute-done.37 = f32[32,768]{1,0:T(8,128)S(1)} collective-permute-done((f32[32,768]{1,0:T(8,128)S(1)}, f32[32,768]{1,0:T(8,128)S(1)}, u32[]{:S(2)}, u32[]{:S(2)}) %collective-permute-start.37) | collective-permute-done | bytes 98336 | tf_op jit(solution)/shard_map/ppermute | solution.py:837
  266.2 3.4 %collective-permute-start.42 = (bf16[24,2304]{1,0:T(8,128)(2,1)S(1)}, bf16[24,2304]{1,0:T(8,128)(2,1)S(1)}, u32[]{:S(2)}, u32[]{:S(2)}) collective-permute-start(bf16[24,2304]{1,0:T(8,128)(2,1)S(1)} %fusion.14.refs_0_), channel_id=1, source_target_pairs={{0,2},{1,3},{2,0},{3,1},{4,6},{5,7},{6,4},{7,5},{8,10},{9,11},{10,... | collective-permute-start | bytes 331784 | tf_op jit(solution)/shard_map/ppermute | solution.py:932
  271.7 2.6 restack.8
  274.3 3.4 %collective-permute-done.42.refs_2_ = bf16[24,2304]{1,0:T(8,128)(2,1)S(1)} collective-permute-done((bf16[24,2304]{1,0:T(8,128)(2,1)S(1)}, bf16[24,2304]{1,0:T(8,128)(2,1)S(1)}, u32[]{:S(2)}, u32[]{:S(2)}) %collective-permute-start.42) | collective-permute-done | bytes 110624 | tf_op jit(solution)/shard_map/ppermute | solution.py:932
  (238 shorter events, 74.1 us)
Async XLA Ops:
  2.8 21.2 %collective-permute-start = (bf16[144,768]{1,0:T(8,128)(2,1)S(1)}, bf16[144,768]{1,0:T(8,128)(2,1)S(1)}, u32[]{:S(2)}, u32[]{:S(2)}) collective-permute-start(bf16[144,768]{1,0:T(8,128)(2,1)S(1)} %get-tuple-element.371), channel_id=1, source_target_pairs={{0,1},{1,2},{2,3},{3,0},{4,5},{5,6},{6,7},{7,4},{8,9},{9,10},{10,1... | collective-permute-start | bytes 663560 | tf_op jit(solution)/shard_map/ppermute | solution.py:844
  5.9 18.2 %collective-permute-start.1 = (bf16[144,768]{1,0:T(8,128)(2,1)S(1)}, bf16[144,768]{1,0:T(8,128)(2,1)S(1)}, u32[]{:S(2)}, u32[]{:S(2)}) collective-permute-start(bf16[144,768]{1,0:T(8,128)(2,1)S(1)} %get-tuple-element.373), channel_id=1, source_target_pairs={{0,2},{1,3},{2,0},{3,1},{4,6},{5,7},{6,4},{7,5},{8,10},{9,11},{10,... | collective-permute-start | bytes 663560 | tf_op jit(solution)/shard_map/ppermute | solution.py:844
  8.4 15.6 %collective-permute-start.2 = (bf16[144,768]{1,0:T(8,128)(2,1)S(1)}, bf16[144,768]{1,0:T(8,128)(2,1)}, u32[]{:S(2)}, u32[]{:S(2)}) collective-permute-start(bf16[144,768]{1,0:T(8,128)(2,1)S(1)} %get-tuple-element.370), channel_id=1, source_target_pairs={{0,3},{1,0},{2,1},{3,2},{4,7},{5,4},{6,5},{7,6},{8,11},{9,8},{10,9... | collective-permute-start | bytes 663560 | tf_op jit(solution)/shard_map/ppermute | solution.py:844
  24.1 30.0 %collective-permute-start.3 = (bf16[144,768]{1,0:T(8,128)(2,1)S(1)}, bf16[144,768]{1,0:T(8,128)(2,1)S(1)}, u32[]{:S(2)}, u32[]{:S(2)}) collective-permute-start(bf16[144,768]{1,0:T(8,128)(2,1)S(1)} %get-tuple-element.202), channel_id=1, source_target_pairs={{0,1},{1,2},{2,3},{3,0},{4,5},{5,6},{6,7},{7,4},{8,9},{9,10},{10,1... | collective-permute-start | bytes 663560 | tf_op jit(solution)/shard_map/ppermute | solution.py:844
  28.2 25.8 %collective-permute-start.4 = (bf16[144,768]{1,0:T(8,128)(2,1)S(1)}, bf16[144,768]{1,0:T(8,128)(2,1)S(1)}, u32[]{:S(2)}, u32[]{:S(2)}) collective-permute-start(bf16[144,768]{1,0:T(8,128)(2,1)S(1)} %get-tuple-element.203), channel_id=1, source_target_pairs={{0,2},{1,3},{2,0},{3,1},{4,6},{5,7},{6,4},{7,5},{8,10},{9,11},{10,... | collective-permute-start | bytes 663560 | tf_op jit(solution)/shard_map/ppermute | solution.py:844
  29.7 24.4 %collective-permute-start.5 = (bf16[144,768]{1,0:T(8,128)(2,1)S(1)}, bf16[144,768]{1,0:T(8,128)(2,1)S(1)}, u32[]{:S(2)}, u32[]{:S(2)}) collective-permute-start(bf16[144,768]{1,0:T(8,128)(2,1)S(1)} %get-tuple-element.204), channel_id=1, source_target_pairs={{0,3},{1,0},{2,1},{3,2},{4,7},{5,4},{6,5},{7,6},{8,11},{9,8},{10,9... | collective-permute-start | bytes 663560 | tf_op jit(solution)/shard_map/ppermute | solution.py:844
  95.1 20.7 %collective-permute-start.10 = (bf16[2,384,768]{2,1,0:T(8,128)(2,1)S(1)}, bf16[2,384,768]{2,1,0:T(8,128)(2,1)S(1)}, u32[]{:S(2)}, u32[]{:S(2)}) collective-permute-start(bf16[2,384,768]{2,1,0:T(8,128)(2,1)S(1)} %pad_maximum_fusion.1), channel_id=1, source_target_pairs={{0,8},{4,20},{8,0},{12,28},{16,24},{20,4},{24,16},{28,12},{1,9},{5... | collective-permute-start | bytes 3538952 | tf_op jit(solution)/shard_map/ppermute | solution.py:914
  96.6 18.6 %collective-permute-start.7 = (bf16[144,768]{1,0:T(8,128)(2,1)}, bf16[144,768]{1,0:T(8,128)(2,1)S(1)}, u32[]{:S(2)}, u32[]{:S(2)}) collective-permute-start(bf16[144,768]{1,0:T(8,128)(2,1)} %get-tuple-element.229), channel_id=1, source_target_pairs={{0,1},{1,2},{2,3},{3,0},{4,5},{5,6},{6,7},{7,4},{8,9},{9,10},{10,1... | collective-permute-start | bytes 663560 | tf_op jit(solution)/shard_map/ppermute | solution.py:844
  97.8 18.0 %collective-permute-start.8 = (bf16[144,768]{1,0:T(8,128)(2,1)S(1)}, bf16[144,768]{1,0:T(8,128)(2,1)S(1)}, u32[]{:S(2)}, u32[]{:S(2)}) collective-permute-start(bf16[144,768]{1,0:T(8,128)(2,1)S(1)} %copy-done.35), channel_id=1, source_target_pairs={{0,2},{1,3},{2,0},{3,1},{4,6},{5,7},{6,4},{7,5},{8,10},{9,11},{10,... | collective-permute-start | bytes 663560 | tf_op jit(solution)/shard_map/ppermute | solution.py:844
  99.2 16.6 %collective-permute-start.9 = (bf16[144,768]{1,0:T(8,128)(2,1)S(1)}, bf16[144,768]{1,0:T(8,128)(2,1)S(1)}, u32[]{:S(2)}, u32[]{:S(2)}) collective-permute-start(bf16[144,768]{1,0:T(8,128)(2,1)S(1)} %copy-done.34), channel_id=1, source_target_pairs={{0,3},{1,0},{2,1},{3,2},{4,7},{5,4},{6,5},{7,6},{8,11},{9,8},{10,9... | collective-permute-start | bytes 663560 | tf_op jit(solution)/shard_map/ppermute | solution.py:844
  116.9 22.1 %collective-permute-start.12 = (bf16[384,3840]{1,0:T(8,128)(2,1)}, bf16[384,3840]{1,0:T(8,128)(2,1)S(1)}, u32[]{:S(2)}, u32[]{:S(2)}) collective-permute-start(bf16[384,3840]{1,0:T(8,128)(2,1)} %get-tuple-element.243), channel_id=1, source_target_pairs={{0,4},{4,0},{8,12},{12,8},{16,20},{20,16},{24,28},{28,24},{1,5},{5... | collective-permute-start | bytes 8847368 | tf_op jit(solution)/shard_map/ppermute | solution.py:837
  120.5 18.5 %collective-permute-start.11 = (bf16[1,384,768]{2,1,0:T(8,128)(2,1)}, bf16[1,384,768]{2,1,0:T(8,128)(2,1)S(1)}, u32[]{:S(2)}, u32[]{:S(2)}) collective-permute-start(bf16[1,384,768]{2,1,0:T(8,128)(2,1)} %add_convert_fusion.5), channel_id=1, source_target_pairs={{0,16},{4,12},{8,24},{12,4},{16,0},{20,28},{24,8},{28,20},{1,17},{... | collective-permute-start | bytes 1769480 | tf_op jit(solution)/shard_map/ppermute | solution.py:914
  142.6 27.8 %collective-permute-start.13 = (bf16[96,768]{1,0:T(8,128)(2,1)}, bf16[96,768]{1,0:T(8,128)(2,1)}, u32[]{:S(2)}, u32[]{:S(2)}) collective-permute-start(bf16[96,768]{1,0:T(8,128)(2,1)} %get-tuple-element.383), channel_id=1, source_target_pairs={{0,1},{1,2},{2,3},{3,0},{4,5},{5,6},{6,7},{7,4},{8,9},{9,10},{10,1... | collective-permute-start | bytes 442376 | tf_op jit(solution)/shard_map/ppermute | solution.py:926
  147.0 23.4 %collective-permute-start.14 = (bf16[96,768]{1,0:T(8,128)(2,1)}, bf16[96,768]{1,0:T(8,128)(2,1)}, u32[]{:S(2)}, u32[]{:S(2)}) collective-permute-start(bf16[96,768]{1,0:T(8,128)(2,1)} %get-tuple-element.382), channel_id=1, source_target_pairs={{0,2},{1,3},{2,0},{3,1},{4,6},{5,7},{6,4},{7,5},{8,10},{9,11},{10,... | collective-permute-start | bytes 442376 | tf_op jit(solution)/shard_map/ppermute | solution.py:926
  147.3 23.2 %collective-permute-start.15 = (bf16[96,768]{1,0:T(8,128)(2,1)}, bf16[96,768]{1,0:T(8,128)(2,1)}, u32[]{:S(2)}, u32[]{:S(2)}) collective-permute-start(bf16[96,768]{1,0:T(8,128)(2,1)} %get-tuple-element.381), channel_id=1, source_target_pairs={{0,3},{1,0},{2,1},{3,2},{4,7},{5,4},{6,5},{7,6},{8,11},{9,8},{10,9... | collective-permute-start | bytes 442376 | tf_op jit(solution)/shard_map/ppermute | solution.py:926
  151.1 19.7 %collective-permute-start.16 = (bf16[2,96,3840]{2,1,0:T(8,128)(2,1)}, bf16[2,96,3840]{2,1,0:T(8,128)(2,1)}, u32[]{:S(2)}, u32[]{:S(2)}) collective-permute-start(bf16[2,96,3840]{2,1,0:T(8,128)(2,1)} %pad_maximum_fusion), channel_id=1, source_target_pairs={{0,8},{4,20},{8,0},{12,28},{16,24},{20,4},{24,16},{28,12},{1,9},{5... | collective-permute-start | bytes 4423688 | tf_op jit(solution)/shard_map/ppermute | solution.py:914
  172.6 16.5 %collective-permute-start.17 = (bf16[96,768]{1,0:T(8,128)(2,1)}, bf16[96,768]{1,0:T(8,128)(2,1)S(1)}, u32[]{:S(2)}, u32[]{:S(2)}) collective-permute-start(bf16[96,768]{1,0:T(8,128)(2,1)} %fusion.11.refs_0_), channel_id=1, source_target_pairs={{0,1},{1,2},{2,3},{3,0},{4,5},{5,6},{6,7},{7,4},{8,9},{9,10},{10,1... | collective-permute-start | bytes 442376 | tf_op jit(solution)/shard_map/ppermute | solution.py:932
  172.6 16.5 %collective-permute-start.18 = (bf16[96,768]{1,0:T(8,128)(2,1)}, bf16[96,768]{1,0:T(8,128)(2,1)S(1)}, u32[]{:S(2)}, u32[]{:S(2)}) collective-permute-start(bf16[96,768]{1,0:T(8,128)(2,1)} %fusion.11.refs_0_), channel_id=1, source_target_pairs={{0,2},{1,3},{2,0},{3,1},{4,6},{5,7},{6,4},{7,5},{8,10},{9,11},{10,... | collective-permute-start | bytes 442376 | tf_op jit(solution)/shard_map/ppermute | solution.py:932
  175.2 14.0 %collective-permute-start.19 = (bf16[96,768]{1,0:T(8,128)(2,1)}, bf16[96,768]{1,0:T(8,128)(2,1)S(1)}, u32[]{:S(2)}, u32[]{:S(2)}) collective-permute-start(bf16[96,768]{1,0:T(8,128)(2,1)} %fusion.11.refs_0_), channel_id=1, source_target_pairs={{0,3},{1,0},{2,1},{3,2},{4,7},{5,4},{6,5},{7,6},{8,11},{9,8},{10,9... | collective-permute-start | bytes 442376 | tf_op jit(solution)/shard_map/ppermute | solution.py:932
  178.9 11.9 %collective-permute-start.21 = (bf16[384,2304]{1,0:T(8,128)(2,1)}, bf16[384,2304]{1,0:T(8,128)(2,1)}, u32[]{:S(2)}, u32[]{:S(2)}) collective-permute-start(bf16[384,2304]{1,0:T(8,128)(2,1)} %get-tuple-element.273), channel_id=1, source_target_pairs={{0,4},{4,0},{8,12},{12,8},{16,20},{20,16},{24,28},{28,24},{1,5},{5... | collective-permute-start | bytes 5308424 | tf_op jit(solution)/shard_map/ppermute | solution.py:837
  190.9 26.5 %collective-permute-start.22 = (bf16[144,768]{1,0:T(8,128)(2,1)}, bf16[144,768]{1,0:T(8,128)(2,1)S(1)}, u32[]{:S(2)}, u32[]{:S(2)}) collective-permute-start(bf16[144,768]{1,0:T(8,128)(2,1)} %get-tuple-element.276), channel_id=1, source_target_pairs={{0,2},{1,3},{2,0},{3,1},{4,6},{5,7},{6,4},{7,5},{8,10},{9,11},{10,... | collective-permute-start | bytes 663560 | tf_op jit(solution)/shard_map/ppermute | solution.py:1015
  197.6 19.8 %collective-permute-start.28 = (bf16[2,96,2304]{2,1,0:T(8,128)(2,1)}, bf16[2,96,2304]{2,1,0:T(8,128)(2,1)}, u32[]{:S(2)}, u32[]{:S(2)}) collective-permute-start(bf16[2,96,2304]{2,1,0:T(8,128)(2,1)} %pad_maximum_fusion.2), channel_id=1, source_target_pairs={{0,8},{4,20},{8,0},{12,28},{16,24},{20,4},{24,16},{28,12},{1,9},{5... | collective-permute-start | bytes 2654216 | tf_op jit(solution)/shard_map/ppermute | solution.py:914
  201.8 15.5 %collective-permute-start.26 = (bf16[24,3840]{1,0:T(8,128)(2,1)S(1)}, bf16[24,3840]{1,0:T(8,128)(2,1)S(1)}, u32[]{:S(2)}, u32[]{:S(2)}) collective-permute-start(bf16[24,3840]{1,0:T(8,128)(2,1)S(1)} %get-tuple-element.379), channel_id=1, source_target_pairs={{0,2},{1,3},{2,0},{3,1},{4,6},{5,7},{6,4},{7,5},{8,10},{9,11},{10,... | collective-permute-start | bytes 552968 | tf_op jit(solution)/shard_map/ppermute | solution.py:926
  217.4 23.9 %collective-permute-start.29 = (bf16[144,768]{1,0:T(8,128)(2,1)}, bf16[144,768]{1,0:T(8,128)(2,1)S(1)}, u32[]{:S(2)}, u32[]{:S(2)}) collective-permute-start(bf16[144,768]{1,0:T(8,128)(2,1)} %get-tuple-element.293), channel_id=1, source_target_pairs={{0,3},{1,0},{2,1},{3,2},{4,7},{5,4},{6,5},{7,6},{8,11},{9,8},{10,9... | collective-permute-start | bytes 663560 | tf_op jit(solution)/shard_map/ppermute | solution.py:1015
  222.6 19.4 %collective-permute-start.35 = (bf16[1,96,2304]{2,1,0:T(8,128)(2,1)S(1)}, bf16[1,96,2304]{2,1,0:T(8,128)(2,1)S(1)}, u32[]{:S(2)}, u32[]{:S(2)}) collective-permute-start(bf16[1,96,2304]{2,1,0:T(8,128)(2,1)S(1)} %add_convert_fusion.9), channel_id=1, source_target_pairs={{0,16},{4,12},{8,24},{12,4},{16,0},{20,28},{24,8},{28,20},{1,17},{... | collective-permute-start | bytes 1327112 | tf_op jit(solution)/shard_map/ppermute | solution.py:914
  226.7 14.5 %collective-permute-start.33 = (bf16[24,3840]{1,0:T(8,128)(2,1)S(1)}, bf16[24,3840]{1,0:T(8,128)(2,1)S(1)}, u32[]{:S(2)}, u32[]{:S(2)}) collective-permute-start(bf16[24,3840]{1,0:T(8,128)(2,1)S(1)} %fusion.6.refs_0_), channel_id=1, source_target_pairs={{0,2},{1,3},{2,0},{3,1},{4,6},{5,7},{6,4},{7,5},{8,10},{9,11},{10,... | collective-permute-start | bytes 552968 | tf_op jit(solution)/shard_map/ppermute | solution.py:932
  228.5 12.8 %collective-permute-start.34 = (bf16[24,3840]{1,0:T(8,128)(2,1)S(1)}, bf16[24,3840]{1,0:T(8,128)(2,1)S(1)}, u32[]{:S(2)}, u32[]{:S(2)}) collective-permute-start(bf16[24,3840]{1,0:T(8,128)(2,1)S(1)} %fusion.6.refs_0_), channel_id=1, source_target_pairs={{0,3},{1,0},{2,1},{3,2},{4,7},{5,4},{6,5},{7,6},{8,11},{9,8},{10,9... | collective-permute-start | bytes 552968 | tf_op jit(solution)/shard_map/ppermute | solution.py:932
  242.0 24.1 %collective-permute-start.36 = (bf16[144,768]{1,0:T(8,128)(2,1)}, bf16[144,768]{1,0:T(8,128)(2,1)S(1)}, u32[]{:S(2)}, u32[]{:S(2)}) collective-permute-start(bf16[144,768]{1,0:T(8,128)(2,1)} %get-tuple-element.302), channel_id=1, source_target_pairs={{0,1},{1,2},{2,3},{3,0},{4,5},{5,6},{6,7},{7,4},{8,9},{9,10},{10,1... | collective-permute-start | bytes 663560 | tf_op jit(solution)/shard_map/ppermute | solution.py:1015
  247.8 18.3 %collective-permute-start.38 = (bf16[24,2304]{1,0:T(8,128)(2,1)S(1)}, bf16[24,2304]{1,0:T(8,128)(2,1)S(1)}, u32[]{:S(2)}, u32[]{:S(2)}) collective-permute-start(bf16[24,2304]{1,0:T(8,128)(2,1)S(1)} %get-tuple-element.386), channel_id=1, source_target_pairs={{0,1},{1,2},{2,3},{3,0},{4,5},{5,6},{6,7},{7,4},{8,9},{9,10},{10,1... | collective-permute-start | bytes 331784 | tf_op jit(solution)/shard_map/ppermute | solution.py:926
  247.9 18.1 %collective-permute-start.39 = (bf16[24,2304]{1,0:T(8,128)(2,1)S(1)}, bf16[24,2304]{1,0:T(8,128)(2,1)S(1)}, u32[]{:S(2)}, u32[]{:S(2)}) collective-permute-start(bf16[24,2304]{1,0:T(8,128)(2,1)S(1)} %get-tuple-element.385), channel_id=1, source_target_pairs={{0,2},{1,3},{2,0},{3,1},{4,6},{5,7},{6,4},{7,5},{8,10},{9,11},{10,... | collective-permute-start | bytes 331784 | tf_op jit(solution)/shard_map/ppermute | solution.py:926
  248.6 17.4 %collective-permute-start.40 = (bf16[24,2304]{1,0:T(8,128)(2,1)S(1)}, bf16[24,2304]{1,0:T(8,128)(2,1)S(1)}, u32[]{:S(2)}, u32[]{:S(2)}) collective-permute-start(bf16[24,2304]{1,0:T(8,128)(2,1)S(1)} %get-tuple-element.384), channel_id=1, source_target_pairs={{0,3},{1,0},{2,1},{3,2},{4,7},{5,4},{6,5},{7,6},{8,11},{9,8},{10,9... | collective-permute-start | bytes 331784 | tf_op jit(solution)/shard_map/ppermute | solution.py:926
  251.7 13.7 %collective-permute-start.37 = (f32[32,768]{1,0:T(8,128)S(1)}, f32[32,768]{1,0:T(8,128)S(1)}, u32[]{:S(2)}, u32[]{:S(2)}) collective-permute-start(f32[32,768]{1,0:T(8,128)S(1)} %add.786), channel_id=1, source_target_pairs={{0,2},{1,3},{2,0},{3,1},{4,6},{5,7},{6,4},{7,5},{8,10},{9,11},{10,... | collective-permute-start | bytes 294920 | tf_op jit(solution)/shard_map/ppermute | solution.py:837
  (52 other events, 383.1 us)
